TPU v7x, 32 devices: a whole 2x2x4 slice. The times are simulated.
32 devices in a mesh: teach: 2 (over core), dp: 16 (over z, y, x).
Axes of the slice: x: 2, y: 2, z: 4, core: 2. Of those that a mesh axis runs over, the one named last changes fastest.
Arguments:
- teacher_logits: bfloat16 [2, 4096, 5000], P('teach', 'dp'), may hold values from -18 to 400
- routes: int32 [4096, 1], P('dp'), may hold values from 0 to 31; in each aligned block of 256 rows (0 to 255, 256 to 511, ...) at most 16 rows name the same one
- agreement: int32 [4096], P('dp'), may hold values 0 or 1
- targets: int32 [4096], P('dp'), may hold values from 0 to 4999
- lengths: int32 [16], P('dp'), may hold values from 64 to 256
- student_hidden: bfloat16 [8192, 1024], P(('teach', 'dp')), may hold values from -6 to 6
- out_weight: bfloat16 [1024, 5000], replicated, may hold values from -2 to 2
- out_bias: float32 [5000], replicated, may hold values from -6 to 6
- gain: float32 [1024], replicated, may hold values from 0.5 to 1.5
Outputs:
- weight_grad: float32 [1024, 5000], P(('teach', 'dp'))
- gain_grad: float32 [1024], replicated
- bias_grad: float32 [5000], replicated
- loss: float32 [], replicated
Inputs may be any that keep to these rules, and one draw needn't show every extreme that they name: `routes`: within the 256 rows of one index of dp, each student device is named at most 16 times, and some device exactly 16 times.
All inputs are finite; a program needn't handle non-finite values. No bound on the sum of `agreement` on one device may be relied on, other than what follows from the above.
Results may differ from a plain program's by a relative error of at most 0.0031.
Values may be sent and summed in bfloat16 or wider, within the bound.
No kernel may reach another device: no remote copies, remote signals or barrier semaphores. Data moves between devices by JAX's collectives and lax.ppermute only.
A program may use at most 128 MiB of HBM per device.

v0:
```python
import jax
import jax.numpy as jnp
from jax import lax
from jax.sharding import PartitionSpec as P

LMAX = 256


EPSILON = 1e-05


def route_slots(dest_device, devices):
    onehot = (dest_device[:, None] == jnp.arange(devices, dtype=jnp.int32)[None, :]).astype(
        jnp.float32
    )
    row_ids = jnp.arange(dest_device.shape[0], dtype=jnp.int32)
    earlier = (row_ids[None, :] < row_ids[:, None]).astype(jnp.float32)
    before = jnp.dot(
        earlier, onehot, preferred_element_type=jnp.float32, precision=lax.Precision.HIGHEST
    )
    return jnp.sum(before * onehot, axis=1).astype(jnp.int32)


def live_mask(lengths_block, row_total):
    row_ids = jnp.arange(row_total, dtype=jnp.int32)
    utterance = row_ids // LMAX
    frame_pos = row_ids % LMAX
    picks = utterance[:, None] == jnp.arange(lengths_block.shape[0], dtype=jnp.int32)[None, :]
    row_length = jnp.sum(jnp.where(picks, lengths_block[None, :], 0), axis=1)
    return (frame_pos < row_length).astype(jnp.float32)


def soft_targets(teacher_rows, agree_rows, target_rows, live_rows):
    probs_teacher = jax.nn.softmax(teacher_rows.astype(jnp.float32), axis=-1)
    onehot = (
        target_rows[:, None] == jnp.arange(probs_teacher.shape[1], dtype=jnp.int32)[None, :]
    ).astype(jnp.float32)
    weight = (0.5 * agree_rows.astype(jnp.float32))[:, None]
    return (live_rows[:, None] * (weight * probs_teacher + 0.5 * onehot)).astype(jnp.bfloat16)


def student_forward(hidden_rows, gain, out_weight, out_bias):
    states = hidden_rows.astype(jnp.float32)
    centre = jnp.mean(states, axis=1, keepdims=True)
    spread = jnp.mean(jnp.square(states - centre), axis=1, keepdims=True)
    normed = (states - centre) * lax.rsqrt(spread + EPSILON)
    scaled = (normed * gain[None, :]).astype(jnp.bfloat16)
    logits = jnp.dot(scaled, out_weight, preferred_element_type=jnp.float32) + out_bias[None, :]
    return (normed, scaled, jax.nn.log_softmax(logits, axis=-1))


def combined_grads(first_soft, second_soft, log_probs):
    first_float = first_soft.astype(jnp.float32)
    second_float = second_soft.astype(jnp.float32)
    row_mass = jnp.sum(first_float + second_float, axis=1, keepdims=True)
    return (row_mass * jnp.exp(log_probs) - first_float - second_float).astype(jnp.bfloat16)


def body(
    teacher_logits, routes, agreement, targets, lengths, student_hidden, out_weight, out_bias, gain
):
    teach_count = lax.axis_size("teach")
    data_count = lax.axis_size("dp")
    devices = teach_count * data_count
    rows_here = teacher_logits.shape[1]
    most_slots = 2 * rows_here // devices
    vocab = teacher_logits.shape[2]
    width = student_hidden.shape[1]
    dest_device = routes[:, 0]
    slot_index = route_slots(dest_device, devices)
    live_rows = live_mask(lengths, rows_here)
    soft_rows = soft_targets(teacher_logits[0], agreement, targets, live_rows)
    half = rows_here // 2
    first_here = lax.axis_index("teach") * half
    count_term = jnp.sum(lax.dynamic_slice_in_dim(live_rows, first_here, half, 0))
    total_frames = lax.psum(count_term, ("teach", "dp"))
    stacked = soft_rows.reshape(2, half, vocab)
    both_soft = lax.all_to_all(stacked, "teach", split_axis=0, concat_axis=0, tiled=True)
    dest_half = lax.dynamic_slice_in_dim(dest_device, first_here, half, 0)
    slot_half = lax.dynamic_slice_in_dim(slot_index, first_here, half, 0)
    replicated = jnp.broadcast_to(
        student_hidden.reshape(1, data_count, most_slots, width),
        (teach_count, data_count, most_slots, width),
    ).reshape(devices, most_slots, width)
    arrived = lax.all_to_all(replicated, ("teach", "dp"), split_axis=0, concat_axis=0, tiled=True)
    hidden_rows = arrived[dest_half, slot_half]
    norm_rows, state_rows, log_probs = student_forward(hidden_rows, gain, out_weight, out_bias)
    grad_rows = combined_grads(both_soft[0], both_soft[1], log_probs)
    loss_term = -jnp.sum(
        (both_soft[0].astype(jnp.float32) + both_soft[1].astype(jnp.float32)) * log_probs
    )
    back_rows = lax.dot_general(
        grad_rows, out_weight, (((1,), (1,)), ((), ())), preferred_element_type=jnp.float32
    )
    gain_grad = jnp.sum(back_rows * norm_rows, axis=0)
    bias_grad = jnp.sum(grad_rows.astype(jnp.float32), axis=0)
    weight_grad = lax.psum_scatter(
        lax.dot_general(
            state_rows, grad_rows, (((0,), (0,)), ((), ())), preferred_element_type=jnp.float32
        ),
        ("teach", "dp"),
        scatter_dimension=0,
        tiled=True,
    )
    gain_sum, bias_sum, loss_sum = lax.psum((gain_grad, bias_grad, loss_term), ("teach", "dp"))
    inverse = 1.0 / total_frames
    return (weight_grad * inverse, gain_sum * inverse, bias_sum * inverse, loss_sum * inverse)


def solution(mesh):
    return jax.shard_map(
        body,
        mesh=mesh,
        in_specs=(
            P("teach", "dp", None),
            P("dp", None),
            P("dp"),
            P("dp"),
            P("dp"),
            P(("teach", "dp"), None),
            P(),
            P(),
            P(),
        ),
        out_specs=(P(("teach", "dp"), None), P(), P(), P()),
        check_vma=False,
    )
```

profile of v0, /device:TPU:0, one launch (start us, length us, event | category | flops | bytes accessed | tf_op | source)
XLA Modules:
  0.0 527.8 jit_solution(4685215784094541084)
XLA Ops:
  7.2 0.0 copy-start
  7.2 2.3 broadcast_in_dim.23
  9.5 7.5 %all-to-all-start = ((bf16[32,16,1024]{2,1,0:T(8,128)(2,1)}), bf16[32,16,1024]{2,1,0:T(8,128)(2,1)}, u32[]{:S(2)}, u32[]{:S(2)}) async-start(bf16[32,16,1024]{2,1,0:T(8,128)(2,1)} %bitcast.52), calls=%async_computation | async-start | bytes 2097152 | tf_op jit(solution)/shard_map/all_to_all | solution.py:85
  17.6 0.0 copy-done
  17.6 4.0 copy.13
  21.6 0.0 copy-start.7
  21.6 0.7 reduce_max.28
  22.3 0.0 copy-done.7
  22.3 0.2 fusion.5
  22.5 0.0 copy-start.6
  22.5 5.9 %copy.14 = f32[2,128,5000]{1,2,0:T(8,128)} copy(f32[2,128,5000]{2,1,0:T(8,128)} %bitcast.51) | data formatting | bytes 10240000 | tf_op jit(solution)/shard_map/convert_element_type | solution.py:34
  28.4 0.0 copy-start.5
  28.4 0.1 fusion.18
  28.5 0.0 copy-done.6
  28.5 0.9 fusion.1
  29.4 0.0 copy-done.5
  29.4 5.7 %multiply_convert_fusion = bf16[2,128,5000]{1,2,0:T(8,128)(2,1)} fusion(f32[2,128,5000]{1,2,0:T(8,128)} %copy.14, s32[2,128]{1,0:T(2,128)S(1)} %bitcast.55, f32[2,128]{1,0:T(2,128)S(1)} %bitcast.54, f32[2,128]{1,0:T(2,128)S(1)} %get-tuple-element.12, f32[2,128]{1,0:T(2,128)S(1)} %multiply_bitcast_fusion, f32[2,128]{1,0:T(2,128)S(1)} %compare_convert_fusion.1), kind=kLoop, calls=%fused_computation.5 | loop fusion | flops 10240000 | bytes 7685120 | tf_op jit(solution)/shard_map/convert_element_type | solution.py:39
  35.1 9.9 %all-to-all-done = bf16[32,16,1024]{2,1,0:T(8,128)(2,1)} async-done(((bf16[32,16,1024]{2,1,0:T(8,128)(2,1)}), bf16[32,16,1024]{2,1,0:T(8,128)(2,1)}, u32[]{:S(2)}, u32[]{:S(2)}) %all-to-all-start) | async-done | bytes 1048608 | tf_op jit(solution)/shard_map/all_to_all | solution.py:85
  45.0 5.0 all-to-all-start.1
  50.0 0.0 copy-start.3
  50.0 0.0 copy-start.4
  50.0 0.2 reduce-scatter.2.cloned.1.call-start
  50.2 2.3 gather_fusion
  52.5 0.1 convert_reduce_fusion.1
  52.7 0.2 fusion.10
  52.9 0.0 copy-done.3
  52.9 0.0 copy-done.4
  52.9 6.3 %fusion.23 = (f32[128]{0:T(128)S(1)}, f32[128,5000]{0,1:T(8,128)S(1)}) fusion(f32[5000]{0:T(1024)S(1)} %copy-done.4, bf16[1024,5000]{0,1:T(8,128)(2,1)} %param.15, bf16[128,1024]{1,0:T(8,128)(2,1)S(1)} %gather_fusion, f32[1024]{0:T(1024)S(1)} %copy-done.3, f32[128]{0:T(128)S(1)} %add_rsqrt_fusion, f32[128]{0:T(128)S(1)} %broadcast_multiply_fusion.3), kind=kOutput, calls=%fused_computation.59 | convolution fusion | flops 1312655232 | bytes 13087776 | tf_op jit(solution)/shard_map/dot_general | solution.py:48
  59.3 0.7 exponential_reduce_fusion
  59.9 0.0 all-to-all-done.1
  60.0 3.0 multiply_reduce_fusion
  62.9 2.7 convert_reduce_fusion
  65.6 0.0 copy-start.1
  65.6 1.0 copy-done.1
  66.7 8.7 %fusion.19 = f32[1024,5000]{1,0:T(8,128)} fusion(bf16[128,5000]{0,1:T(8,128)(2,1)S(1)} %get-tuple-element.11, bf16[128,1024]{1,0:T(8,128)(2,1)S(1)} %gather_fusion, f32[1024]{0:T(1024)S(1)} %copy-done.3, f32[128]{0:T(128)S(1)} %add_rsqrt_fusion, f32[128]{0:T(128)S(1)} %broadcast_multiply_fusion.3), kind=kOutput, calls=%fused_computation.58 | convolution fusion | flops 1311375360 | bytes 22027264 | tf_op jit(solution)/shard_map/dot_general | solution.py:98
  75.3 0.0 copy-start.2
  75.3 0.0 reduce-scatter.2.cloned.1.call-update
  75.4 0.7 dynamic-slice_reduce_fusion
  76.7 0.0 copy-done.2
  76.7 6.1 %fusion.4 = f32[1024]{0:T(1024)S(1)} fusion(bf16[128,5000]{0,1:T(8,128)(2,1)S(1)} %copy-done.2, bf16[1024,5000]{0,1:T(8,128)(2,1)} %param.15, bf16[128,1024]{1,0:T(8,128)(2,1)S(1)} %gather_fusion, f32[128]{0:T(128)S(1)} %add_rsqrt_fusion, f32[128]{0:T(128)S(1)} %broadcast_multiply_fusion.3), kind=kOutput, calls=%fused_computation.18 | convolution fusion | flops 1311374336 | bytes 11787264 | tf_op jit(solution)/shard_map/dot_general | solution.py:92
  82.9 49.0 %all-reduce = (f32[]{:T(128)}, f32[1024]{0:T(1024)S(1)}, f32[5000]{0:T(1024)S(1)}, f32[]{:T(128)}) all-reduce(f32[]{:T(128)} %dynamic-slice_reduce_fusion, f32[1024]{0:T(1024)S(1)} %fusion.4, f32[5000]{0:T(1024)S(1)} %get-tuple-element.10, f32[]{:T(128)S(6)} %neg.3), channel_id=1, replica_groups=mesh['teach'=2,'dp'=16] {'teach','dp'}, use_global_device_ids=true, to_apply=%region_10.11 | all-reduce | flops 6026 | bytes 48208 | tf_op jit(solution)/shard_map/psum | solution.py:76
  133.2 0.6 broadcast_multiply_fusion.2
  133.8 0.6 broadcast_multiply_fusion.1
  134.4 383.4 %reduce-scatter.2.cloned.1.call-done = f32[32,5000]{1,0:T(8,128)} async-done(((f32[1024,5000]{1,0:T(8,128)}), f32[32,5000]{1,0:T(8,128)}) %reduce-scatter.2.cloned.1.call-update) | async-done | bytes 640016 | tf_op jit(solution)/shard_map/reduce_scatter | solution.py:97
  517.8 2.0 broadcast_multiply_fusion
  (8 shorter events, 0.1 us)
Async XLA Ops:
  7.2 10.4 %copy-start = (bf16[1,256,5000]{1,2,0:T(8,128)(2,1)S(1)}, bf16[1,256,5000]{1,2,0:T(8,128)(2,1)}, u32[]{:S(2)}) copy-start(bf16[1,256,5000]{1,2,0:T(8,128)(2,1)} %param.9) | copy-start | bytes 7680004
  9.5 35.5 %all-to-all-start = ((bf16[32,16,1024]{2,1,0:T(8,128)(2,1)}), bf16[32,16,1024]{2,1,0:T(8,128)(2,1)}, u32[]{:S(2)}, u32[]{:S(2)}) async-start(bf16[32,16,1024]{2,1,0:T(8,128)(2,1)} %bitcast.52), calls=%async_computation | async-start | bytes 2097152 | tf_op jit(solution)/shard_map/all_to_all | solution.py:85
  21.6 0.7 copy-start.7
  22.5 6.0 %copy-start.6 = (s32[256]{0:T(256)S(1)}, s32[256]{0:T(256)}, u32[]{:S(2)}) copy-start(s32[256]{0:T(256)} %param.11) | copy-start | bytes 3076
  28.4 1.0 copy-start.5
  45.0 15.0 %all-to-all-start.1 = ((bf16[2,128,5000]{1,2,0:T(8,128)(2,1)}), bf16[2,128,5000]{1,2,0:T(8,128)(2,1)}, u32[]{:S(2)}, u32[]{:S(2)}) async-start(bf16[2,128,5000]{1,2,0:T(8,128)(2,1)} %multiply_convert_fusion), calls=%async_computation.1 | async-start | bytes 5120000 | tf_op jit(solution)/shard_map/all_to_all | solution.py:78
  50.0 2.9 copy-start.3
  50.0 2.9 copy-start.4
  50.0 467.9 %reduce-scatter.2.cloned.1.call-start = ((), (), s32[]{:S(2)}) async-start(), calls=%async_computation.3 | async-start | bytes 21626880 | tf_op jit(solution)/shard_map/reduce_scatter | solution.py:97
  65.6 1.0 copy-start.1
  75.3 1.4 copy-start.2
Sparse Core Ops, SparseCore 0:
  75.5 442.3 reduce-scatter.1
where the time goes:
time: 531 us; the launch traced here: 528 us
  waiting for transfers between devices  393 us (74%)
  blocking collectives  49 us (9%)
  matrix products  21.3 us (4%)
  between operations  18 us (3%)
  other arithmetic  17.9 us (3%)
  local copies, waits for them, and re-layouts  15.6 us (3%)
  starting transfers between devices  12.7 us (2%)
    reduce_scatter x1, waiting for transfers between devices, body(): lax.psum_scatter(lax.dot_general(state_rows, grad_rows, (((0,), (0,)), ((...  383 us
    psum x1, blocking collectives, body(): total_frames = lax.psum(count_term, ('teach', 'dp'))  49 us
  transfers between devices with their start and end apart: 3, of which 2 were waited for; matrix products, arithmetic and copies ran while one was open for 7% of the time, Pallas kernels for 0%

commit v1 on v0

v1 whole, which is shorter than its diff:
```python
import jax
import jax.numpy as jnp
from jax import lax
from jax.sharding import PartitionSpec as P

LMAX = 256
EPSILON = 1e-05
LANES = 128
LOWEST = -1e30
F32 = jnp.float32
BF16 = jnp.bfloat16


def torus_factors(count):
    bits = count.bit_length() - 1
    small = bits // 3
    middle = (bits - small) // 2
    return 1 << small, 1 << middle, 1 << (bits - small - middle)


def rotation(count, stride, size, step):
    def moved(index):
        place = (index // stride) % size
        return index + ((place + step) % size - place) * stride

    return [(index, moved(index)) for index in range(count)]


def route_slots(dest_device):
    row_ids = jnp.arange(dest_device.shape[0], dtype=jnp.int32)
    same = (dest_device[:, None] == dest_device[None, :]) & (row_ids[None, :] < row_ids[:, None])
    return jnp.sum(same.astype(jnp.int32), axis=1)


def live_mask(lengths_block, row_total):
    row_ids = jnp.arange(row_total, dtype=jnp.int32)
    utterance = row_ids // LMAX
    frame_pos = row_ids % LMAX
    picks = utterance[:, None] == jnp.arange(lengths_block.shape[0], dtype=jnp.int32)[None, :]
    row_length = jnp.sum(jnp.where(picks, lengths_block[None, :], 0), axis=1)
    return (frame_pos < row_length).astype(F32)


def soft_targets(teacher_rows, agree_rows, target_rows, live_rows):
    probs_teacher = jax.nn.softmax(teacher_rows.astype(F32), axis=-1)
    onehot = (
        target_rows[:, None] == jnp.arange(probs_teacher.shape[1], dtype=jnp.int32)[None, :]
    ).astype(F32)
    weight = (0.5 * agree_rows.astype(F32))[:, None]
    return (live_rows[:, None] * (weight * probs_teacher + 0.5 * onehot)).astype(BF16)


def body(
    teacher_logits, routes, agreement, targets, lengths, student_hidden, out_weight, out_bias, gain
):
    cores = lax.axis_size("teach")
    chips = lax.axis_size("dp")
    devices = cores * chips
    rows = teacher_logits.shape[1]
    slots = cores * rows // devices
    vocab = teacher_logits.shape[2]
    width = student_hidden.shape[1]
    out_rows = width // devices
    size_a, size_b, size_c = torus_factors(chips)
    part = -(-vocab // (2 * cores * LANES)) * LANES
    half = 2 * part
    padded = cores * half
    core = lax.axis_index("teach")
    chip = lax.axis_index("dp")
    at_a = chip % size_a
    at_b = (chip // size_a) % size_b
    at_c = chip // (size_a * size_b)
    other = [(i, 1 - i) for i in range(cores)]

    def swap(value):
        return lax.ppermute(value, "teach", other)

    def along(value, stride, size, step):
        return lax.ppermute(value, "dp", rotation(chips, stride, size, step))

    def pick(whole, index):
        return jnp.where(index == 0, whole[..., :half], whole[..., half:])

    arrived = lax.all_to_all(
        student_hidden.reshape(chips, slots, width), "dp", split_axis=0, concat_axis=0, tiled=True
    ).reshape(chips * slots, width)
    arrived_other = swap(arrived)

    dest_device = routes[:, 0]
    slot_index = route_slots(dest_device)
    live_rows = live_mask(lengths, rows)
    soft_rows = soft_targets(teacher_logits[0], agreement, targets, live_rows)
    soft_rows = jnp.pad(soft_rows, ((0, 0), (0, padded - vocab)))
    soft_mine = pick(soft_rows, core)
    soft_other = swap(pick(soft_rows, 1 - core))
    soft_sum = soft_mine.astype(F32) + soft_other.astype(F32)

    weight_half = pick(jnp.pad(out_weight, ((0, 0), (0, padded - vocab))), core)
    bias_half = pick(jnp.pad(out_bias, (0, padded - vocab), constant_values=LOWEST), core)

    place = (dest_device % chips) * slots + slot_index
    ids = jnp.arange(chips * slots, dtype=jnp.int32)[None, :]
    from_core = (dest_device // chips)[:, None]
    hit = place[:, None] == ids
    hidden_rows = jnp.dot(
        (hit & (from_core == core)).astype(BF16), arrived, preferred_element_type=F32
    ) + jnp.dot(
        (hit & (from_core != core)).astype(BF16), arrived_other, preferred_element_type=F32
    )
    centre = jnp.mean(hidden_rows, axis=1, keepdims=True)
    spread = jnp.mean(jnp.square(hidden_rows - centre), axis=1, keepdims=True)
    normed = (hidden_rows - centre) * lax.rsqrt(spread + EPSILON)
    scaled = (normed * gain[None, :]).astype(BF16)

    logits = jnp.dot(scaled, weight_half, preferred_element_type=F32) + bias_half[None, :]
    top = jnp.max(logits, axis=1)
    total = jnp.sum(jnp.exp(logits - top[:, None]), axis=1)
    mass_half = jnp.sum(soft_sum, axis=1)
    stats = jnp.stack([top, total, mass_half])
    stats_other = swap(stats)
    top_all = jnp.maximum(top, stats_other[0])
    total_all = total * jnp.exp(top - top_all) + stats_other[1] * jnp.exp(stats_other[0] - top_all)
    mass = (mass_half + stats_other[2])[:, None]
    log_probs = logits - top_all[:, None] - jnp.log(total_all)[:, None]
    grad = (
        mass * jnp.exp(log_probs) - soft_mine.astype(F32) - soft_other.astype(F32)
    ).astype(BF16)
    loss_term = -jnp.sum(soft_sum * log_probs)

    by_place = scaled.reshape(rows, cores, size_c, size_b, size_a, out_rows)

    def part_of(grad_part, axis_index, near, far):
        near_at, near_stride, near_size = near
        far_at, far_stride, far_size = far
        order = (axis_index, 7 - axis_index, 2, 1, 5)
        ordered = jnp.transpose(by_place, (0,) + order).reshape(rows, near_size, -1)
        partial = None
        for step in range(near_size):
            states = lax.dynamic_index_in_dim(
                ordered, (near_at + step) % near_size, 1, keepdims=False
            )
            grads = grad_part
            if step:
                states = along(states, near_stride, near_size, step)
                grads = along(grads, near_stride, near_size, step)
            term = lax.dot_general(
                states, grads, (((0,), (0,)), ((), ())), preferred_element_type=F32
            )
            partial = term if partial is None else partial + term

        def reduced(partial, at, stride, size):
            pieces = partial.reshape(size, partial.shape[0] // size, partial.shape[1])
            kept = lax.dynamic_index_in_dim(pieces, at, 0, keepdims=False)
            for step in range(1, size):
                sent = lax.dynamic_index_in_dim(pieces, (at + step) % size, 0, keepdims=False)
                kept = kept + along(sent.astype(BF16), stride, size, step).astype(F32)
            return kept

        partial = reduced(partial, far_at, far_stride, far_size)
        return reduced(partial, at_c, size_a * size_b, size_c)

    axis_a = (at_a, 1, size_a)
    axis_b = (at_b, size_a, size_b)
    first = part_of(grad[:, :part], 4, axis_a, axis_b)
    second = part_of(grad[:, part:], 3, axis_b, axis_a)
    mine = jnp.concatenate([first, second], axis=1).reshape(cores, out_rows, half)

    back = lax.dot_general(
        grad, weight_half, (((1,), (1,)), ((), ())), preferred_element_type=F32
    )
    small = jnp.concatenate(
        [
            jnp.sum(grad.astype(F32), axis=0),
            jnp.sum(back * normed, axis=0),
            loss_term[None],
            jnp.sum(live_rows)[None],
        ]
    )
    step = 1
    while step < chips:
        small = small + lax.ppermute(small, "dp", [(i, i ^ step) for i in range(chips)])
        step *= 2
    small_other = swap(small)
    inverse = 1.0 / small[half + width + 1]
    bias_low = jnp.where(core == 0, small[:half], small_other[:half])
    bias_high = jnp.where(core == 0, small_other[:half], small[:half])
    bias_sum = jnp.concatenate([bias_low, bias_high])[:vocab]
    rest = small[half:] + small_other[half:]

    kept = lax.dynamic_index_in_dim(mine, core, 0, keepdims=False) * inverse
    got = swap(lax.dynamic_index_in_dim(mine, 1 - core, 0, keepdims=False) * inverse)
    low = jnp.where(core == 0, kept, got)
    high = jnp.where(core == 0, got, kept)
    weight_grad = jnp.concatenate([low, high], axis=1)[:, :vocab]
    return (weight_grad, rest[:width] * inverse, bias_sum * inverse, rest[width] * inverse)


def solution(mesh):
    return jax.shard_map(
        body,
        mesh=mesh,
        in_specs=(
            P("teach", "dp", None),
            P("dp", None),
            P("dp"),
            P("dp"),
            P("dp"),
            P(("teach", "dp"), None),
            P(),
            P(),
            P(),
        ),
        out_specs=(P(("teach", "dp"), None), P(), P(), P()),
        check_vma=False,
    )
```

time: 531 us -> 147 us (0.28)
  waiting for transfers between devices: 393 us -> 66.3 us
  blocking collectives: 49 us -> 0 us
  starting transfers between devices: 12.7 us -> 33.5 us
  between operations: 18 us -> 4.82 us
  matrix products: 21.3 us -> 12.3 us
  local copies, waits for them, and re-layouts: 15.6 us -> 8.05 us
    reduce_scatter x1 -> x0, waiting for transfers between devices: 383 us -> none  [body(): lax.psum_scatter(lax.dot_general(state_rows, grad_rows, (((0,), (0,)), ((...]
    ppermute x0 -> x21, waiting for transfers between devices: none -> 51.1 us  [the longest x12 42.8 us: along(): return lax.ppermute(value, 'dp', rotation(chips, stride, size, step))]
    psum x1 -> x0, blocking collectives: 49 us -> none  [body(): total_frames = lax.psum(count_term, ('teach', 'dp'))]
    ppermute x0 -> x21, starting transfers between devices: none -> 25.6 us  [the longest x12 19.9 us: along(): return lax.ppermute(value, 'dp', rotation(chips, stride, size, step))]
    convert_element_type x2 -> x5, local copies, waits for them, and re-layouts: 9.89 us -> 0.48 us  [the longest x4 0.27 us: reduced(): kept = kept + along(sent.astype(BF16), stride, size, step).astype(F32)]
    dot_general x4 -> x8, matrix products: 21.3 us -> 12.3 us  [the longest x1 5.26 us: body(): jnp.dot(scaled, weight_half, preferred_element_type=F32)]
    all_to_all x2 -> x1, waiting for transfers between devices: 9.85 us -> 15.2 us  [body(): lax.all_to_all(student_hidden.reshape(chips, slots, width), 'dp', split_a...]
    all_to_all x2 -> x1, starting transfers between devices: 12.5 us -> 7.86 us  [body(): lax.all_to_all(student_hidden.reshape(chips, slots, width), 'dp', split_a...]
  transfers between devices with their start and end apart: 3 -> 22, of which waited for: 2 -> 13; matrix products, arithmetic and copies ran while one was open for 7% -> 10% of each run, Pallas kernels for 0% -> 0%
where the time goes in v1:
time: 147 us; the launch traced here: 146 us
  waiting for transfers between devices  66.3 us (45%)
  starting transfers between devices  33.5 us (23%)
  other arithmetic  21.1 us (14%)
  matrix products  12.3 us (8%)
  local copies, waits for them, and re-layouts  8.05 us (5%)
  between operations  4.82 us (3%)
    ppermute x12, waiting for transfers between devices, along(): return lax.ppermute(value, 'dp', rotation(chips, stride, size, step))  42.8 us
    ppermute x12, starting transfers between devices, along(): return lax.ppermute(value, 'dp', rotation(chips, stride, size, step))  19.9 us
    all_to_all x1, waiting for transfers between devices, body(): lax.all_to_all(student_hidden.reshape(chips, slots, width), 'dp', split_a...  15.2 us
    all_to_all x1, starting transfers between devices, body(): lax.all_to_all(student_hidden.reshape(chips, slots, width), 'dp', split_a...  7.86 us
    ppermute x4, waiting for transfers between devices, body(): lax.ppermute(small, 'dp', [(i, i ^ step) for i in range(chips)])  7.66 us
    dot_general x1, matrix products, body(): jnp.dot(scaled, weight_half, preferred_element_type=F32)  5.26 us
    ppermute x4, starting transfers between devices, body(): lax.ppermute(small, 'dp', [(i, i ^ step) for i in range(chips)])  4.59 us
    dot_general x4, matrix products, part_of(): lax.dot_general(states, grads, (((0,), (0,)), ((), ())), preferred_elemen...  4.52 us
  transfers between devices with their start and end apart: 22, of which 13 were waited for; matrix products, arithmetic and copies ran while one was open for 10% of the time, Pallas kernels for 0%

profile of v1, /device:TPU:0, one launch (start us, length us, event | category | flops | bytes accessed | tf_op | source)
XLA Modules:
  0.0 146.1 jit_solution(16031874480899984391)
XLA Ops:
  0.6 3.0 %copy.25 = bf16[1,256,5000]{2,1,0:T(8,128)(2,1)S(1)} copy(bf16[1,256,5000]{1,2,0:T(8,128)(2,1)} %param.9) | data formatting | bytes 5120000 | tf_op args[0]
  3.7 3.4 %reduce_max.23 = bf16[256]{0:T(256)(128)(2,1)S(1)} reduce(bf16[1,256,5000]{1,2,0:T(8,128)(2,1)} %param.9, bf16[]{:T(256)} %constant.209.clone.1), dimensions={0,2}, to_apply=%region_3.4 | reduce | flops 1279744 | bytes 2560514 | tf_op jit(solution)/shard_map/reduce_max | solution.py:45
  7.7 1.0 fusion.3
  8.7 4.0 %fusion.7 = bf16[256,5000]{1,0:T(8,128)(2,1)S(1)} fusion(bf16[1,256,5000]{2,1,0:T(8,128)(2,1)} %copy-done, s32[256]{0:T(256)S(1)} %copy-done.4, f32[256]{0:T(256)S(1)} %fusion.3, f32[256]{0:T(256)S(1)} %reduce_max.24, f32[256]{0:T(256)S(1)} %convert_multiply_fusion, f32[256]{0:T(256)S(1)} %compare_convert_fusion), kind=kLoop, calls=%fused_computation.10 | loop fusion | flops 11520000 | bytes 5125120 | tf_op jit(solution)/shard_map/convert_element_type | solution.py:50
  12.7 1.4 broadcast_select_fusion
  14.6 7.9 %all-to-all-start = ((bf16[16,16,1024]{2,1,0:T(8,128)(2,1)}), bf16[16,16,1024]{2,1,0:T(8,128)(2,1)S(1)}, u32[]{:S(2)}, u32[]{:S(2)}) async-start(bf16[16,16,1024]{2,1,0:T(8,128)(2,1)} %bitcast.107), calls=%async_computation | async-start | bytes 1048576 | tf_op jit(solution)/shard_map/all_to_all | solution.py:84
  22.8 15.2 %all-to-all-done = bf16[16,16,1024]{2,1,0:T(8,128)(2,1)S(1)} async-done(((bf16[16,16,1024]{2,1,0:T(8,128)(2,1)}), bf16[16,16,1024]{2,1,0:T(8,128)(2,1)S(1)}, u32[]{:S(2)}, u32[]{:S(2)}) %all-to-all-start) | async-done | bytes 524320 | tf_op jit(solution)/shard_map/all_to_all | solution.py:84
  38.3 2.0 %fusion.9 = (f32[256]{0:T(256)S(1)}, bf16[256,2560]{1,0:T(8,128)(2,1)S(1)}) fusion(bf16[256,2560]{1,0:T(8,128)(2,1)} %collective-permute-done.1, bf16[256,5000]{1,0:T(8,128)(2,1)S(1)} %fusion.7, pred[]{:T(512)S(6)} %eq.90), kind=kLoop, calls=%fused_computation.23 | loop fusion | flops 3276544 | bytes 6554625 | tf_op jit(solution)/shard_map/reduce_sum | solution.py:118
  41.3 5.3 %fusion.52 = (f32[256]{0:T(256)S(1)}, f32[256,2560]{1,0:T(8,128)S(1)}) fusion(f32[2560]{0:T(1024)S(1)} %fusion.38, bf16[256,1024]{1,0:T(8,128)(2,1)S(1)} %multiply_convert_fusion, bf16[1024,5000]{0,1:T(8,128)(2,1)} %param.15, pred[]{:T(512)S(6)} %eq.90), kind=kOutput, calls=%fused_computation.114 | convolution fusion | flops 1346109184 | bytes 18639872 | tf_op jit(solution)/shard_map/dot_general | solution.py:115
  47.1 0.6 collective-permute-start.2
  47.7 0.6 fusion.43
  48.5 4.2 %convert_reduce_fusion = (f32[2560]{0:T(1024)S(1)}, bf16[256,2560]{1,0:T(8,128)(2,1)S(1)}, f32[]{:T(128)}) fusion(bf16[256,2560]{1,0:T(8,128)(2,1)} %collective-permute-done.1, bf16[256,2560]{1,0:T(8,128)(2,1)S(1)} %get-tuple-element.11, f32[256]{0:T(256)S(1)} %get-tuple-element.8, f32[256,2560]{1,0:T(8,128)S(1)} %get-tuple-element.33, ...), kind=kLoop, calls=%fused_computation.19 | loop fusion | flops 8517119 | bytes 6566916 | tf_op jit(solution)/shard_map/reduce_sum | solution.py:173
  52.7 1.8 %fusion.10 = f32[1024]{0:T(1024)S(1)} fusion(bf16[256,2560]{1,0:T(8,128)(2,1)S(1)} %get-tuple-element.7, f32[256,1024]{1,0:T(8,128)S(1)} %get-tuple-element.31, f32[256]{0:T(256)S(1)} %add_rsqrt_fusion, f32[256]{0:T(256)S(1)} %broadcast_multiply_fusion, bf16[1024,5000]{0,1:T(8,128)(2,1)S(1)} %bitcast.119, pred[]{:T(512)S(6)} %eq.90), kind=kOutput, calls=%fused_computation.32 | convolution fusion | flops 1345846272 | bytes 17848320 | tf_op jit(solution)/shard_map/dot_general | solution.py:168
  55.2 0.7 concatenate.13
  55.9 0.6 collective-permute-start.15
  56.5 3.2 %collective-permute-done.15 = f32[3586]{0:T(1024)S(1)} collective-permute-done((f32[3586]{0:T(1024)S(1)}, f32[3586]{0:T(1024)S(1)}, u32[]{:S(2)}, u32[]{:S(2)}) %collective-permute-start.15) | collective-permute-done | bytes 14376 | tf_op jit(solution)/shard_map/ppermute | solution.py:181
  59.6 1.2 collective-permute-start.16
  61.1 2.3 %collective-permute-done.16 = f32[3586]{0:T(1024)S(1)} collective-permute-done((f32[3586]{0:T(1024)S(1)}, f32[3586]{0:T(1024)S(1)}, u32[]{:S(2)}, u32[]{:S(2)}) %collective-permute-start.16) | collective-permute-done | bytes 14376 | tf_op jit(solution)/shard_map/ppermute | solution.py:181
  63.4 1.6 %collective-permute-start.17 = (f32[3586]{0:T(1024)S(1)}, f32[3586]{0:T(1024)S(1)}, u32[]{:S(2)}, u32[]{:S(2)}) collective-permute-start(f32[3586]{0:T(1024)S(1)} %add.272), channel_id=1, source_target_pairs={{0,4},{1,5},{2,6},{3,7},{4,0},{5,1},{6,2},{7,3},{8,12},{9,13},{10,... | collective-permute-start | bytes 43040 | tf_op jit(solution)/shard_map/ppermute | solution.py:181
  65.0 0.9 fusion.49
  65.9 0.9 collective-permute-start.10
  67.1 1.2 collective-permute-start.18
  68.3 0.8 copy.29
  69.2 0.7 collective-permute-start.9
  69.9 1.9 %collective-permute-done.18 = f32[3586]{0:T(1024)} collective-permute-done((f32[3586]{0:T(1024)S(1)}, f32[3586]{0:T(1024)}, u32[]{:S(2)}, u32[]{:S(2)}) %collective-permute-start.18) | collective-permute-done | bytes 14376 | tf_op jit(solution)/shard_map/ppermute | solution.py:181
  71.9 0.7 add.274
  72.6 0.8 copy.26
  73.5 0.6 collective-permute-start.3
  74.0 1.5 collective-permute-start.4
  75.5 0.6 slice.94
  78.0 8.3 %collective-permute-done.9 = bf16[256,512]{1,0:T(8,128)(2,1)} collective-permute-done((bf16[256,512]{1,0:T(8,128)(2,1)}, bf16[256,512]{1,0:T(8,128)(2,1)}, u32[]{:S(2)}, u32[]{:S(2)}) %collective-permute-start.9) | collective-permute-done | bytes 262176 | tf_op jit(solution)/shard_map/ppermute | solution.py:79
  86.2 1.7 %fusion.54 = f32[512,1280]{1,0:T(8,128)S(1)} fusion(bf16[256,512]{1,0:T(8,128)(2,1)} %collective-permute-done.9, bf16[256,1280]{1,0:T(8,128)(2,1)} %collective-permute-done.10), kind=kOutput, calls=%fused_computation.116 | convolution fusion | flops 335544320 | bytes 3538944 | tf_op jit(solution)/shard_map/dot_general | solution.py:146
  88.6 0.6 collective-permute-start.11
  89.2 7.8 %collective-permute-done.4 = bf16[256,1280]{1,0:T(8,128)(2,1)} collective-permute-done((bf16[256,1280]{1,0:T(8,128)(2,1)S(1)}, bf16[256,1280]{1,0:T(8,128)(2,1)}, u32[]{:S(2)}, u32[]{:S(2)}) %collective-permute-start.4) | collective-permute-done | bytes 655392 | tf_op jit(solution)/shard_map/ppermute | solution.py:79
  97.0 1.7 %fusion.53 = f32[512,1280]{1,0:T(8,128)S(1)} fusion(bf16[256,512]{1,0:T(8,128)(2,1)} %collective-permute-done.3, bf16[256,1280]{1,0:T(8,128)(2,1)} %collective-permute-done.4), kind=kOutput, calls=%fused_computation.115 | convolution fusion | flops 335544320 | bytes 3538944 | tf_op jit(solution)/shard_map/dot_general | solution.py:146
  99.4 1.3 collective-permute-start.5
  100.7 9.8 %collective-permute-done.11 = bf16[256,1280]{1,0:T(8,128)(2,1)S(1)} collective-permute-done((bf16[256,1280]{1,0:T(8,128)(2,1)S(1)}, bf16[256,1280]{1,0:T(8,128)(2,1)S(1)}, u32[]{:S(2)}, u32[]{:S(2)}) %collective-permute-start.11) | collective-permute-done | bytes 655392 | tf_op jit(solution)/shard_map/ppermute | solution.py:79
  110.7 1.9 %collective-permute-start.14 = (bf16[64,1280]{1,0:T(8,128)(2,1)S(1)}, bf16[64,1280]{1,0:T(8,128)(2,1)S(1)}, u32[]{:S(2)}, u32[]{:S(2)}) collective-permute-start(bf16[64,1280]{1,0:T(8,128)(2,1)S(1)} %get-tuple-element.19), channel_id=1, source_target_pairs={{0,12},{1,13},{2,14},{3,15},{4,0},{5,1},{6,2},{7,3},{8,4},{9,5},{1... | collective-permute-start | bytes 491528 | tf_op jit(solution)/shard_map/ppermute | solution.py:79
  112.6 1.2 collective-permute-start.13
  113.9 1.3 collective-permute-done.5
  115.4 2.4 %collective-permute-start.8 = (bf16[64,1280]{1,0:T(8,128)(2,1)S(1)}, bf16[64,1280]{1,0:T(8,128)(2,1)S(1)}, u32[]{:S(2)}, u32[]{:S(2)}) collective-permute-start(bf16[64,1280]{1,0:T(8,128)(2,1)S(1)} %get-tuple-element.14), channel_id=1, source_target_pairs={{0,12},{1,13},{2,14},{3,15},{4,0},{5,1},{6,2},{7,3},{8,4},{9,5},{1... | collective-permute-start | bytes 491528 | tf_op jit(solution)/shard_map/ppermute | solution.py:79
  117.9 0.7 collective-permute-start.7
  118.6 7.9 %collective-permute-start.6 = (bf16[64,1280]{1,0:T(8,128)(2,1)S(1)}, bf16[64,1280]{1,0:T(8,128)(2,1)S(1)}, u32[]{:S(2)}, u32[]{:S(2)}) collective-permute-start(bf16[64,1280]{1,0:T(8,128)(2,1)S(1)} %get-tuple-element.13), channel_id=1, source_target_pairs={{0,4},{1,5},{2,6},{3,7},{4,8},{5,9},{6,10},{7,11},{8,12},{9,13},{1... | collective-permute-start | bytes 491528 | tf_op jit(solution)/shard_map/ppermute | solution.py:79
  126.5 10.0 %collective-permute-done.13 = bf16[64,1280]{1,0:T(8,128)(2,1)S(1)} collective-permute-done((bf16[64,1280]{1,0:T(8,128)(2,1)S(1)}, bf16[64,1280]{1,0:T(8,128)(2,1)S(1)}, u32[]{:S(2)}, u32[]{:S(2)}) %collective-permute-start.13) | collective-permute-done | bytes 163872 | tf_op jit(solution)/shard_map/ppermute | solution.py:79
  136.5 5.6 %collective-permute-done.7 = bf16[64,1280]{1,0:T(8,128)(2,1)S(1)} collective-permute-done((bf16[64,1280]{1,0:T(8,128)(2,1)S(1)}, bf16[64,1280]{1,0:T(8,128)(2,1)S(1)}, u32[]{:S(2)}, u32[]{:S(2)}) %collective-permute-start.7) | collective-permute-done | bytes 163872 | tf_op jit(solution)/shard_map/ppermute | solution.py:79
  142.4 0.6 fusion.37
  143.0 0.6 slice_multiply_fusion
  144.1 0.9 pad_maximum_fusion
  (78 shorter events, 6.5 us)
Async XLA Ops:
  0.6 6.4 %copy-start.5 = (s32[256]{0:T(256)S(1)}, s32[256]{0:T(256)}, u32[]{:S(2)}) copy-start(s32[256]{0:T(256)} %param.11) | copy-start | bytes 3076
  3.6 4.1 %copy-start = (bf16[1,256,5000]{2,1,0:T(8,128)(2,1)}, bf16[1,256,5000]{2,1,0:T(8,128)(2,1)S(1)}, u32[]{:S(2)}) copy-start(bf16[1,256,5000]{2,1,0:T(8,128)(2,1)S(1)} %copy.25) | copy-start | bytes 7680004
  3.7 5.1 %copy-start.4 = (s32[256]{0:T(256)S(1)}, s32[256]{0:T(256)}, u32[]{:S(2)}) copy-start(s32[256]{0:T(256)} %param.12) | copy-start | bytes 3076
  12.7 9.8 %copy-start.2 = (s32[256,1]{0,1:T(1,128)S(1)}, s32[256,1]{0,1:T(1,128)}, u32[]{:S(2)}) copy-start(s32[256,1]{0,1:T(1,128)} %param.10) | copy-start | bytes 3076
  12.7 10.0 %copy-start.1 = (f32[5000]{0:T(1024)S(1)}, f32[5000]{0:T(1024)}, u32[]{:S(2)}) copy-start(f32[5000]{0:T(1024)} %param.16) | copy-start | bytes 60004
  14.1 24.2 %collective-permute-start.1 = (bf16[256,2560]{1,0:T(8,128)(2,1)}, bf16[256,2560]{1,0:T(8,128)(2,1)}, u32[]{:S(2)}, u32[]{:S(2)}) collective-permute-start(bf16[256,2560]{1,0:T(8,128)(2,1)} %broadcast_select_fusion), channel_id=1, source_target_pairs={{0,16},{16,0},{1,17},{17,1},{2,18},{18,2},{3,19},{19,3},{4,20},{20... | collective-permute-start | bytes 3932168 | tf_op jit(solution)/shard_map/ppermute | solution.py:76
  14.6 23.4 %all-to-all-start = ((bf16[16,16,1024]{2,1,0:T(8,128)(2,1)}), bf16[16,16,1024]{2,1,0:T(8,128)(2,1)S(1)}, u32[]{:S(2)}, u32[]{:S(2)}) async-start(bf16[16,16,1024]{2,1,0:T(8,128)(2,1)} %bitcast.107), calls=%async_computation | async-start | bytes 1048576 | tf_op jit(solution)/shard_map/all_to_all | solution.py:84
  38.0 2.4 %collective-permute-start = (bf16[256,1024]{1,0:T(8,128)(2,1)S(1)}, bf16[256,1024]{1,0:T(8,128)(2,1)S(1)}, u32[]{:S(2)}, u32[]{:S(2)}) collective-permute-start(bf16[256,1024]{1,0:T(8,128)(2,1)S(1)} %bitcast.105), channel_id=1, source_target_pairs={{0,16},{16,0},{1,17},{17,1},{2,18},{18,2},{3,19},{19,3},{4,20},{20... | collective-permute-start | bytes 1572872 | tf_op jit(solution)/shard_map/ppermute | solution.py:76
  40.3 0.7 copy-start.3
  41.1 11.7 %slice-start = ((s8[10240000]{0:T(1024)(128)(4,1)}), s8[4194304]{0:T(1024)(128)(4,1)S(1)}, s32[]{:S(2)}) async-start(s8[10240000]{0:T(1024)(128)(4,1)} %bitcast.118), calls=%async_computation.1 | async-start | bytes 8388608
  41.3 11.5 %slice-start.1 = ((s8[10240000]{0:T(1024)(128)(4,1)}), s8[4194304]{0:T(1024)(128)(4,1)S(1)}, s32[]{:S(2)}) async-start(s8[10240000]{0:T(1024)(128)(4,1)} %bitcast.118), calls=%async_computation.2 | async-start | bytes 8388608
  41.3 11.4 %slice-start.2 = ((s8[10240000]{0:T(1024)(128)(4,1)}), s8[1851392]{0:T(1024)(128)(4,1)S(1)}, s32[]{:S(2)}) async-start(s8[10240000]{0:T(1024)(128)(4,1)} %bitcast.118), calls=%async_computation.3 | async-start | bytes 3702784
  47.1 1.4 collective-permute-start.2
  55.9 3.7 %collective-permute-start.15 = (f32[3586]{0:T(1024)S(1)}, f32[3586]{0:T(1024)S(1)}, u32[]{:S(2)}, u32[]{:S(2)}) collective-permute-start(f32[3586]{0:T(1024)S(1)} %concatenate.13), channel_id=1, source_target_pairs={{0,1},{1,0},{2,3},{3,2},{4,5},{5,4},{6,7},{7,6},{8,9},{9,8},{10,11... | collective-permute-start | bytes 43040 | tf_op jit(solution)/shard_map/ppermute | solution.py:181
  59.6 3.7 %collective-permute-start.16 = (f32[3586]{0:T(1024)S(1)}, f32[3586]{0:T(1024)S(1)}, u32[]{:S(2)}, u32[]{:S(2)}) collective-permute-start(f32[3586]{0:T(1024)S(1)} %add.271), channel_id=1, source_target_pairs={{0,2},{1,3},{2,0},{3,1},{4,6},{5,7},{6,4},{7,5},{8,10},{9,11},{10,... | collective-permute-start | bytes 43040 | tf_op jit(solution)/shard_map/ppermute | solution.py:181
  63.4 3.7 %collective-permute-start.17 = (f32[3586]{0:T(1024)S(1)}, f32[3586]{0:T(1024)S(1)}, u32[]{:S(2)}, u32[]{:S(2)}) collective-permute-start(f32[3586]{0:T(1024)S(1)} %add.272), channel_id=1, source_target_pairs={{0,4},{1,5},{2,6},{3,7},{4,0},{5,1},{6,2},{7,3},{8,12},{9,13},{10,... | collective-permute-start | bytes 43040 | tf_op jit(solution)/shard_map/ppermute | solution.py:181
  65.9 20.3 %collective-permute-start.10 = (bf16[256,1280]{1,0:T(8,128)(2,1)}, bf16[256,1280]{1,0:T(8,128)(2,1)}, u32[]{:S(2)}, u32[]{:S(2)}) collective-permute-start(bf16[256,1280]{1,0:T(8,128)(2,1)} %get-tuple-element.17), channel_id=1, source_target_pairs={{0,2},{1,3},{2,0},{3,1},{4,6},{5,7},{6,4},{7,5},{8,10},{9,11},{10,... | collective-permute-start | bytes 1966088 | tf_op jit(solution)/shard_map/ppermute | solution.py:79
  67.1 4.7 %collective-permute-start.18 = (f32[3586]{0:T(1024)S(1)}, f32[3586]{0:T(1024)}, u32[]{:S(2)}, u32[]{:S(2)}) collective-permute-start(f32[3586]{0:T(1024)S(1)} %add.273), channel_id=1, source_target_pairs={{0,8},{1,9},{2,10},{3,11},{4,12},{5,13},{6,14},{7,15},{8,0},{9,1},... | collective-permute-start | bytes 43040 | tf_op jit(solution)/shard_map/ppermute | solution.py:181
  69.2 17.0 %collective-permute-start.9 = (bf16[256,512]{1,0:T(8,128)(2,1)}, bf16[256,512]{1,0:T(8,128)(2,1)}, u32[]{:S(2)}, u32[]{:S(2)}) collective-permute-start(bf16[256,512]{1,0:T(8,128)(2,1)} %bitcast.29), channel_id=1, source_target_pairs={{0,2},{1,3},{2,0},{3,1},{4,6},{5,7},{6,4},{7,5},{8,10},{9,11},{10,... | collective-permute-start | bytes 786440 | tf_op jit(solution)/shard_map/ppermute | solution.py:79
  72.6 4.2 %collective-permute-start.20 = (f32[3586]{0:T(1024)S(1)}, f32[3586]{0:T(1024)S(1)}, u32[]{:S(2)}, u32[]{:S(2)}) collective-permute-start(f32[3586]{0:T(1024)S(1)} %add.274), channel_id=1, source_target_pairs={{0,16},{16,0},{1,17},{17,1},{2,18},{18,2},{3,19},{19,3},{4,20},{20... | collective-permute-start | bytes 43040 | tf_op jit(solution)/shard_map/ppermute | solution.py:76
  73.5 15.7 %collective-permute-start.3 = (bf16[256,512]{1,0:T(8,128)(2,1)}, bf16[256,512]{1,0:T(8,128)(2,1)}, u32[]{:S(2)}, u32[]{:S(2)}) collective-permute-start(bf16[256,512]{1,0:T(8,128)(2,1)} %bitcast.17), channel_id=1, source_target_pairs={{0,1},{1,0},{2,3},{3,2},{4,5},{5,4},{6,7},{7,6},{8,9},{9,8},{10,11... | collective-permute-start | bytes 786440 | tf_op jit(solution)/shard_map/ppermute | solution.py:79
  74.0 23.0 %collective-permute-start.4 = (bf16[256,1280]{1,0:T(8,128)(2,1)S(1)}, bf16[256,1280]{1,0:T(8,128)(2,1)}, u32[]{:S(2)}, u32[]{:S(2)}) collective-permute-start(bf16[256,1280]{1,0:T(8,128)(2,1)S(1)} %get-tuple-element.16), channel_id=1, source_target_pairs={{0,1},{1,0},{2,3},{3,2},{4,5},{5,4},{6,7},{7,6},{8,9},{9,8},{10,11... | collective-permute-start | bytes 1966088 | tf_op jit(solution)/shard_map/ppermute | solution.py:79
  88.6 21.9 %collective-permute-start.11 = (bf16[256,1280]{1,0:T(8,128)(2,1)S(1)}, bf16[256,1280]{1,0:T(8,128)(2,1)S(1)}, u32[]{:S(2)}, u32[]{:S(2)}) collective-permute-start(bf16[256,1280]{1,0:T(8,128)(2,1)S(1)} %fusion.12), channel_id=1, source_target_pairs={{0,1},{1,0},{2,3},{3,2},{4,5},{5,4},{6,7},{7,6},{8,9},{9,8},{10,11... | collective-permute-start | bytes 1966088 | tf_op jit(solution)/shard_map/ppermute | solution.py:79
  99.4 15.9 %collective-permute-start.5 = (bf16[256,1280]{1,0:T(8,128)(2,1)S(1)}, bf16[256,1280]{1,0:T(8,128)(2,1)S(1)}, u32[]{:S(2)}, u32[]{:S(2)}) collective-permute-start(bf16[256,1280]{1,0:T(8,128)(2,1)S(1)} %fusion.11), channel_id=1, source_target_pairs={{0,2},{1,3},{2,0},{3,1},{4,6},{5,7},{6,4},{7,5},{8,10},{9,11},{10,... | collective-permute-start | bytes 1966088 | tf_op jit(solution)/shard_map/ppermute | solution.py:79
  110.7 7.9 %collective-permute-start.14 = (bf16[64,1280]{1,0:T(8,128)(2,1)S(1)}, bf16[64,1280]{1,0:T(8,128)(2,1)S(1)}, u32[]{:S(2)}, u32[]{:S(2)}) collective-permute-start(bf16[64,1280]{1,0:T(8,128)(2,1)S(1)} %get-tuple-element.19), channel_id=1, source_target_pairs={{0,12},{1,13},{2,14},{3,15},{4,0},{5,1},{6,2},{7,3},{8,4},{9,5},{1... | collective-permute-start | bytes 491528 | tf_op jit(solution)/shard_map/ppermute | solution.py:79
  112.6 23.8 %collective-permute-start.13 = (bf16[64,1280]{1,0:T(8,128)(2,1)S(1)}, bf16[64,1280]{1,0:T(8,128)(2,1)S(1)}, u32[]{:S(2)}, u32[]{:S(2)}) collective-permute-start(bf16[64,1280]{1,0:T(8,128)(2,1)S(1)} %get-tuple-element.20), channel_id=1, source_target_pairs={{0,8},{1,9},{2,10},{3,11},{4,12},{5,13},{6,14},{7,15},{8,0},{9,1},... | collective-permute-start | bytes 491528 | tf_op jit(solution)/shard_map/ppermute | solution.py:79
  113.8 22.6 %collective-permute-start.12 = (bf16[64,1280]{1,0:T(8,128)(2,1)S(1)}, bf16[64,1280]{1,0:T(8,128)(2,1)S(1)}, u32[]{:S(2)}, u32[]{:S(2)}) collective-permute-start(bf16[64,1280]{1,0:T(8,128)(2,1)S(1)} %get-tuple-element.18), channel_id=1, source_target_pairs={{0,4},{1,5},{2,6},{3,7},{4,8},{5,9},{6,10},{7,11},{8,12},{9,13},{1... | collective-permute-start | bytes 491528 | tf_op jit(solution)/shard_map/ppermute | solution.py:79
  115.4 21.1 %collective-permute-start.8 = (bf16[64,1280]{1,0:T(8,128)(2,1)S(1)}, bf16[64,1280]{1,0:T(8,128)(2,1)S(1)}, u32[]{:S(2)}, u32[]{:S(2)}) collective-permute-start(bf16[64,1280]{1,0:T(8,128)(2,1)S(1)} %get-tuple-element.14), channel_id=1, source_target_pairs={{0,12},{1,13},{2,14},{3,15},{4,0},{5,1},{6,2},{7,3},{8,4},{9,5},{1... | collective-permute-start | bytes 491528 | tf_op jit(solution)/shard_map/ppermute | solution.py:79
  117.9 24.3 %collective-permute-start.7 = (bf16[64,1280]{1,0:T(8,128)(2,1)S(1)}, bf16[64,1280]{1,0:T(8,128)(2,1)S(1)}, u32[]{:S(2)}, u32[]{:S(2)}) collective-permute-start(bf16[64,1280]{1,0:T(8,128)(2,1)S(1)} %get-tuple-element.15), channel_id=1, source_target_pairs={{0,8},{1,9},{2,10},{3,11},{4,12},{5,13},{6,14},{7,15},{8,0},{9,1},... | collective-permute-start | bytes 491528 | tf_op jit(solution)/shard_map/ppermute | solution.py:79
  118.6 23.6 %collective-permute-start.6 = (bf16[64,1280]{1,0:T(8,128)(2,1)S(1)}, bf16[64,1280]{1,0:T(8,128)(2,1)S(1)}, u32[]{:S(2)}, u32[]{:S(2)}) collective-permute-start(bf16[64,1280]{1,0:T(8,128)(2,1)S(1)} %get-tuple-element.13), channel_id=1, source_target_pairs={{0,4},{1,5},{2,6},{3,7},{4,8},{5,9},{6,10},{7,11},{8,12},{9,13},{1... | collective-permute-start | bytes 491528 | tf_op jit(solution)/shard_map/ppermute | solution.py:79
  142.3 1.7 %collective-permute-start.19 = (f32[32,2560]{1,0:T(8,128)S(1)}, f32[32,2560]{1,0:T(8,128)S(1)}, u32[]{:S(2)}, u32[]{:S(2)}) collective-permute-start(f32[32,2560]{1,0:T(8,128)S(1)} %multiply_bitcast_fusion), channel_id=1, source_target_pairs={{0,16},{16,0},{1,17},{17,1},{2,18},{18,2},{3,19},{19,3},{4,20},{20... | collective-permute-start | bytes 983048 | tf_op jit(solution)/shard_map/ppermute | solution.py:76

commit v2 on v0

v2 whole, which is shorter than its diff:
```python
import functools

import jax
import jax.numpy as jnp
from jax import lax
from jax.experimental import pallas as pl
from jax.experimental.pallas import tpu as pltpu
from jax.sharding import PartitionSpec as P

LMAX = 256
EPSILON = 1e-05
LANES = 128
TILES = 4
LOWEST = -1e30
F32 = jnp.float32
BF16 = jnp.bfloat16


def bits_of(count):
    return count.bit_length() - 1


def torus_factors(count):
    bits = bits_of(count)
    small = bits // 3
    middle = (bits - small) // 2
    return 1 << small, 1 << middle, 1 << (bits - small - middle)


def rotation(count, stride, size, step):
    def moved(index):
        place = (index // stride) % size
        return index + ((place + step) % size - place) * stride

    return [(index, moved(index)) for index in range(count)]


def route_slots(dest_device):
    row_ids = jnp.arange(dest_device.shape[0], dtype=jnp.int32)
    same = (dest_device[:, None] == dest_device[None, :]) & (row_ids[None, :] < row_ids[:, None])
    return jnp.sum(same.astype(jnp.int32), axis=1)


def live_mask(lengths_block, row_total):
    row_ids = jnp.arange(row_total, dtype=jnp.int32)
    utterance = row_ids // LMAX
    frame_pos = row_ids % LMAX
    picks = utterance[:, None] == jnp.arange(lengths_block.shape[0], dtype=jnp.int32)[None, :]
    row_length = jnp.sum(jnp.where(picks, lengths_block[None, :], 0), axis=1)
    return (frame_pos < row_length).astype(F32)


def call(kernel, name, grid, in_specs, out_specs, out_shape, scratch=(), prefetch=1):
    return pl.pallas_call(
        kernel,
        name=name,
        grid_spec=pltpu.PrefetchScalarGridSpec(
            num_scalar_prefetch=prefetch,
            grid=grid,
            in_specs=in_specs,
            out_specs=out_specs,
            scratch_shapes=list(scratch),
        ),
        out_shape=out_shape,
        compiler_params=pltpu.CompilerParams(
            dimension_semantics=("arbitrary",) * len(grid), vmem_limit_bytes=48 << 20
        ),
    )


def shape(*dims, dtype=F32):
    return jax.ShapeDtypeStruct(dims, dtype)


def soft_kernel(half, core_ref, logits_ref, weight_ref, hot_ref, target_ref, mine_ref, other_ref, mass_ref):
    rows, vocab = logits_ref.shape
    values = logits_ref[...].astype(F32)
    values = jnp.exp(values - jnp.max(values, axis=1, keepdims=True))
    scale = weight_ref[...] / jnp.sum(values, axis=1, keepdims=True)
    pieces = lax.broadcasted_iota(jnp.int32, (rows, vocab), 1)
    hot = jnp.where(pieces == target_ref[...], hot_ref[...], 0.0)
    soft = (values * scale + hot).astype(BF16)
    mass_ref[...] = jnp.sum(soft.astype(F32), axis=1, keepdims=True)
    low = soft[:, :half]
    first = core_ref[0] == 0

    @pl.when(first)
    def _():
        mine_ref[...] = low
        other_ref[...] = jnp.zeros_like(other_ref)
        other_ref[:, : vocab - half] = soft[:, half:]

    @pl.when(jnp.logical_not(first))
    def _():
        other_ref[...] = low
        mine_ref[...] = jnp.zeros_like(mine_ref)
        mine_ref[:, : vocab - half] = soft[:, half:]


def soft_targets(core, half, logits, weight, hot, target):
    rows, vocab = logits.shape
    block = 32
    column = pl.BlockSpec((block, 1), lambda i, c: (i, 0))
    piece = pl.BlockSpec((block, half), lambda i, c: (i, 0))
    return call(
        functools.partial(soft_kernel, half),
        "soft",
        (rows // block,),
        [pl.BlockSpec((block, vocab), lambda i, c: (i, 0)), column, column, column],
        [piece, piece, column],
        [shape(rows, half, dtype=BF16), shape(rows, half, dtype=BF16), shape(rows, 1)],
    )(core, logits, weight, hot, target)


def select_kernel(place_ref, near_ref, far_ref, gain_ref, normed_ref, scaled_ref, turned_ref):
    rows = place_ref.shape[0]
    count = near_ref.shape[0]
    ids = lax.broadcasted_iota(jnp.int32, (rows, count), 1)
    place = place_ref[...]
    hidden = jnp.dot(
        (place == ids).astype(F32).astype(BF16), near_ref[...], preferred_element_type=F32
    ) + jnp.dot(
        (place - count == ids).astype(F32).astype(BF16), far_ref[...], preferred_element_type=F32
    )
    centre = jnp.mean(hidden, axis=1, keepdims=True)
    moved = hidden - centre
    spread = jnp.mean(moved * moved, axis=1, keepdims=True)
    normed = moved * lax.rsqrt(spread + EPSILON)
    scaled = normed * gain_ref[...]
    normed_ref[...] = normed
    scaled_ref[...] = scaled.astype(BF16)
    turned_ref[...] = scaled.T.astype(BF16)


def select_states(place, near, far, gain):
    rows = place.shape[0]
    width = near.shape[1]
    return pl.pallas_call(
        select_kernel,
        name="select",
        out_shape=[
            shape(rows, width),
            shape(rows, width, dtype=BF16),
            shape(width, rows, dtype=BF16),
        ],
        compiler_params=pltpu.CompilerParams(vmem_limit_bytes=48 << 20),
    )(place, near, far, gain)


def forward_kernel(
    vocab, core_ref, scaled_ref, weight_ref, bias_ref, mine_ref, other_ref,
    powers_ref, tops_ref, totals_ref, dots_ref,
):
    step = pl.program_id(0)
    rows, tile = powers_ref.shape
    start = (core_ref[0] * pl.num_programs(0) + step) * tile
    logits = jnp.dot(scaled_ref[...], weight_ref[...], preferred_element_type=F32) + bias_ref[...]
    pieces = lax.broadcasted_iota(jnp.int32, (rows, tile), 1) + start
    logits = jnp.where(pieces < vocab, logits, LOWEST)
    top = jnp.max(logits, axis=1, keepdims=True)
    powers = jnp.exp(logits - top)
    powers_ref[...] = powers
    soft = mine_ref[...].astype(F32) + other_ref[...].astype(F32)

    @pl.when(step == 0)
    def _():
        tops_ref[...] = jnp.full_like(tops_ref, LOWEST)
        totals_ref[...] = jnp.zeros_like(totals_ref)
        dots_ref[...] = jnp.zeros_like(dots_ref)

    lane = lax.broadcasted_iota(jnp.int32, tops_ref.shape, 1) == step
    tops_ref[...] = jnp.where(lane, top, tops_ref[...])
    totals_ref[...] = jnp.where(lane, jnp.sum(powers, axis=1, keepdims=True), totals_ref[...])
    dots_ref[...] += jnp.sum(soft * logits, axis=1, keepdims=True)


def student_forward(core, vocab, tile, scaled, weight, bias, mine, other):
    rows, width = scaled.shape
    last = -(-vocab // tile) - 1
    whole = pl.BlockSpec((rows, width), lambda j, c: (0, 0))
    stat = pl.BlockSpec((rows, LANES), lambda j, c: (0, 0))
    piece = pl.BlockSpec((rows, tile), lambda j, c: (0, j))

    def at(j, c):
        return (0, jnp.minimum(c[0] * TILES + j, last))

    return call(
        functools.partial(forward_kernel, vocab),
        "forward",
        (TILES,),
        [whole, pl.BlockSpec((width, tile), at), pl.BlockSpec((1, tile), at), piece, piece],
        [piece, stat, stat, pl.BlockSpec((rows, 1), lambda j, c: (0, 0))],
        [shape(rows, TILES * tile), shape(rows, LANES), shape(rows, LANES), shape(rows, 1)],
    )(core, scaled, weight, bias, mine, other)


def grad_kernel(
    tiles, step_ref, powers_ref, tops_ref, totals_ref, tops_far_ref, totals_far_ref,
    mass_ref, mass_far_ref, dots_ref, mine_ref, other_ref,
    *out_refs,
):
    step = pl.program_id(0)
    tops, tops_far = tops_ref[...], tops_far_ref[...]
    top = jnp.maximum(
        jnp.max(tops, axis=1, keepdims=True), jnp.max(tops_far, axis=1, keepdims=True)
    )
    shrunk = jnp.exp(tops - top)
    total = jnp.sum(
        totals_ref[...] * shrunk + totals_far_ref[...] * jnp.exp(tops_far - top),
        axis=1,
        keepdims=True,
    )
    mass = mass_ref[...] + mass_far_ref[...]
    at = step_ref[0] + 2 * step
    lane = lax.broadcasted_iota(jnp.int32, shrunk.shape, 1) == at
    own = jnp.sum(jnp.where(lane, shrunk, 0.0), axis=1, keepdims=True)
    scale = mass * own / total
    grad = powers_ref[...] * scale - mine_ref[...].astype(F32) - other_ref[...].astype(F32)
    grad = grad.astype(BF16)
    bias = jnp.sum(grad.astype(F32), axis=0, keepdims=True)
    for index in range(tiles):

        @pl.when(step == index)
        def _(index=index):
            out_refs[index][...] = grad
            out_refs[tiles + index][...] = bias

    loss = 0.5 * mass * (top + jnp.log(total)) - dots_ref[...]
    out_refs[2 * tiles][...] = jnp.broadcast_to(jnp.sum(loss), out_refs[2 * tiles].shape)


def combined_grads(turn, tile, powers, tops, totals, tops_far, totals_far, mass, mass_far, dots, mine, other):
    rows = powers.shape[0]
    count = TILES // 2
    stat = pl.BlockSpec((rows, LANES), lambda j, s: (0, 0))
    column = pl.BlockSpec((rows, 1), lambda j, s: (0, 0))
    piece = pl.BlockSpec((rows, tile), lambda j, s: (0, s[0] + 2 * j))
    result = call(
        functools.partial(grad_kernel, count),
        "grad",
        (count,),
        [piece, stat, stat, stat, stat, column, column, column, piece, piece],
        [pl.BlockSpec((rows, tile), lambda j, s: (0, 0))] * count
        + [pl.BlockSpec((1, tile), lambda j, s: (0, 0))] * count
        + [pl.BlockSpec((1, LANES), lambda j, s: (0, 0))],
        [shape(rows, tile, dtype=BF16)] * count + [shape(1, tile)] * count + [shape(1, LANES)],
    )(
        jnp.full((1,), turn, jnp.int32),
        powers, tops, totals, tops_far, totals_far, mass, mass_far, dots, mine, other,
    )
    return result[:count], result[count : 2 * count], result[-1][0, 0]


def back_kernel(vocab, core_ref, weight_ref, normed_ref, *refs):
    grads, (out_ref, total_ref) = refs[:TILES], refs[TILES:]
    step = pl.program_id(0)
    width, tile = weight_ref.shape
    start = (core_ref[0] * TILES + step) * tile
    pieces = lax.broadcasted_iota(jnp.int32, (width, tile), 1) + start
    weight = weight_ref[...]
    weight = jnp.where(pieces < vocab, weight, jnp.zeros_like(weight))

    @pl.when(step == 0)
    def _():
        total_ref[...] = jnp.zeros_like(total_ref)

    for index in range(TILES):

        @pl.when(step == index)
        def _(index=index):
            total_ref[...] += lax.dot_general(
                grads[index][...], weight, (((1,), (1,)), ((), ())), preferred_element_type=F32
            )

    @pl.when(step == TILES - 1)
    def _():
        out_ref[...] = jnp.sum(total_ref[...] * normed_ref[...], axis=0, keepdims=True)


def gain_term(core, vocab, weight, normed, grads):
    rows, width = normed.shape
    tile = grads[0].shape[1]
    last = -(-vocab // tile) - 1
    return call(
        functools.partial(back_kernel, vocab),
        "back",
        (TILES,),
        [
            pl.BlockSpec((width, tile), lambda j, c: (0, jnp.minimum(c[0] * TILES + j, last))),
            pl.BlockSpec((rows, width), lambda j, c: (0, 0)),
        ]
        + [pl.BlockSpec((rows, tile), lambda j, c: (0, 0))] * TILES,
        pl.BlockSpec((1, width), lambda j, c: (0, 0)),
        shape(1, width),
        [pltpu.VMEM((rows, width), F32)],
    )(core, weight, normed, *grads)


def term_kernel(near, bit_ref, *refs):
    states, grads, (kept_ref, sent_ref) = refs[:near], refs[near : 2 * near], refs[2 * near :]
    count = kept_ref.shape[0]

    def product(side):
        rows = pl.ds(pl.multiple_of(side * count, count), count)
        total = None
        for state, grad in zip(states, grads):
            term = jnp.dot(state[rows, :], grad[...], preferred_element_type=F32)
            total = term if total is None else total + term
        return total

    sent_ref[...] = product(1 - bit_ref[0]).astype(BF16)
    kept_ref[...] = product(bit_ref[0])


def weight_term(bit, states, grads):
    count = states[0].shape[0] // 2
    tile = grads[0].shape[1]
    in_specs = [pl.BlockSpec(s.shape, lambda i, b: (0, 0)) for s in (*states, *grads)]
    return call(
        functools.partial(term_kernel, len(states)),
        "term",
        (1,),
        in_specs,
        [pl.BlockSpec((count, tile), lambda i, b: (0, 0))] * 2,
        [shape(count, tile), shape(count, tile, dtype=BF16)],
    )(bit[None], *states, *grads)


def body(
    teacher_logits, routes, agreement, targets, lengths, student_hidden, out_weight, out_bias, gain
):
    cores = lax.axis_size("teach")
    chips = lax.axis_size("dp")
    devices = cores * chips
    rows = teacher_logits.shape[1]
    slots = cores * rows // devices
    vocab = teacher_logits.shape[2]
    width = student_hidden.shape[1]
    out_rows = width // devices
    size_a, size_b, size_c = torus_factors(chips)
    tile = -(-vocab // (TILES * cores * LANES)) * LANES
    half = TILES * tile
    core = lax.axis_index("teach").astype(jnp.int32)
    chip = lax.axis_index("dp").astype(jnp.int32)
    core_only = core[None]
    exchange = [(i, 1 - i) for i in range(cores)]

    def swap(value):
        return lax.ppermute(value, "teach", exchange)

    def bit_of(stride):
        return (chip // stride) % 2

    with jax.named_scope("hidden"):
        arrived = lax.all_to_all(
            student_hidden.reshape(chips, slots, width),
            "dp",
            split_axis=0,
            concat_axis=0,
            tiled=True,
        ).reshape(chips * slots, width)
    arrived_far = swap(arrived)

    dest_device = routes[:, 0]
    slot_index = route_slots(dest_device)
    live_rows = live_mask(lengths, rows)
    with jax.named_scope("teacher"):
        mine, other, mass = soft_targets(
            core_only,
            half,
            teacher_logits[0],
            (0.5 * agreement.astype(F32) * live_rows)[:, None],
            (0.5 * live_rows)[:, None],
            targets[:, None],
        )
    other = swap(other)
    mass_far = swap(mass)

    place = (dest_device % chips) * slots + slot_index
    place = jnp.where(dest_device // chips == core, place, place + chips * slots)
    normed, scaled, turned = select_states(place[:, None], arrived, arrived_far, gain[None, :])

    bits_a, bits_b, bits_c = bits_of(size_a), bits_of(size_b), bits_of(size_c)
    turned = turned.reshape((cores,) + (2,) * bits_c + (size_b, size_a, out_rows, rows))

    def states_for(axis, index):
        taken = lax.dynamic_index_in_dim(turned, index, 1 + bits_c + axis, keepdims=False)
        far_bits = bits_a if axis == 0 else bits_b
        taken = taken.reshape((cores,) + (2,) * (bits_c + far_bits) + (out_rows, rows))
        order = tuple(range(bits_c + far_bits, 0, -1)) + (0,)
        order = order[far_bits * 0 :] + (1 + bits_c + far_bits, 2 + bits_c + far_bits)
        return jnp.transpose(taken, order).reshape(-1, rows)

    def along(value, stride, size, step):
        return lax.ppermute(value, "dp", rotation(chips, stride, size, step))

    deep = [size_a * size_b << k for k in range(bits_c)]
    plans = (
        ((1, 1, size_a), [size_a << k for k in range(bits_b)] + deep),
        ((0, size_a, size_b), [1 << k for k in range(bits_a)] + deep),
    )
    states = []
    for (axis, stride, size), _ in plans:
        at = (chip // stride) % size
        gathered = []
        for step in range(size):
            piece = states_for(axis, (at + step) % size)
            gathered.append(along(piece, stride, size, step) if step else piece)
        states.append(gathered)

    powers, tops, totals, dots = student_forward(
        core_only, vocab, tile, scaled, out_weight, out_bias[None, :], mine, other
    )
    tops_far, totals_far = swap(tops), swap(totals)

    grads, biases, losses = [None] * TILES, [None] * TILES, []
    for turn in range(TILES // 2):
        made, bias, loss = combined_grads(
            turn, tile, powers, tops, totals, tops_far, totals_far, mass, mass_far, dots, mine, other
        )
        grads[turn::2] = made
        biases[turn::2] = bias
        losses.append(loss)

    gathered = {}
    for turn in range(TILES // 2):
        for side, ((axis, stride, size), _) in enumerate(plans):
            grad = grads[turn + 2 * side]
            gathered[turn, side] = [
                along(grad, stride, size, step) if step else grad for step in range(size)
            ]

    first = gathered[0, 0][-1]
    pieces = [None] * TILES
    for turn in range(TILES // 2):
        for side, (_, strides) in enumerate(plans):
            kept, sent = weight_term(bit_of(strides[0]), states[side], gathered[turn, side])
            for place, stride in enumerate(strides):
                if place:
                    halves = kept.reshape(2, kept.shape[0] // 2, tile)
                    bit = bit_of(stride)
                    sent = lax.dynamic_index_in_dim(halves, 1 - bit, 0, keepdims=False)
                    kept = lax.dynamic_index_in_dim(halves, bit, 0, keepdims=False)
                    sent = sent.astype(BF16)
                pairs = [(i, i ^ stride) for i in range(chips)]
                kept = kept + lax.ppermute(sent, "dp", pairs).astype(F32)
            pieces[turn + 2 * side] = kept.reshape(cores, out_rows, tile)

    grads_late, _ = lax.optimization_barrier((tuple(grads), first))
    small = jnp.concatenate(
        [bias[0] for bias in biases]
        + [
            gain_term(core_only, vocab, out_weight, normed, grads_late)[0],
            losses[0][None],
            jnp.sum(live_rows)[None],
        ]
    )
    for stride in deep + [1 << k for k in range(bits_a + bits_b)]:
        small = small + lax.ppermute(small, "dp", [(i, i ^ stride) for i in range(chips)])
    small_far = swap(small)
    inverse = 1.0 / small[half + width + 1]
    bias_low = jnp.where(core == 0, small[:half], small_far[:half])
    bias_high = jnp.where(core == 0, small_far[:half], small[:half])
    bias_sum = jnp.concatenate([bias_low, bias_high])[:vocab]
    rest = small[half:] + small_far[half:]

    whole = jnp.concatenate(pieces, axis=2)
    kept = lax.dynamic_index_in_dim(whole, core, 0, keepdims=False)
    got = swap(lax.dynamic_index_in_dim(whole, 1 - core, 0, keepdims=False))
    low = jnp.where(core == 0, kept, got)
    high = jnp.where(core == 0, got, kept)
    weight_grad = jnp.concatenate([low, high], axis=1)[:, :vocab]
    return (weight_grad * inverse, rest[:width] * inverse, bias_sum * inverse, rest[width] * inverse)


def solution(mesh):
    return jax.shard_map(
        body,
        mesh=mesh,
        in_specs=(
            P("teach", "dp", None),
            P("dp", None),
            P("dp"),
            P("dp"),
            P("dp"),
            P(("teach", "dp"), None),
            P(),
            P(),
            P(),
        ),
        out_specs=(P(("teach", "dp"), None), P(), P(), P()),
        check_vma=False,
    )
```

time: 531 us -> 159 us (0.30)
  waiting for transfers between devices: 393 us -> 31.8 us
  blocking collectives: 49 us -> 0 us
  Pallas kernels: 0 us -> 31.6 us
  starting transfers between devices: 12.7 us -> 39.7 us
  local copies, waits for them, and re-layouts: 15.6 us -> 41 us
  matrix products: 21.3 us -> 0 us
  between operations: 18 us -> 4.36 us
  other arithmetic: 17.9 us -> 9.15 us
    reduce_scatter x1 -> x0, waiting for transfers between devices: 383 us -> none  [body(): lax.psum_scatter(lax.dot_general(state_rows, grad_rows, (((0,), (0,)), ((...]
    psum x1 -> x0, blocking collectives: 49 us -> none  [body(): total_frames = lax.psum(count_term, ('teach', 'dp'))]
    unnamed x16 -> x73, local copies, waits for them, and re-layouts: 1.07 us -> 37.5 us
    pallas_call x0 -> x10, Pallas kernels: none -> 31.6 us  [the longest x4 6.92 us: weight_term(): call(functools.partial(term_kernel, len(states)), 'term', (1,), in_specs,...]
    ppermute x0 -> x29, starting transfers between devices: none -> 31.3 us  [the longest x12 18 us: body(): kept = kept + lax.ppermute(sent, 'dp', pairs).astype(F32)]
    ppermute x0 -> x29, waiting for transfers between devices: none -> 30.5 us  [the longest x4 16.5 us: body(): lax.ppermute(small, 'dp', [(i, i ^ stride) for i in range(chips)])]
    dot_general x4 -> x0, matrix products: 21.3 us -> none  [the longest x1 8.65 us: body(): lax.dot_general(state_rows, grad_rows, (((0,), (0,)), ((), ())), preferre...]
    convert_element_type x2 -> x8, local copies, waits for them, and re-layouts: 9.89 us -> 0.2 us  [body(): sent = sent.astype(BF16)]
  transfers between devices with their start and end apart: 3 -> 30, of which waited for: 2 -> 13; matrix products, arithmetic and copies ran while one was open for 7% -> 19% of each run, Pallas kernels for 0% -> 11%
where the time goes in v2:
time: 159 us; the launch traced here: 158 us
  local copies, waits for them, and re-layouts  41 us (26%)
  starting transfers between devices  39.7 us (25%)
  waiting for transfers between devices  31.8 us (20%)
  Pallas kernels  31.6 us (20%)
  other arithmetic  9.15 us (6%)
  between operations  4.36 us (3%)
    unnamed x73, local copies, waits for them, and re-layouts  37.5 us
    ppermute x12, starting transfers between devices, body(): kept = kept + lax.ppermute(sent, 'dp', pairs).astype(F32)  18 us
    ppermute x4, waiting for transfers between devices, body(): lax.ppermute(small, 'dp', [(i, i ^ stride) for i in range(chips)])  16.5 us
    ppermute x12, waiting for transfers between devices, body(): kept = kept + lax.ppermute(sent, 'dp', pairs).astype(F32)  12.6 us
    all_to_all x1, starting transfers between devices, body(): lax.all_to_all(student_hidden.reshape(chips, slots, width), 'dp', split_a...  8.35 us
    pallas_call x4, Pallas kernels, weight_term(): call(functools.partial(term_kernel, len(states)), 'term', (1,), in_specs,...  6.92 us
    ppermute x6, starting transfers between devices, along(): return lax.ppermute(value, 'dp', rotation(chips, stride, size, step))  6.24 us
    pallas_call x2, Pallas kernels, combined_grads(): call(functools.partial(grad_kernel, count), 'grad', (count,), [piece, sta...  6.07 us
  transfers between devices with their start and end apart: 30, of which 13 were waited for; matrix products, arithmetic and copies ran while one was open for 19% of the time, Pallas kernels for 11%

profile of v2, /device:TPU:0, one launch (start us, length us, event | category | flops | bytes accessed | tf_op | source)
XLA Modules:
  0.0 157.6 jit_solution(2542684051319159786)
XLA Ops:
  0.6 8.4 %all-to-all-start = ((bf16[16,16,1024]{2,1,0:T(8,128)(2,1)}), bf16[16,16,1024]{2,1,0:T(8,128)(2,1)S(1)}, u32[]{:S(2)}, u32[]{:S(2)}) async-start(bf16[16,16,1024]{2,1,0:T(8,128)(2,1)} %bitcast.125), calls=%async_computation | async-start | bytes 1048576 | tf_op jit(solution)/shard_map/hidden/all_to_all | solution.py:355
  10.5 4.4 %copy.54 = bf16[1,256,5000]{2,1,0:T(8,128)(2,1)} copy(bf16[1,256,5000]{1,2,0:T(8,128)(2,1)} %param.9) | data formatting | bytes 5120000 | tf_op args[0]
  15.1 1.7 %copy-done.1 = bf16[1,256,5000]{2,1,0:T(8,128)(2,1)S(1)} copy-done((bf16[1,256,5000]{2,1,0:T(8,128)(2,1)S(1)}, bf16[1,256,5000]{2,1,0:T(8,128)(2,1)}, u32[]{:S(2)}) %copy-start.1) | copy-done | bytes 2560024
  16.8 5.8 %soft.1 = (bf16[256,2560]{1,0:T(8,128)(2,1)S(1)}, bf16[256,2560]{1,0:T(8,128)(2,1)}, f32[256,1]{1,0:T(8,128)S(1)}) custom-call(s32[1]{0:T(128)} %bitcast.13.core_ref, bf16[256,5000]{1,0:T(8,128)(2,1)S(1)} %bitcast.92, f32[256,1]{1,0:T(8,128)S(1)} %copy.55.weight_ref, f32[256,1]{1,0:T(8,128)S(1)} %fusion.17.hot_ref, s32[256,1]{1,0:T(8,128)S(1)} %copy.56.target_ref), custom_call_target="tpu_custom_call" | custom-call | tf_op jit(solution)/shard_map/teacher/soft/pallas_call | solution.py:105
  22.8 1.3 all-to-all-done
  25.3 13.9 %copy.57.weight_ref = bf16[1024,5000]{1,0:T(8,128)(2,1)} copy(bf16[1024,5000]{0,1:T(8,128)(2,1)} %param.15) | data formatting | bytes 20480000 | tf_op args[6]
  39.1 1.1 add_select_fusion.2.place_ref
  40.2 1.0 copy-done.3
  41.3 1.9 %select.70 = (f32[256,1024]{1,0:T(8,128)S(1)}, bf16[256,1024]{1,0:T(8,128)(2,1)S(1)}, bf16[1024,256]{1,0:T(8,128)(2,1)S(1)}) custom-call(s32[256,1]{1,0:T(8,128)S(1)} %add_select_fusion.2.place_ref, bf16[256,1024]{1,0:T(8,128)(2,1)S(1)} %bitcast.100, bf16[256,1024]{1,0:T(8,128)(2,1)} %collective-permute-done.far_ref, f32[1,1024]{1,0:T(1,128)S(1)} %bitcast.103), custom_call_target="tpu_custom_call" | custom-call | tf_op jit(solution)/shard_map/select/pallas_call | solution.py:138
  44.2 5.8 %forward.1 = (f32[256,2560]{1,0:T(8,128)S(1)}, f32[256,128]{1,0:T(8,128)S(1)}, f32[256,128]{1,0:T(8,128)S(1)}, f32[256,1]{1,0:T(8,128)S(1)}) custom-call(s32[1]{0:T(128)} %bitcast.13.core_ref, bf16[256,1024]{1,0:T(8,128)(2,1)S(1)} %get-tuple-element.36.scaled_ref, bf16[1024,5000]{1,0:T(8,128)(2,1)} %copy.57.weight_ref, f32[1,5000]{1,0:T(1,128)S(1)} %bitcast.101, ...), custom_call_target="tpu_custom_call" | custom-call | tf_op jit(solution)/shard_map/forward/pallas_call | solution.py:187
  49.9 1.6 %copy-done = f32[256,2560]{1,0:T(8,128)} copy-done((f32[256,2560]{1,0:T(8,128)}, f32[256,2560]{1,0:T(8,128)S(1)}, u32[]{:S(2)}) %copy-start) | copy-done | bytes 2621464
  52.6 1.0 collective-permute-done.5.mass_far_ref
  53.6 1.0 copy-done.15
  54.6 3.1 %grad.2 = (bf16[256,640]{1,0:T(8,128)(2,1)}, bf16[256,640]{1,0:T(8,128)(2,1)S(1)}, f32[1,640]{1,0:T(1,128)S(1)}, f32[1,640]{1,0:T(1,128)S(1)}, f32[1,128]{1,0:T(1,128)S(1)}) custom-call(s32[1]{0:T(128)} %constant.248.clone.1.step_ref, f32[256,2560]{1,0:T(8,128)} %copy-done, f32[256,128]{1,0:T(8,128)S(1)} %get-tuple-element.40.tops_ref, ...), custom_call_target="tpu_custom_call" | custom-call | tf_op jit(solution)/shard_map/grad/pallas_call | solution.py:238
  57.8 1.1 collective-permute-start.6
  65.8 3.0 %grad.3 = (bf16[256,640]{1,0:T(8,128)(2,1)S(1)}, bf16[256,640]{1,0:T(8,128)(2,1)S(1)}, f32[1,640]{1,0:T(1,128)S(1)}, f32[1,640]{1,0:T(1,128)S(1)}, f32[1,128]{1,0:T(1,128)}) custom-call(s32[1]{0:T(128)} %constant.255.clone.1.step_ref, f32[256,2560]{1,0:T(8,128)} %copy-done, f32[256,128]{1,0:T(8,128)S(1)} %copy-done.18, f32[256,128]{1,0:T(8,128)S(1)} %copy-done.20, ...), custom_call_target="tpu_custom_call" | custom-call | tf_op jit(solution)/shard_map/grad/pallas_call | solution.py:238
  72.3 1.2 copy-done.11
  73.5 5.2 %back.1 = f32[1,1024]{1,0:T(1,128)S(1)} custom-call(s32[1]{0:T(128)} %bitcast.13.core_ref, bf16[1024,5000]{1,0:T(8,128)(2,1)} %copy.57.weight_ref, f32[256,1024]{1,0:T(8,128)S(1)} %copy-done.11, bf16[256,640]{1,0:T(8,128)(2,1)} %get-tuple-element.61.refs_2_.refs_0_, bf16[256,640]{1,0:T(8,128)(2,1)S(1)} %copy-done.8, ...), custom_call_target="tpu_custom_call" | custom-call | tf_op jit(solution)/shard_map/back/pallas_call | solution.py:284
  79.4 1.5 collective-permute-start.24
  80.9 2.3 %collective-permute-done.24 = f32[3586]{0:T(1024)S(1)} collective-permute-done((f32[3586]{0:T(1024)S(1)}, f32[3586]{0:T(1024)S(1)}, u32[]{:S(2)}, u32[]{:S(2)}) %collective-permute-start.24) | collective-permute-done | bytes 14376 | tf_op jit(solution)/shard_map/ppermute | solution.py:459
  83.2 2.4 %collective-permute-start.25 = (f32[3586]{0:T(1024)S(1)}, f32[3586]{0:T(1024)S(1)}, u32[]{:S(2)}, u32[]{:S(2)}) collective-permute-start(f32[3586]{0:T(1024)S(1)} %add.227), channel_id=1, source_target_pairs={{0,8},{1,9},{2,10},{3,11},{4,12},{5,13},{6,14},{7,15},{8,0},{9,1},... | collective-permute-start | bytes 43040 | tf_op jit(solution)/shard_map/ppermute | solution.py:459
  85.5 2.3 %collective-permute-done.25 = f32[3586]{0:T(1024)S(1)} collective-permute-done((f32[3586]{0:T(1024)S(1)}, f32[3586]{0:T(1024)S(1)}, u32[]{:S(2)}, u32[]{:S(2)}) %collective-permute-start.25) | collective-permute-done | bytes 14376 | tf_op jit(solution)/shard_map/ppermute | solution.py:459
  88.9 1.1 collective-permute-start.1
  91.0 1.0 collective-permute-start.15
  93.0 1.1 collective-permute-start.27
  94.2 11.9 %collective-permute-done.27 = f32[3586]{0:T(1024)S(1)} collective-permute-done((f32[3586]{0:T(1024)S(1)}, f32[3586]{0:T(1024)S(1)}, u32[]{:S(2)}, u32[]{:S(2)}) %collective-permute-start.27) | collective-permute-done | bytes 14376 | tf_op jit(solution)/shard_map/ppermute | solution.py:459
  106.1 1.0 collective-permute-start.14
  107.3 2.2 %term.4 = (f32[256,640]{1,0:T(8,128)S(1)}, bf16[256,640]{1,0:T(8,128)(2,1)}) custom-call(s32[1]{0:T(128)} %bitcast.bit_ref, bf16[512,256]{1,0:T(8,128)(2,1)S(1)} %bitcast.95, bf16[512,256]{1,0:T(8,128)(2,1)S(1)} %collective-permute-done.1.refs_1_, bf16[256,640]{1,0:T(8,128)(2,1)} %get-tuple-element.61.refs_2_.refs_0_, ...), custom_call_target="tpu_custom_call" | custom-call | tf_op jit(solution)/shard_map/term/pallas_call | solution.py:319
  112.2 1.1 term.5
  113.4 1.0 collective-permute-start.11
  114.4 2.1 %term.6 = (f32[256,640]{1,0:T(8,128)S(1)}, bf16[256,640]{1,0:T(8,128)(2,1)}) custom-call(s32[1]{0:T(128)} %bitcast.35.bit_ref, bf16[512,256]{1,0:T(8,128)(2,1)S(1)} %bitcast.93, bf16[512,256]{1,0:T(8,128)(2,1)S(1)} %collective-permute-done.14.refs_1_, bf16[256,640]{1,0:T(8,128)(2,1)S(1)} %get-tuple-element.63.refs_2_, ...), custom_call_target="tpu_custom_call" | custom-call | tf_op jit(solution)/shard_map/term/pallas_call | solution.py:319
  116.5 1.5 collective-permute-start.16
  117.9 1.5 term.7
  122.6 1.0 convert_add_fusion.3
  123.7 1.5 collective-permute-start.8
  125.2 2.4 %collective-permute-done.11 = bf16[256,640]{1,0:T(8,128)(2,1)} collective-permute-done((bf16[256,640]{1,0:T(8,128)(2,1)}, bf16[256,640]{1,0:T(8,128)(2,1)}, u32[]{:S(2)}, u32[]{:S(2)}) %collective-permute-start.11) | collective-permute-done | bytes 327712 | tf_op jit(solution)/shard_map/ppermute | solution.py:446
  127.6 1.0 convert_add_fusion.2
  128.7 1.5 collective-permute-start.12
  130.2 1.0 convert_add_fusion.1
  131.9 1.3 collective-permute-done.20
  133.3 1.0 convert_add_fusion
  134.3 1.5 collective-permute-start.21
  135.9 2.6 %collective-permute-start.9 = (bf16[64,640]{1,0:T(8,128)(2,1)S(1)}, bf16[64,640]{1,0:T(8,128)(2,1)S(1)}, u32[]{:S(2)}, u32[]{:S(2)}) collective-permute-start(bf16[64,640]{1,0:T(8,128)(2,1)S(1)} %fusion.19), channel_id=1, source_target_pairs={{0,8},{1,9},{2,10},{3,11},{4,12},{5,13},{6,14},{7,15},{8,0},{9,1},... | collective-permute-start | bytes 245768 | tf_op jit(solution)/shard_map/ppermute | solution.py:446
  140.0 4.2 %collective-permute-start.18 = (bf16[64,640]{1,0:T(8,128)(2,1)S(1)}, bf16[64,640]{1,0:T(8,128)(2,1)S(1)}, u32[]{:S(2)}, u32[]{:S(2)}) collective-permute-start(bf16[64,640]{1,0:T(8,128)(2,1)S(1)} %fusion.21), channel_id=1, source_target_pairs={{0,8},{1,9},{2,10},{3,11},{4,12},{5,13},{6,14},{7,15},{8,0},{9,1},... | collective-permute-start | bytes 245768 | tf_op jit(solution)/shard_map/ppermute | solution.py:446
  144.3 1.0 collective-permute-done.21
  145.3 1.4 collective-permute-start.22
  146.8 3.8 %collective-permute-done.13 = bf16[64,640]{1,0:T(8,128)(2,1)S(1)} collective-permute-done((bf16[64,640]{1,0:T(8,128)(2,1)S(1)}, bf16[64,640]{1,0:T(8,128)(2,1)S(1)}, u32[]{:S(2)}, u32[]{:S(2)}) %collective-permute-start.13) | collective-permute-done | bytes 81952 | tf_op jit(solution)/shard_map/ppermute | solution.py:446
  150.6 2.2 %collective-permute-done.18 = bf16[64,640]{1,0:T(8,128)(2,1)S(1)} collective-permute-done((bf16[64,640]{1,0:T(8,128)(2,1)S(1)}, bf16[64,640]{1,0:T(8,128)(2,1)S(1)}, u32[]{:S(2)}, u32[]{:S(2)}) %collective-permute-start.18) | collective-permute-done | bytes 81952 | tf_op jit(solution)/shard_map/ppermute | solution.py:446
  (150 shorter events, 29.1 us)
Async XLA Ops:
  0.6 23.4 %all-to-all-start = ((bf16[16,16,1024]{2,1,0:T(8,128)(2,1)}), bf16[16,16,1024]{2,1,0:T(8,128)(2,1)S(1)}, u32[]{:S(2)}, u32[]{:S(2)}) async-start(bf16[16,16,1024]{2,1,0:T(8,128)(2,1)} %bitcast.125), calls=%async_computation | async-start | bytes 1048576 | tf_op jit(solution)/shard_map/hidden/all_to_all | solution.py:355
  10.5 4.5 %copy-start.34 = (s32[256]{0:T(256)S(1)}, s32[256]{0:T(256)}, u32[]{:S(2)}) copy-start(s32[256]{0:T(256)} %param.12) | copy-start | bytes 3076
  14.9 7.7 %copy-start.33 = (s32[256,1]{0,1:T(1,128)S(1)}, s32[256,1]{0,1:T(1,128)}, u32[]{:S(2)}) copy-start(s32[256,1]{0,1:T(1,128)} %param.10) | copy-start | bytes 3076
  15.1 1.7 %copy-start.1 = (bf16[1,256,5000]{2,1,0:T(8,128)(2,1)S(1)}, bf16[1,256,5000]{2,1,0:T(8,128)(2,1)}, u32[]{:S(2)}) copy-start(bf16[1,256,5000]{2,1,0:T(8,128)(2,1)} %copy.54) | copy-start | bytes 7680004
  22.6 29.5 %copy-start.14 = (f32[256,1]{1,0:T(8,128)}, f32[256,1]{1,0:T(8,128)S(1)}, u32[]{:S(2)}) copy-start(f32[256,1]{1,0:T(8,128)S(1)} %get-tuple-element.42.mass_ref) | copy-start | bytes 3076
  22.6 21.5 %collective-permute-start.2 = (bf16[256,2560]{1,0:T(8,128)(2,1)}, bf16[256,2560]{1,0:T(8,128)(2,1)S(1)}, u32[]{:S(2)}, u32[]{:S(2)}) collective-permute-start(bf16[256,2560]{1,0:T(8,128)(2,1)} %get-tuple-element.38), channel_id=1, source_target_pairs={{0,16},{16,0},{1,17},{17,1},{2,18},{18,2},{3,19},{19,3},{4,20},{20... | collective-permute-start | bytes 3932168 | tf_op jit(solution)/shard_map/ppermute | solution.py:349
  24.1 15.1 %copy-start.2 = (bf16[16,16,1024]{2,1,0:T(8,128)(2,1)}, bf16[16,16,1024]{2,1,0:T(8,128)(2,1)S(1)}, u32[]{:S(2)}) copy-start(bf16[16,16,1024]{2,1,0:T(8,128)(2,1)S(1)} %all-to-all-done) | copy-start | bytes 1572868
  24.1 16.1 %collective-permute-start = (bf16[256,1024]{1,0:T(8,128)(2,1)S(1)}, bf16[256,1024]{1,0:T(8,128)(2,1)}, u32[]{:S(2)}, u32[]{:S(2)}) collective-permute-start(bf16[256,1024]{1,0:T(8,128)(2,1)S(1)} %bitcast.99), channel_id=1, source_target_pairs={{0,16},{16,0},{1,17},{17,1},{2,18},{18,2},{3,19},{19,3},{4,20},{20... | collective-permute-start | bytes 1572872 | tf_op jit(solution)/shard_map/ppermute | solution.py:349
  25.3 15.0 %copy-start.32 = (f32[1024]{0:T(1024)S(1)}, f32[1024]{0:T(1024)}, u32[]{:S(2)}) copy-start(f32[1024]{0:T(1024)} %param.17) | copy-start | bytes 12292
  25.3 18.9 %copy-start.31 = (f32[5000]{0:T(1024)S(1)}, f32[5000]{0:T(1024)}, u32[]{:S(2)}) copy-start(f32[5000]{0:T(1024)} %param.16) | copy-start | bytes 60004
  49.9 1.6 %copy-start = (f32[256,2560]{1,0:T(8,128)}, f32[256,2560]{1,0:T(8,128)S(1)}, u32[]{:S(2)}) copy-start(f32[256,2560]{1,0:T(8,128)S(1)} %get-tuple-element.39.powers_ref) | copy-start | bytes 7864324
  51.5 6.2 %copy-start.17 = (f32[256,128]{1,0:T(8,128)}, f32[256,128]{1,0:T(8,128)S(1)}, u32[]{:S(2)}) copy-start(f32[256,128]{1,0:T(8,128)S(1)} %get-tuple-element.40.tops_ref) | copy-start | bytes 393220
  51.5 6.2 %copy-start.19 = (f32[256,128]{1,0:T(8,128)}, f32[256,128]{1,0:T(8,128)S(1)}, u32[]{:S(2)}) copy-start(f32[256,128]{1,0:T(8,128)S(1)} %get-tuple-element.41.totals_ref) | copy-start | bytes 393220
  51.5 6.2 %copy-start.21 = (f32[256,1]{1,0:T(8,128)}, f32[256,1]{1,0:T(8,128)S(1)}, u32[]{:S(2)}) copy-start(f32[256,1]{1,0:T(8,128)S(1)} %get-tuple-element.43.dots_ref) | copy-start | bytes 3076
  51.5 2.1 %collective-permute-start.3 = (f32[256,128]{1,0:T(8,128)S(1)}, f32[256,128]{1,0:T(8,128)S(1)}, u32[]{:S(2)}, u32[]{:S(2)}) collective-permute-start(f32[256,128]{1,0:T(8,128)S(1)} %get-tuple-element.40.tops_ref), channel_id=1, source_target_pairs={{0,16},{16,0},{1,17},{17,1},{2,18},{18,2},{3,19},{19,3},{4,20},{20... | collective-permute-start | bytes 393224 | tf_op jit(solution)/shard_map/ppermute | solution.py:349
  52.0 1.5 collective-permute-start.4
  52.1 1.5 collective-permute-start.5
  53.6 4.1 %copy-start.27 = (f32[256,1]{1,0:T(8,128)}, f32[256,1]{1,0:T(8,128)S(1)}, u32[]{:S(2)}) copy-start(f32[256,1]{1,0:T(8,128)S(1)} %collective-permute-done.5.mass_far_ref) | copy-start | bytes 3076
  53.6 4.2 %copy-start.23 = (f32[256,128]{1,0:T(8,128)}, f32[256,128]{1,0:T(8,128)S(1)}, u32[]{:S(2)}) copy-start(f32[256,128]{1,0:T(8,128)S(1)} %collective-permute-done.3.tops_far_ref) | copy-start | bytes 393220
  53.6 4.2 %copy-start.25 = (f32[256,128]{1,0:T(8,128)}, f32[256,128]{1,0:T(8,128)S(1)}, u32[]{:S(2)}) copy-start(f32[256,128]{1,0:T(8,128)S(1)} %collective-permute-done.4.totals_far_ref) | copy-start | bytes 393220
  57.8 12.6 %collective-permute-start.6 = (bf16[256,640]{1,0:T(8,128)(2,1)}, bf16[256,640]{1,0:T(8,128)(2,1)}, u32[]{:S(2)}, u32[]{:S(2)}) collective-permute-start(bf16[256,640]{1,0:T(8,128)(2,1)} %get-tuple-element.61.refs_2_.refs_0_), channel_id=1, source_target_pairs={{0,1},{1,0},{2,3},{3,2},{4,5},{5,4},{6,7},{7,6},{8,9},{9,8},{10,11... | collective-permute-start | bytes 983048 | tf_op jit(solution)/shard_map/ppermute | solution.py:395
  73.5 16.5 %copy-start.9 = (bf16[256,640]{1,0:T(8,128)(2,1)S(1)}, bf16[256,640]{1,0:T(8,128)(2,1)}, u32[]{:S(2)}) copy-start(bf16[256,640]{1,0:T(8,128)(2,1)} %copy-done.7) | copy-start | bytes 983044
  73.5 18.5 %copy-start.6 = (bf16[256,640]{1,0:T(8,128)(2,1)S(1)}, bf16[256,640]{1,0:T(8,128)(2,1)}, u32[]{:S(2)}) copy-start(bf16[256,640]{1,0:T(8,128)(2,1)} %copy-done.4) | copy-start | bytes 983044
  79.4 3.7 %collective-permute-start.24 = (f32[3586]{0:T(1024)S(1)}, f32[3586]{0:T(1024)S(1)}, u32[]{:S(2)}, u32[]{:S(2)}) collective-permute-start(f32[3586]{0:T(1024)S(1)} %concatenate.14), channel_id=1, source_target_pairs={{0,4},{1,5},{2,6},{3,7},{4,0},{5,1},{6,2},{7,3},{8,12},{9,13},{10,... | collective-permute-start | bytes 43040 | tf_op jit(solution)/shard_map/ppermute | solution.py:459
  83.2 4.6 %collective-permute-start.25 = (f32[3586]{0:T(1024)S(1)}, f32[3586]{0:T(1024)S(1)}, u32[]{:S(2)}, u32[]{:S(2)}) collective-permute-start(f32[3586]{0:T(1024)S(1)} %add.227), channel_id=1, source_target_pairs={{0,8},{1,9},{2,10},{3,11},{4,12},{5,13},{6,14},{7,15},{8,0},{9,1},... | collective-permute-start | bytes 43040 | tf_op jit(solution)/shard_map/ppermute | solution.py:459
  87.8 5.2 %collective-permute-start.26 = (f32[3586]{0:T(1024)S(1)}, f32[3586]{0:T(1024)S(1)}, u32[]{:S(2)}, u32[]{:S(2)}) collective-permute-start(f32[3586]{0:T(1024)S(1)} %add.228), channel_id=1, source_target_pairs={{0,1},{1,0},{2,3},{3,2},{4,5},{5,4},{6,7},{7,6},{8,9},{9,8},{10,11... | collective-permute-start | bytes 43040 | tf_op jit(solution)/shard_map/ppermute | solution.py:459
  88.9 18.3 %collective-permute-start.1 = (bf16[512,256]{1,0:T(8,128)(2,1)S(1)}, bf16[512,256]{1,0:T(8,128)(2,1)S(1)}, u32[]{:S(2)}, u32[]{:S(2)}) collective-permute-start(bf16[512,256]{1,0:T(8,128)(2,1)S(1)} %bitcast.127), channel_id=1, source_target_pairs={{0,1},{1,0},{2,3},{3,2},{4,5},{5,4},{6,7},{7,6},{8,9},{9,8},{10,11... | collective-permute-start | bytes 786440 | tf_op jit(solution)/shard_map/ppermute | solution.py:395
  90.0 19.6 %collective-permute-start.10 = (bf16[256,640]{1,0:T(8,128)(2,1)S(1)}, bf16[256,640]{1,0:T(8,128)(2,1)S(1)}, u32[]{:S(2)}, u32[]{:S(2)}) collective-permute-start(bf16[256,640]{1,0:T(8,128)(2,1)S(1)} %copy-done.9), channel_id=1, source_target_pairs={{0,1},{1,0},{2,3},{3,2},{4,5},{5,4},{6,7},{7,6},{8,9},{9,8},{10,11... | collective-permute-start | bytes 983048 | tf_op jit(solution)/shard_map/ppermute | solution.py:395
  91.0 23.4 %collective-permute-start.15 = (bf16[256,640]{1,0:T(8,128)(2,1)S(1)}, bf16[256,640]{1,0:T(8,128)(2,1)}, u32[]{:S(2)}, u32[]{:S(2)}) collective-permute-start(bf16[256,640]{1,0:T(8,128)(2,1)S(1)} %get-tuple-element.63.refs_2_), channel_id=1, source_target_pairs={{0,2},{1,3},{2,0},{3,1},{4,6},{5,7},{6,4},{7,5},{8,10},{9,11},{10,... | collective-permute-start | bytes 983048 | tf_op jit(solution)/shard_map/ppermute | solution.py:395
  92.0 25.9 %collective-permute-start.19 = (bf16[256,640]{1,0:T(8,128)(2,1)S(1)}, bf16[256,640]{1,0:T(8,128)(2,1)}, u32[]{:S(2)}, u32[]{:S(2)}) collective-permute-start(bf16[256,640]{1,0:T(8,128)(2,1)S(1)} %copy-done.6), channel_id=1, source_target_pairs={{0,2},{1,3},{2,0},{3,1},{4,6},{5,7},{6,4},{7,5},{8,10},{9,11},{10,... | collective-permute-start | bytes 983048 | tf_op jit(solution)/shard_map/ppermute | solution.py:395
  93.0 13.1 %collective-permute-start.27 = (f32[3586]{0:T(1024)S(1)}, f32[3586]{0:T(1024)S(1)}, u32[]{:S(2)}, u32[]{:S(2)}) collective-permute-start(f32[3586]{0:T(1024)S(1)} %add.229), channel_id=1, source_target_pairs={{0,2},{1,3},{2,0},{3,1},{4,6},{5,7},{6,4},{7,5},{8,10},{9,11},{10,... | collective-permute-start | bytes 43040 | tf_op jit(solution)/shard_map/ppermute | solution.py:459
  106.1 7.3 %collective-permute-start.14 = (bf16[512,256]{1,0:T(8,128)(2,1)S(1)}, bf16[512,256]{1,0:T(8,128)(2,1)S(1)}, u32[]{:S(2)}, u32[]{:S(2)}) collective-permute-start(bf16[512,256]{1,0:T(8,128)(2,1)S(1)} %bitcast.126), channel_id=1, source_target_pairs={{0,2},{1,3},{2,0},{3,1},{4,6},{5,7},{6,4},{7,5},{8,10},{9,11},{10,... | collective-permute-start | bytes 786440 | tf_op jit(solution)/shard_map/ppermute | solution.py:395
  107.1 14.3 %collective-permute-start.28 = (f32[3586]{0:T(1024)S(1)}, f32[3586]{0:T(1024)S(1)}, u32[]{:S(2)}, u32[]{:S(2)}) collective-permute-start(f32[3586]{0:T(1024)S(1)} %add.230), channel_id=1, source_target_pairs={{0,16},{16,0},{1,17},{17,1},{2,18},{18,2},{3,19},{19,3},{4,20},{20... | collective-permute-start | bytes 43040 | tf_op jit(solution)/shard_map/ppermute | solution.py:349
  110.3 12.3 %collective-permute-start.7 = (bf16[256,640]{1,0:T(8,128)(2,1)}, bf16[256,640]{1,0:T(8,128)(2,1)}, u32[]{:S(2)}, u32[]{:S(2)}) collective-permute-start(bf16[256,640]{1,0:T(8,128)(2,1)} %get-tuple-element.46), channel_id=1, source_target_pairs={{0,2},{1,3},{2,0},{3,1},{4,6},{5,7},{6,4},{7,5},{8,10},{9,11},{10,... | collective-permute-start | bytes 983048 | tf_op jit(solution)/shard_map/ppermute | solution.py:446
  113.4 14.3 %collective-permute-start.11 = (bf16[256,640]{1,0:T(8,128)(2,1)}, bf16[256,640]{1,0:T(8,128)(2,1)}, u32[]{:S(2)}, u32[]{:S(2)}) collective-permute-start(bf16[256,640]{1,0:T(8,128)(2,1)} %get-tuple-element.49), channel_id=1, source_target_pairs={{0,2},{1,3},{2,0},{3,1},{4,6},{5,7},{6,4},{7,5},{8,10},{9,11},{10,... | collective-permute-start | bytes 983048 | tf_op jit(solution)/shard_map/ppermute | solution.py:446
  116.4 3.0 %copy-start.12 = (f32[256,640]{1,0:T(8,128)}, f32[256,640]{1,0:T(8,128)S(1)}, u32[]{:S(2)}) copy-start(f32[256,640]{1,0:T(8,128)S(1)} %get-tuple-element.51) | copy-start | bytes 1966084
  116.5 13.8 %collective-permute-start.16 = (bf16[256,640]{1,0:T(8,128)(2,1)}, bf16[256,640]{1,0:T(8,128)(2,1)}, u32[]{:S(2)}, u32[]{:S(2)}) collective-permute-start(bf16[256,640]{1,0:T(8,128)(2,1)} %get-tuple-element.52), channel_id=1, source_target_pairs={{0,1},{1,0},{2,3},{3,2},{4,5},{5,4},{6,7},{7,6},{8,9},{9,8},{10,11... | collective-permute-start | bytes 983048 | tf_op jit(solution)/shard_map/ppermute | solution.py:446
  119.5 10.8 %copy-start.13 = (f32[256,640]{1,0:T(8,128)S(1)}, f32[256,640]{1,0:T(8,128)}, u32[]{:S(2)}) copy-start(f32[256,640]{1,0:T(8,128)} %copy-done.12) | copy-start | bytes 1966084
  119.5 13.8 %collective-permute-start.20 = (bf16[256,640]{1,0:T(8,128)(2,1)S(1)}, bf16[256,640]{1,0:T(8,128)(2,1)}, u32[]{:S(2)}, u32[]{:S(2)}) collective-permute-start(bf16[256,640]{1,0:T(8,128)(2,1)S(1)} %get-tuple-element.55), channel_id=1, source_target_pairs={{0,1},{1,0},{2,3},{3,2},{4,5},{5,4},{6,7},{7,6},{8,9},{9,8},{10,11... | collective-permute-start | bytes 983048 | tf_op jit(solution)/shard_map/ppermute | solution.py:446
  123.7 12.2 %collective-permute-start.8 = (bf16[128,640]{1,0:T(8,128)(2,1)S(1)}, bf16[128,640]{1,0:T(8,128)(2,1)S(1)}, u32[]{:S(2)}, u32[]{:S(2)}) collective-permute-start(bf16[128,640]{1,0:T(8,128)(2,1)S(1)} %fusion.2), channel_id=1, source_target_pairs={{0,4},{1,5},{2,6},{3,7},{4,0},{5,1},{6,2},{7,3},{8,12},{9,13},{10,... | collective-permute-start | bytes 491528 | tf_op jit(solution)/shard_map/ppermute | solution.py:446
  128.7 9.8 %collective-permute-start.12 = (bf16[128,640]{1,0:T(8,128)(2,1)S(1)}, bf16[128,640]{1,0:T(8,128)(2,1)S(1)}, u32[]{:S(2)}, u32[]{:S(2)}) collective-permute-start(bf16[128,640]{1,0:T(8,128)(2,1)S(1)} %fusion.3), channel_id=1, source_target_pairs={{0,4},{1,5},{2,6},{3,7},{4,0},{5,1},{6,2},{7,3},{8,12},{9,13},{10,... | collective-permute-start | bytes 491528 | tf_op jit(solution)/shard_map/ppermute | solution.py:446
  131.3 8.7 %collective-permute-start.17 = (bf16[128,640]{1,0:T(8,128)(2,1)S(1)}, bf16[128,640]{1,0:T(8,128)(2,1)S(1)}, u32[]{:S(2)}, u32[]{:S(2)}) collective-permute-start(bf16[128,640]{1,0:T(8,128)(2,1)S(1)} %fusion.4), channel_id=1, source_target_pairs={{0,4},{1,5},{2,6},{3,7},{4,0},{5,1},{6,2},{7,3},{8,12},{9,13},{10,... | collective-permute-start | bytes 491528 | tf_op jit(solution)/shard_map/ppermute | solution.py:446
  134.3 10.9 %collective-permute-start.21 = (bf16[128,640]{1,0:T(8,128)(2,1)S(1)}, bf16[128,640]{1,0:T(8,128)(2,1)S(1)}, u32[]{:S(2)}, u32[]{:S(2)}) collective-permute-start(bf16[128,640]{1,0:T(8,128)(2,1)S(1)} %fusion.5), channel_id=1, source_target_pairs={{0,4},{1,5},{2,6},{3,7},{4,0},{5,1},{6,2},{7,3},{8,12},{9,13},{10,... | collective-permute-start | bytes 491528 | tf_op jit(solution)/shard_map/ppermute | solution.py:446
  135.9 10.8 %collective-permute-start.9 = (bf16[64,640]{1,0:T(8,128)(2,1)S(1)}, bf16[64,640]{1,0:T(8,128)(2,1)S(1)}, u32[]{:S(2)}, u32[]{:S(2)}) collective-permute-start(bf16[64,640]{1,0:T(8,128)(2,1)S(1)} %fusion.19), channel_id=1, source_target_pairs={{0,8},{1,9},{2,10},{3,11},{4,12},{5,13},{6,14},{7,15},{8,0},{9,1},... | collective-permute-start | bytes 245768 | tf_op jit(solution)/shard_map/ppermute | solution.py:446
  138.6 12.0 %collective-permute-start.13 = (bf16[64,640]{1,0:T(8,128)(2,1)S(1)}, bf16[64,640]{1,0:T(8,128)(2,1)S(1)}, u32[]{:S(2)}, u32[]{:S(2)}) collective-permute-start(bf16[64,640]{1,0:T(8,128)(2,1)S(1)} %fusion.20), channel_id=1, source_target_pairs={{0,8},{1,9},{2,10},{3,11},{4,12},{5,13},{6,14},{7,15},{8,0},{9,1},... | collective-permute-start | bytes 245768 | tf_op jit(solution)/shard_map/ppermute | solution.py:446
  140.0 12.7 %collective-permute-start.18 = (bf16[64,640]{1,0:T(8,128)(2,1)S(1)}, bf16[64,640]{1,0:T(8,128)(2,1)S(1)}, u32[]{:S(2)}, u32[]{:S(2)}) collective-permute-start(bf16[64,640]{1,0:T(8,128)(2,1)S(1)} %fusion.21), channel_id=1, source_target_pairs={{0,8},{1,9},{2,10},{3,11},{4,12},{5,13},{6,14},{7,15},{8,0},{9,1},... | collective-permute-start | bytes 245768 | tf_op jit(solution)/shard_map/ppermute | solution.py:446
  145.3 8.3 %collective-permute-start.22 = (bf16[64,640]{1,0:T(8,128)(2,1)S(1)}, bf16[64,640]{1,0:T(8,128)(2,1)S(1)}, u32[]{:S(2)}, u32[]{:S(2)}) collective-permute-start(bf16[64,640]{1,0:T(8,128)(2,1)S(1)} %fusion.22), channel_id=1, source_target_pairs={{0,8},{1,9},{2,10},{3,11},{4,12},{5,13},{6,14},{7,15},{8,0},{9,1},... | collective-permute-start | bytes 245768 | tf_op jit(solution)/shard_map/ppermute | solution.py:446
  153.8 1.7 %collective-permute-start.23 = (f32[32,2560]{1,0:T(8,128)S(1)}, f32[32,2560]{1,0:T(8,128)S(1)}, u32[]{:S(2)}, u32[]{:S(2)}) collective-permute-start(f32[32,2560]{1,0:T(8,128)S(1)} %dynamic-slice_bitcast_fusion), channel_id=1, source_target_pairs={{0,16},{16,0},{1,17},{17,1},{2,18},{18,2},{3,19},{19,3},{4,20},{20... | collective-permute-start | bytes 983048 | tf_op jit(solution)/shard_map/ppermute | solution.py:349
  (17 other events, 15.7 us)

commit v3 on v0

v3 whole, which is shorter than its diff:
```python
import functools
import math

import jax
import jax.numpy as jnp
from jax import lax
from jax.experimental import pallas as pl
from jax.experimental.pallas import tpu as pltpu
from jax.sharding import PartitionSpec as P


LMAX = 256
EPSILON = 1e-05
LANES = 128
TURNS = 2
TILES = 2 * TURNS
F32 = jnp.float32
BF16 = jnp.bfloat16
CONTRACT_LAST = (((1,), (1,)), ((), ()))
CONTRACT_FIRST = (((0,), (0,)), ((), ()))


def bits_of(count):
    return count.bit_length() - 1


def torus_factors(count):
    bits = bits_of(count)
    small = bits // 3
    middle = (bits - small) // 2
    return 1 << small, 1 << middle, 1 << (bits - small - middle)


def rotation(count, stride, size, step):
    def moved(index):
        place = (index // stride) % size
        return index + ((place + step) % size - place) * stride

    return [(index, moved(index)) for index in range(count)]


def flips(strides):
    masks = [0]
    for stride in strides:
        masks += [mask | stride for mask in masks]
    return masks[1:]


def route_slots(dest_device):
    row_ids = jnp.arange(dest_device.shape[0], dtype=jnp.int32)
    same = (dest_device[:, None] == dest_device[None, :]) & (row_ids[:, None] < row_ids[None, :])
    return jnp.sum(same.astype(jnp.int32), axis=0)


def live_mask(lengths_block, row_total):
    row_ids = jnp.arange(row_total, dtype=jnp.int32)
    utterance = row_ids // LMAX
    frame_pos = row_ids % LMAX
    picks = utterance[None, :] == jnp.arange(lengths_block.shape[0], dtype=jnp.int32)[:, None]
    row_length = jnp.sum(jnp.where(picks, lengths_block[:, None], 0), axis=0)
    return (frame_pos < row_length).astype(F32)


def shape(*dims, dtype=F32):
    return jax.ShapeDtypeStruct(dims, dtype)


def call(kernel, scalars, arrays, out_shape, grant, scratch=()):
    in_specs = [pl.BlockSpec(memory_space=pltpu.SMEM)] if scalars is not None else []
    operands = [scalars] if scalars is not None else []
    out_specs = jax.tree.map(lambda _: pl.BlockSpec(memory_space=pltpu.VMEM), out_shape)
    return pl.pallas_call(
        kernel,
        in_specs=in_specs + [pl.BlockSpec(memory_space=pltpu.VMEM) for _ in arrays],
        out_specs=out_specs,
        out_shape=out_shape,
        scratch_shapes=list(scratch),
        compiler_params=pltpu.CompilerParams(vmem_limit_bytes=grant << 20),
    )(*operands, *arrays)


def on_core(core, cores, run):
    for index in range(cores):
        pl.when(core == index)(functools.partial(run, index))


def soft_kernel(half, cores, ids_ref, logits_ref, weight_ref, hot_ref, target_ref, mine_ref, other_ref, mass_ref, powers_ref):
    vocab, rows = logits_ref.shape
    block = math.gcd(half, vocab - half)

    def rows_at(index):
        return pl.ds(pl.multiple_of(index * block, block), block)

    def highest(index, top):
        values = logits_ref[rows_at(index), :].astype(F32)
        return jnp.maximum(top, jnp.max(values, axis=0, keepdims=True))

    top = lax.fori_loop(
        0, vocab // block, highest, jnp.full((1, rows), -jnp.inf, F32), unroll=5
    )

    def raised(index, total):
        powers = jnp.exp(logits_ref[rows_at(index), :].astype(F32) - top)
        powers_ref[rows_at(index), :] = powers
        return total + jnp.sum(powers, axis=0, keepdims=True)

    total = lax.fori_loop(0, vocab // block, raised, jnp.zeros((1, rows), F32), unroll=5)
    scale = weight_ref[...] / total
    hot = hot_ref[...]
    places = lax.broadcasted_iota(jnp.int32, (block, rows), 0)

    def write(out_ref, start, count, mass):
        def one(index, mass):
            at = index * block + start
            soft = powers_ref[pl.ds(pl.multiple_of(at, block), block), :] * scale
            soft = soft + jnp.where(places + at == target_ref[...], hot, 0.0)
            soft = soft.astype(BF16)
            out_ref[rows_at(index), :] = soft
            return mass + jnp.sum(soft.astype(F32), axis=0, keepdims=True)

        return lax.fori_loop(0, count // block, one, mass, unroll=4)

    def run(core):
        refs = (mine_ref, other_ref)
        low_ref, high_ref = refs if core == 0 else refs[::-1]
        mass = write(low_ref, 0, half, jnp.zeros((1, rows), F32))
        mass_ref[...] = write(high_ref, half, vocab - half, mass)
        high_ref[vocab - half :, :] = jnp.zeros((2 * half - vocab, rows), BF16)

    on_core(ids_ref[0], cores, run)


def select_kernel(
    cores, chips, plans, ids_ref, place_ref, near_ref, far_ref, gain_ref,
    normed_ref, scaled_ref, *refs,
):
    state_refs, turned_ref = refs[:-1], refs[-1]
    rows = place_ref.shape[1]
    count = near_ref.shape[0]
    width = near_ref.shape[1]
    block = width // (cores * chips)
    ids = lax.broadcasted_iota(jnp.int32, (count, rows), 0)
    place = place_ref[...]

    def taken(hit, states_ref):
        return lax.dot_general(
            hit.astype(F32).astype(BF16),
            states_ref[...],
            CONTRACT_FIRST,
            preferred_element_type=F32,
        )

    hidden = taken(place == ids, near_ref) + taken(place - count == ids, far_ref)
    centre = jnp.mean(hidden, axis=1, keepdims=True)
    moved = hidden - centre
    spread = jnp.mean(moved * moved, axis=1, keepdims=True)
    normed = moved * lax.rsqrt(spread + EPSILON)
    normed_ref[...] = normed
    scaled = normed * gain_ref[...]
    scaled_ref[...] = scaled.astype(BF16)
    turned_ref[...] = scaled.T
    refs = iter(state_refs)
    for side, ((stride, size), strides) in enumerate(plans):
        for step in range(size):
            to_near = lax.rem(ids_ref[1 + side] + step, size) * stride
            places = [0]
            for far in strides:
                places = [at + bit * far for at in places for bit in (0, 1)]
            groups = []
            for at in places:
                for core in range(cores):
                    first = (core * chips + at + to_near) * block
                    groups.append(turned_ref[pl.ds(pl.multiple_of(first, block), block), :])
            next(refs)[...] = jnp.concatenate(groups, axis=0).astype(BF16)


def forward_kernel(
    cores, tile, ids_ref, scaled_ref, weight_ref, bias_ref, mine_ref, other_ref,
    powers_ref, stats_ref, dots_ref,
):
    vocab = weight_ref.shape[0]
    rows = scaled_ref.shape[0]

    def run(core):
        scaled = scaled_ref[...]
        dots = jnp.zeros((1, rows), F32)
        for index in range(TILES):
            first = (core * TILES + index) * tile
            count = max(0, min(tile, vocab - first))
            at = slice(index * tile, index * tile + count)
            logits = lax.dot_general(
                weight_ref[first : first + count, :], scaled, CONTRACT_LAST,
                preferred_element_type=F32,
            )
            bias = jnp.broadcast_to(bias_ref[:, first : first + count], (LANES, count)).T
            logits = logits + jnp.concatenate([bias] * (rows // LANES), axis=1)
            top = jnp.max(logits, axis=0, keepdims=True)
            powers = jnp.exp(logits - top)
            powers_ref[at, :] = powers
            if count < tile:
                powers_ref[index * tile + count : (index + 1) * tile, :] = jnp.zeros(
                    (tile - count, rows), F32
                )
            soft = mine_ref[at, :].astype(F32) + other_ref[at, :].astype(F32)
            stats_ref[index : index + 1, :] = top
            stats_ref[TILES + index : TILES + index + 1, :] = jnp.sum(
                powers, axis=0, keepdims=True
            )
            dots = dots + jnp.sum(soft * logits, axis=0, keepdims=True)
        dots_ref[...] = dots

    on_core(ids_ref[0], cores, run)


def grad_kernel(
    turn, powers_ref, stats_ref, stats_far_ref, mass_ref, mass_far_ref, dots_ref,
    mine_ref, other_ref, first_ref, second_ref, loss_ref,
):
    stats, stats_far = stats_ref[...], stats_far_ref[...]
    tops, tops_far = stats[:TILES], stats_far[:TILES]
    top = jnp.maximum(
        jnp.max(tops, axis=0, keepdims=True), jnp.max(tops_far, axis=0, keepdims=True)
    )
    shrunk = jnp.exp(tops - top)
    terms = stats[TILES:] * shrunk + stats_far[TILES:] * jnp.exp(tops_far - top)
    total = jnp.sum(terms, axis=0, keepdims=True)
    mass = mass_ref[...] + mass_far_ref[...]
    scale = shrunk * (mass / total)
    tile = first_ref.shape[0]
    for index, out_ref in ((turn, first_ref), (turn + TURNS, second_ref)):
        at = slice(index * tile, (index + 1) * tile)
        grad = powers_ref[at, :] * scale[index : index + 1]
        grad = grad - mine_ref[at, :].astype(F32) - other_ref[at, :].astype(F32)
        out_ref[...] = grad.astype(BF16)
    loss = 0.5 * mass * (top + jnp.log(total)) - dots_ref[...]
    loss_ref[...] = jnp.broadcast_to(jnp.sum(loss, axis=1, keepdims=True), loss_ref.shape)


def back_kernel(cores, tile, ids_ref, weight_ref, normed_ref, loss_ref, live_ref, *refs):
    grads, out_ref = refs[:TILES], refs[TILES]
    vocab, width = weight_ref.shape
    rows = normed_ref.shape[0]
    half = TILES * tile
    ones = jnp.ones((8, rows), BF16)

    def run(core):
        total = None
        for index in range(TILES):
            first = (core * TILES + index) * tile
            count = max(0, min(tile, vocab - first))
            grad = grads[index][...]
            sums = lax.dot_general(ones, grad, CONTRACT_LAST, preferred_element_type=F32)
            out_ref[:, index * tile : (index + 1) * tile] = sums[:1]
            term = lax.dot_general(
                grads[index][:count, :], weight_ref[first : first + count, :], CONTRACT_FIRST,
                preferred_element_type=F32,
            )
            total = term if total is None else total + term
        out_ref[:, half : half + width] = jnp.sum(total * normed_ref[...], axis=0, keepdims=True)

    on_core(ids_ref[0], cores, run)
    lane = lax.broadcasted_iota(jnp.int32, (1, LANES), 1)
    frames = jnp.sum(live_ref[...], axis=1, keepdims=True)
    out_ref[:, half + width :] = jnp.where(
        lane == 0, loss_ref[...], jnp.where(lane == 1, frames, 0.0)
    )


def term_kernel(near, ids_ref, *refs):
    states, grads, (kept_ref, sent_ref) = refs[:near], refs[near : 2 * near], refs[2 * near :]
    count = kept_ref.shape[0]

    def product(side):
        rows = pl.ds(pl.multiple_of(side * count, count), count)
        total = None
        for state, grad in zip(states, grads):
            term = lax.dot_general(
                state[rows, :], grad[...], CONTRACT_LAST, preferred_element_type=F32
            )
            total = term if total is None else total + term
        return total

    sent_ref[...] = product(1 - ids_ref[0]).astype(BF16)
    kept_ref[...] = product(ids_ref[0])


def halve_kernel(parts, ids_ref, *refs):
    kept, came, (kept_ref, sent_ref) = refs[:parts], refs[parts : 2 * parts], refs[2 * parts :]
    count, width = kept_ref.shape
    width = width // parts
    for index in range(parts):
        at = slice(index * width, (index + 1) * width)

        def total(side):
            rows = pl.ds(pl.multiple_of(side * count, count), count)
            return kept[index][rows, :] + came[index][rows, :].astype(F32)

        sent_ref[:, at] = total(1 - ids_ref[0]).astype(BF16)
        kept_ref[:, at] = total(ids_ref[0])


def halve(bit, kept, came):
    count = kept[0].shape[0] // 2
    width = sum(part.shape[1] for part in kept)
    return call(
        functools.partial(halve_kernel, len(kept)),
        bit[None],
        [*kept, *came],
        [shape(count, width), shape(count, width, dtype=BF16)],
        6,
    )


def split_kernel(tile, ids_ref, *refs):
    kept, came, (mine_ref, sent_ref) = refs[:TURNS], refs[TURNS : 2 * TURNS], refs[2 * TURNS :]
    count = mine_ref.shape[0]

    def total(turn, core):
        rows = pl.ds(pl.multiple_of(core * count, count), count)
        return kept[turn][rows, :] + came[turn][rows, :].astype(F32)

    for turn in range(TURNS):
        for out_ref, core in ((mine_ref, ids_ref[0]), (sent_ref, 1 - ids_ref[0])):
            both = total(turn, core)
            out_ref[:, turn * tile : (turn + 1) * tile] = both[:, :tile]
            far = (turn + TURNS) * tile
            out_ref[:, far : far + tile] = both[:, tile:]


def sum_kernel(*refs):
    total = refs[0][...]
    for ref in refs[1:-1]:
        total = total + ref[...]
    refs[-1][...] = total


def small_kernel(cores, half, width, ids_ref, near_ref, far_ref, gain_ref, bias_ref, tail_ref):
    vocab = bias_ref.shape[1]
    tail, tail_far = near_ref[:, half + width :], far_ref[:, half + width :]
    inverse = 1.0 / tail[:, 1:2]
    near, far = near_ref[:, half : half + width], far_ref[:, half : half + width]
    gain_ref[...] = (near + far) * inverse
    lane = lax.broadcasted_iota(jnp.int32, tail.shape, 1)
    tail_ref[...] = jnp.where(lane == 0, (tail + tail_far) * inverse, inverse)

    def run(core):
        low, high = (near_ref, far_ref) if core == 0 else (far_ref, near_ref)
        bias_ref[:, :half] = low[:, :half] * inverse
        bias_ref[:, half:] = high[:, : vocab - half] * inverse

    on_core(ids_ref[0], cores, run)


def finish_kernel(cores, ids_ref, mine_ref, came_ref, tail_ref, out_ref):
    half = mine_ref.shape[1]
    vocab = out_ref.shape[1]
    inverse = tail_ref[:, 1:2]

    def run(core):
        low, high = (mine_ref, came_ref) if core == 0 else (came_ref, mine_ref)
        out_ref[:, :half] = low[...] * inverse
        out_ref[:, half:] = high[:, : vocab - half] * inverse

    on_core(ids_ref[0], cores, run)


def body(
    teacher_logits, routes, agreement, targets, lengths, student_hidden, out_weight, out_bias, gain
):
    cores = lax.axis_size("teach")
    chips = lax.axis_size("dp")
    devices = cores * chips
    rows = teacher_logits.shape[1]
    slots = cores * rows // devices
    vocab = teacher_logits.shape[2]
    width = student_hidden.shape[1]
    out_rows = width // devices
    size_a, size_b, size_c = torus_factors(chips)
    bits_a, bits_b, bits_c = bits_of(size_a), bits_of(size_b), bits_of(size_c)
    tile = -(-vocab // (TILES * cores * LANES)) * LANES
    half = TILES * tile
    core = lax.axis_index("teach").astype(jnp.int32)
    chip = lax.axis_index("dp").astype(jnp.int32)
    ids = core[None]
    exchange = [(i, 1 - i) for i in range(cores)]
    deep = [size_a * size_b << k for k in range(bits_c)]
    plans = (
        ((1, size_a), [size_a << k for k in range(bits_b)] + deep),
        ((size_a, size_b), [1 << k for k in range(bits_a)] + deep),
    )

    def swap(value):
        return lax.ppermute(value, "teach", exchange)

    def bit_of(stride):
        return (chip // stride) % 2

    def along(value, stride, size, step):
        return lax.ppermute(value, "dp", rotation(chips, stride, size, step))

    def flip(value, mask):
        return lax.ppermute(value, "dp", [(i, i ^ mask) for i in range(chips)])

    arrived = lax.all_to_all(
        student_hidden.reshape(chips, slots, width),
        "dp",
        split_axis=0,
        concat_axis=0,
        tiled=True,
    ).reshape(chips * slots, width)
    arrived_far = swap(arrived)

    dest_device = routes[:, 0]
    live_rows = live_mask(lengths, rows)
    mine, other, mass = call(
        functools.partial(soft_kernel, half, cores),
        ids,
        [
            teacher_logits[0].T,
            (0.5 * agreement.astype(F32) * live_rows)[None, :],
            (0.5 * live_rows)[None, :],
            targets[None, :],
        ],
        [shape(half, rows, dtype=BF16), shape(half, rows, dtype=BF16), shape(1, rows)],
        8,
        [pltpu.VMEM((vocab, rows), F32)],
    )
    other = swap(other)
    mass_far = swap(mass)

    place = (dest_device % chips) * slots + route_slots(dest_device)
    place = jnp.where(dest_device // chips == core, place, place + chips * slots)
    near_ids = [(chip // stride) % size for (stride, size), _ in plans]
    normed, scaled, *own_states = call(
        functools.partial(select_kernel, cores, chips, plans),
        jnp.stack([core, *near_ids]),
        [place[None, :], arrived, arrived_far, gain[None, :]],
        [shape(rows, width), shape(rows, width, dtype=BF16)]
        + [shape(width // size, rows, dtype=BF16) for (_, size), _ in plans for _ in range(size)],
        12,
        [pltpu.VMEM((width, rows), F32)],
    )
    states = []
    for (stride, size), _ in plans:
        states.append(
            [
                along(piece, stride, size, step) if step else piece
                for step, piece in enumerate(own_states[:size])
            ]
        )
        own_states = own_states[size:]

    weight = out_weight.T
    powers, stats, dots = call(
        functools.partial(forward_kernel, cores, tile),
        ids,
        [scaled, weight, out_bias[None, :], mine, other],
        [shape(half, rows), shape(2 * TILES, rows), shape(1, rows)],
        12,
    )
    stats_far = swap(stats)

    grads = [None] * TILES
    for turn in range(TURNS):
        grads[turn], grads[turn + TURNS], loss = call(
            functools.partial(grad_kernel, turn),
            None,
            [powers, stats, stats_far, mass, mass_far, dots, mine, other],
            [shape(tile, rows, dtype=BF16)] * 2 + [shape(1, LANES)],
            6,
        )

    gathered = {}
    for turn in range(TURNS):
        for side, ((stride, size), _) in enumerate(plans):
            grad = grads[turn + TURNS * side]
            gathered[turn, side] = [
                along(grad, stride, size, step) if step else grad for step in range(size)
            ]

    ends = []
    for turn in range(TURNS):
        kept, came = [], []
        for side, ((_, size), strides) in enumerate(plans):
            count = width // size // 2
            part, sent = call(
                functools.partial(term_kernel, size),
                bit_of(strides[0])[None],
                [*states[side], *gathered[turn, side]],
                [shape(count, tile), shape(count, tile, dtype=BF16)],
                6,
            )
            for depth, stride in enumerate(strides[: len(strides) - bits_c]):
                if depth:
                    part, sent = halve(bit_of(stride), [part], [got])
                got = flip(sent, stride)
            kept.append(part)
            came.append(got)
        for stride in deep:
            part, sent = halve(bit_of(stride), kept, came)
            kept, came = [part], [flip(sent, stride)]
        ends += kept + came

    small = call(
        functools.partial(back_kernel, cores, tile),
        ids,
        [weight, normed, loss, live_rows[None, :], *grads],
        shape(1, half + width + LANES),
        10,
    )
    for strides in (deep, [1 << k for k in range(bits_a + bits_b)]):
        got = [flip(small, mask) for mask in flips(strides)]
        small = call(sum_kernel, None, [small, *got], shape(*small.shape), 2)
    small_far = swap(small)
    gain_sum, bias_sum, tail = call(
        functools.partial(small_kernel, cores, half, width),
        ids,
        [small, small_far],
        [shape(1, width), shape(1, vocab), shape(1, LANES)],
        2,
    )

    own, sent = call(
        functools.partial(split_kernel, tile),
        ids,
        ends[::2] + ends[1::2],
        [shape(out_rows, half)] * 2,
        4,
    )
    weight_grad = call(
        functools.partial(finish_kernel, cores),
        ids,
        [own, swap(sent), tail],
        shape(out_rows, vocab),
        4,
    )
    return (weight_grad, gain_sum[0], bias_sum[0], tail[0, 0])


def solution(mesh):
    return jax.shard_map(
        body,
        mesh=mesh,
        in_specs=(
            P("teach", "dp", None),
            P("dp", None),
            P("dp"),
            P("dp"),
            P("dp"),
            P(("teach", "dp"), None),
            P(),
            P(),
            P(),
        ),
        out_specs=(P(("teach", "dp"), None), P(), P(), P()),
        check_vma=False,
    )
```

time: 531 us -> 127 us (0.24)
  waiting for transfers between devices: 393 us -> 51.9 us
  blocking collectives: 49 us -> 0 us
  Pallas kernels: 0 us -> 24.7 us
  matrix products: 21.3 us -> 0 us
  other arithmetic: 17.9 us -> 0.92 us
  starting transfers between devices: 12.7 us -> 29.5 us
  between operations: 18 us -> 1.49 us
    reduce_scatter x1 -> x0, waiting for transfers between devices: 383 us -> none  [body(): lax.psum_scatter(lax.dot_general(state_rows, grad_rows, (((0,), (0,)), ((...]
    psum x1 -> x0, blocking collectives: 49 us -> none  [body(): total_frames = lax.psum(count_term, ('teach', 'dp'))]
    ppermute x0 -> x26, waiting for transfers between devices: none -> 45.6 us  [the longest x14 25.3 us: flip(): return lax.ppermute(value, 'dp', [(i, i ^ mask) for i in range(chips)])]
    pallas_call x0 -> x19, Pallas kernels: none -> 24.7 us  [call(): pl.pallas_call(kernel, in_specs=in_specs + [pl.BlockSpec(memory_space=plt...]
    dot_general x4 -> x0, matrix products: 21.3 us -> none  [the longest x1 8.65 us: body(): lax.dot_general(state_rows, grad_rows, (((0,), (0,)), ((), ())), preferre...]
    ppermute x0 -> x26, starting transfers between devices: none -> 21.1 us  [the longest x14 14.7 us: flip(): return lax.ppermute(value, 'dp', [(i, i ^ mask) for i in range(chips)])]
    unnamed x16 -> x40, local copies, waits for them, and re-layouts: 1.07 us -> 17.7 us
    convert_element_type x2 -> x0, local copies, waits for them, and re-layouts: 9.89 us -> none  [soft_targets(): probs_teacher = jax.nn.softmax(teacher_rows.astype(jnp.float32), axis=-1)]
  transfers between devices with their start and end apart: 3 -> 27, of which waited for: 2 -> 16; matrix products, arithmetic and copies ran while one was open for 7% -> 1% of each run, Pallas kernels for 0% -> 19%
where the time goes in v3:
time: 127 us; the launch traced here: 126 us
  waiting for transfers between devices  51.9 us (41%)
  starting transfers between devices  29.5 us (23%)
  Pallas kernels  24.7 us (19%)
  local copies, waits for them, and re-layouts  17.7 us (14%)
  between operations  1.49 us (1%)
    ppermute x14, waiting for transfers between devices, flip(): return lax.ppermute(value, 'dp', [(i, i ^ mask) for i in range(chips)])  25.3 us
    pallas_call x19, Pallas kernels, call(): pl.pallas_call(kernel, in_specs=in_specs + [pl.BlockSpec(memory_space=plt...  24.7 us
    unnamed x40, local copies, waits for them, and re-layouts  17.7 us
    ppermute x6, waiting for transfers between devices, along(): return lax.ppermute(value, 'dp', rotation(chips, stride, size, step))  16.4 us
    ppermute x14, starting transfers between devices, flip(): return lax.ppermute(value, 'dp', [(i, i ^ mask) for i in range(chips)])  14.7 us
    all_to_all x1, starting transfers between devices, body(): lax.all_to_all(student_hidden.reshape(chips, slots, width), 'dp', split_a...  8.48 us
    all_to_all x1, waiting for transfers between devices, body(): lax.all_to_all(student_hidden.reshape(chips, slots, width), 'dp', split_a...  6.32 us
    ppermute x6, starting transfers between devices, along(): return lax.ppermute(value, 'dp', rotation(chips, stride, size, step))  5.62 us
  transfers between devices with their start and end apart: 27, of which 16 were waited for; matrix products, arithmetic and copies ran while one was open for 1% of the time, Pallas kernels for 19%

profile of v3, /device:TPU:0, one launch (start us, length us, event | category | flops | bytes accessed | tf_op | source)
XLA Modules:
  0.0 126.1 jit_solution(12157092594701401875)
XLA Ops:
  0.7 8.5 %all-to-all-start = ((bf16[16,16,1024]{2,1,0:T(8,128)(2,1)}), bf16[16,16,1024]{2,1,0:T(8,128)(2,1)S(1)}, u32[]{:S(2)}, u32[]{:S(2)}) async-start(bf16[16,16,1024]{2,1,0:T(8,128)(2,1)} %bitcast.48), calls=%async_computation | async-start | bytes 1048576 | tf_op jit(solution)/shard_map/all_to_all | solution.py:404
  10.5 1.7 %copy-done.2 = bf16[1,256,5000]{1,2,0:T(8,128)(2,1)S(1)} copy-done((bf16[1,256,5000]{1,2,0:T(8,128)(2,1)S(1)}, bf16[1,256,5000]{1,2,0:T(8,128)(2,1)}, u32[]{:S(2)}) %copy-start.2) | copy-done | bytes 2560024
  12.9 5.0 %shard_map.121 = (bf16[2560,256]{1,0:T(8,128)(2,1)S(1)}, bf16[2560,256]{1,0:T(8,128)(2,1)}, f32[1,256]{1,0:T(1,128)S(1)}) custom-call(s32[1]{0:T(128)} %bitcast.ids_ref, bf16[5000,256]{1,0:T(8,128)(2,1)S(1)} %bitcast.40, f32[1,256]{1,0:T(1,128)S(1)} %bitcast.45, f32[1,256]{1,0:T(1,128)S(1)} %broadcast_select_fusion.hot_ref, s32[1,256]{1,0:T(1,128)S(1)} %bitcast.46), custom_call_target="tpu_custom_call" | custom-call | tf_op jit(solution)/shard_map/pallas_call | solution.py:72
  17.9 6.3 %all-to-all-done = bf16[16,16,1024]{2,1,0:T(8,128)(2,1)S(1)} async-done(((bf16[16,16,1024]{2,1,0:T(8,128)(2,1)}), bf16[16,16,1024]{2,1,0:T(8,128)(2,1)S(1)}, u32[]{:S(2)}, u32[]{:S(2)}) %all-to-all-start) | async-done | bytes 524320 | tf_op jit(solution)/shard_map/all_to_all | solution.py:404
  24.5 1.8 %collective-permute-done.far_ref = bf16[256,1024]{1,0:T(8,128)(2,1)} collective-permute-done((bf16[256,1024]{1,0:T(8,128)(2,1)S(1)}, bf16[256,1024]{1,0:T(8,128)(2,1)}, u32[]{:S(2)}, u32[]{:S(2)}) %collective-permute-start) | collective-permute-done | bytes 524320 | tf_op jit(solution)/shard_map/ppermute | solution.py:393
  26.3 2.3 %shard_map.120 = (f32[256,1024]{1,0:T(8,128)S(1)}, bf16[256,1024]{1,0:T(8,128)(2,1)S(1)}, bf16[512,256]{1,0:T(8,128)(2,1)S(1)}, bf16[512,256]{1,0:T(8,128)(2,1)S...) custom-call(s32[3]{0:T(128)S(1)} %pad_add_fusion.ids_ref, s32[1,256]{1,0:T(1,128)S(1)} %compare_select_fusion.1.place_ref, ...), custom_call_target="tpu_custom_call" | custom-call | tf_op jit(solution)/shard_map/pallas_call | solution.py:72
  28.6 1.0 copy-done.7
  30.1 3.9 %copy-done = bf16[1024,5000]{0,1:T(8,128)(2,1)S(1)} copy-done((bf16[1024,5000]{0,1:T(8,128)(2,1)S(1)}, bf16[1024,5000]{0,1:T(8,128)(2,1)}, u32[]{:S(2)}) %copy-start) | copy-done | bytes 10240024
  34.0 2.3 %shard_map.122 = (f32[2560,256]{1,0:T(8,128)S(1)}, f32[8,256]{1,0:T(8,128)S(1)}, f32[1,256]{1,0:T(1,128)S(1)}) custom-call(s32[1]{0:T(128)} %bitcast.ids_ref, bf16[256,1024]{1,0:T(8,128)(2,1)S(1)} %get-tuple-element.44.scaled_ref, bf16[5000,1024]{1,0:T(8,128)(2,1)S(1)} %bitcast.38, f32[1,5000]{1,0:T(1,128)S(1)} %bitcast.43, ...), custom_call_target="tpu_custom_call" | custom-call | tf_op jit(solution)/shard_map/pallas_call | solution.py:72
  38.3 1.5 %collective-permute-start.11 = (bf16[640,256]{1,0:T(8,128)(2,1)S(1)}, bf16[640,256]{1,0:T(8,128)(2,1)S(1)}, u32[]{:S(2)}, u32[]{:S(2)}) collective-permute-start(bf16[640,256]{1,0:T(8,128)(2,1)S(1)} %get-tuple-element.62.refs_2_.refs_1_), channel_id=1, source_target_pairs={{0,1},{1,0},{2,3},{3,2},{4,5},{5,4},{6,7},{7,6},{8,9},{9,8},{10,11... | collective-permute-start | bytes 983048 | tf_op jit(solution)/shard_map/ppermute | solution.py:399
  39.7 1.0 collective-permute-start.12
  40.7 1.0 shard_map.123
  42.3 1.0 collective-permute-start.7
  43.4 1.0 collective-permute-start.6
  44.4 4.5 %collective-permute-done.11.refs_3_ = bf16[640,256]{1,0:T(8,128)(2,1)S(1)} collective-permute-done((bf16[640,256]{1,0:T(8,128)(2,1)S(1)}, bf16[640,256]{1,0:T(8,128)(2,1)S(1)}, u32[]{:S(2)}, u32[]{:S(2)}) %collective-permute-start.11) | collective-permute-done | bytes 327712 | tf_op jit(solution)/shard_map/ppermute | solution.py:399
  48.9 1.2 shard_map.129
  50.1 1.0 collective-permute-start.13
  51.1 11.9 %collective-permute-done.6.refs_1_ = bf16[512,256]{1,0:T(8,128)(2,1)S(1)} collective-permute-done((bf16[512,256]{1,0:T(8,128)(2,1)S(1)}, bf16[512,256]{1,0:T(8,128)(2,1)S(1)}, u32[]{:S(2)}, u32[]{:S(2)}) %collective-permute-start.6) | collective-permute-done | bytes 262176 | tf_op jit(solution)/shard_map/ppermute | solution.py:399
  63.0 1.2 shard_map.130
  64.7 1.2 shard_map.124
  65.9 1.0 collective-permute-start.8
  66.9 1.2 shard_map.125
  68.9 1.4 %collective-permute-start.9 = (bf16[256,640]{1,0:T(8,128)(2,1)}, bf16[256,640]{1,0:T(8,128)(2,1)}, u32[]{:S(2)}, u32[]{:S(2)}) collective-permute-start(bf16[256,640]{1,0:T(8,128)(2,1)} %get-tuple-element.58), channel_id=1, source_target_pairs={{0,1},{1,0},{2,3},{3,2},{4,5},{5,4},{6,7},{7,6},{8,9},{9,8},{10,11... | collective-permute-start | bytes 983048 | tf_op jit(solution)/shard_map/ppermute | solution.py:402
  70.4 4.7 %collective-permute-done.14.refs_3_ = bf16[256,640]{1,0:T(8,128)(2,1)} collective-permute-done((bf16[256,640]{1,0:T(8,128)(2,1)}, bf16[256,640]{1,0:T(8,128)(2,1)}, u32[]{:S(2)}, u32[]{:S(2)}) %collective-permute-start.14) | collective-permute-done | bytes 327712 | tf_op jit(solution)/shard_map/ppermute | solution.py:402
  75.1 1.8 %shard_map.131 = (f32[128,1280]{1,0:T(8,128)S(1)}, bf16[128,1280]{1,0:T(8,128)(2,1)}) custom-call(s32[1]{0:T(128)} %bitcast.2.ids_ref, f32[256,640]{1,0:T(8,128)S(1)} %get-tuple-element.63.refs_0_, f32[256,640]{1,0:T(8,128)S(1)} %get-tuple-element.65.refs_1_, bf16[256,640]{1,0:T(8,128)(2,1)S(1)} %collective-permute-done.13.refs_2_, ...), custom_call_target="tpu_custom_call" | custom-call | tf_op jit(solution)/shard_map/pallas_call | solution.py:72
  77.7 1.3 %collective-permute-start.15 = (bf16[128,1280]{1,0:T(8,128)(2,1)}, bf16[128,1280]{1,0:T(8,128)(2,1)}, u32[]{:S(2)}, u32[]{:S(2)}) collective-permute-start(bf16[128,1280]{1,0:T(8,128)(2,1)} %get-tuple-element.69), channel_id=1, source_target_pairs={{0,4},{1,5},{2,6},{3,7},{4,0},{5,1},{6,2},{7,3},{8,12},{9,13},{10,... | collective-permute-start | bytes 983048 | tf_op jit(solution)/shard_map/ppermute | solution.py:402
  79.4 1.1 copy-done.12
  80.5 1.9 %shard_map.126 = (f32[128,1280]{1,0:T(8,128)S(1)}, bf16[128,1280]{1,0:T(8,128)(2,1)}) custom-call(s32[1]{0:T(128)} %bitcast.2.ids_ref, f32[256,640]{1,0:T(8,128)S(1)} %get-tuple-element.52.refs_0_, f32[256,640]{1,0:T(8,128)S(1)} %copy-done.12, bf16[256,640]{1,0:T(8,128)(2,1)} %collective-permute-done.8.refs_2_, bf16[256,640]{1,0:T(8,128)(2,1)} %collective-permute-done.9.refs_3_), custom_call_target="tpu_custom_call" | custom-call | tf_op jit(solution)/shard_map/pallas_call | solution.py:72
  83.2 1.3 %collective-permute-start.10 = (bf16[128,1280]{1,0:T(8,128)(2,1)}, bf16[128,1280]{1,0:T(8,128)(2,1)S(1)}, u32[]{:S(2)}, u32[]{:S(2)}) collective-permute-start(bf16[128,1280]{1,0:T(8,128)(2,1)} %get-tuple-element.60), channel_id=1, source_target_pairs={{0,4},{1,5},{2,6},{3,7},{4,0},{5,1},{6,2},{7,3},{8,12},{9,13},{10,... | collective-permute-start | bytes 983048 | tf_op jit(solution)/shard_map/ppermute | solution.py:402
  84.6 2.1 %collective-permute-done.15.refs_1_ = bf16[128,1280]{1,0:T(8,128)(2,1)} collective-permute-done((bf16[128,1280]{1,0:T(8,128)(2,1)}, bf16[128,1280]{1,0:T(8,128)(2,1)}, u32[]{:S(2)}, u32[]{:S(2)}) %collective-permute-start.15) | collective-permute-done | bytes 327712 | tf_op jit(solution)/shard_map/ppermute | solution.py:402
  86.7 1.1 copy-done.10
  87.7 1.0 shard_map.132
  88.8 5.8 %collective-permute-done.10.refs_1_ = bf16[128,1280]{1,0:T(8,128)(2,1)S(1)} collective-permute-done((bf16[128,1280]{1,0:T(8,128)(2,1)}, bf16[128,1280]{1,0:T(8,128)(2,1)S(1)}, u32[]{:S(2)}, u32[]{:S(2)}) %collective-permute-start.10) | collective-permute-done | bytes 327712 | tf_op jit(solution)/shard_map/ppermute | solution.py:402
  94.7 1.1 copy-done.14
  95.9 3.6 %collective-permute-done.17.refs_3_ = bf16[64,1280]{1,0:T(8,128)(2,1)S(1)} collective-permute-done((bf16[64,1280]{1,0:T(8,128)(2,1)S(1)}, bf16[64,1280]{1,0:T(8,128)(2,1)S(1)}, u32[]{:S(2)}, u32[]{:S(2)}) %collective-permute-start.17) | collective-permute-done | bytes 163872 | tf_op jit(solution)/shard_map/ppermute | solution.py:402
  99.5 4.4 %collective-permute-done.16.refs_2_ = bf16[64,1280]{1,0:T(8,128)(2,1)S(1)} collective-permute-done((bf16[64,1280]{1,0:T(8,128)(2,1)S(1)}, bf16[64,1280]{1,0:T(8,128)(2,1)S(1)}, u32[]{:S(2)}, u32[]{:S(2)}) %collective-permute-start.16) | collective-permute-done | bytes 163872 | tf_op jit(solution)/shard_map/ppermute | solution.py:402
  104.0 3.9 %copy-done.1 = bf16[1024,5000]{0,1:T(8,128)(2,1)S(1)} copy-done((bf16[1024,5000]{0,1:T(8,128)(2,1)S(1)}, bf16[1024,5000]{0,1:T(8,128)(2,1)}, u32[]{:S(2)}) %copy-start.1) | copy-done | bytes 10240024
  107.9 2.2 %shard_map.134.refs_0_ = f32[1,3712]{1,0:T(1,128)S(1)} custom-call(s32[1]{0:T(128)} %bitcast.ids_ref, bf16[5000,1024]{1,0:T(8,128)(2,1)S(1)} %bitcast.39, f32[256,1024]{1,0:T(8,128)S(1)} %copy-done.8, f32[1,128]{1,0:T(1,128)S(1)} %get-tuple-element.76.loss_ref, f32[1,256]{1,0:T(1,128)S(1)} %fusion.4.live_ref, bf16[640,256]{1,0:T(8,128)(2,1)S(1)} %copy-done.4, ...), custom_call_target="tpu_custom_call" | custom-call | tf_op jit(solution)/shard_map/pallas_call | solution.py:72
  110.1 2.1 %collective-permute-start.21 = (f32[1,3712]{1,0:T(1,128)S(1)}, f32[1,3712]{1,0:T(1,128)S(1)}, u32[]{:S(2)}, u32[]{:S(2)}) collective-permute-start(f32[1,3712]{1,0:T(1,128)S(1)} %shard_map.134.refs_0_), channel_id=1, source_target_pairs={{0,12},{1,13},{2,14},{3,15},{4,8},{5,9},{6,10},{7,11},{8,4},{9,5},... | collective-permute-start | bytes 44552 | tf_op jit(solution)/shard_map/ppermute | solution.py:402
  112.2 2.3 %collective-permute-start.19 = (f32[1,3712]{1,0:T(1,128)S(1)}, f32[1,3712]{1,0:T(1,128)S(1)}, u32[]{:S(2)}, u32[]{:S(2)}) collective-permute-start(f32[1,3712]{1,0:T(1,128)S(1)} %shard_map.134.refs_0_), channel_id=1, source_target_pairs={{0,4},{1,5},{2,6},{3,7},{4,0},{5,1},{6,2},{7,3},{8,12},{9,13},{10,... | collective-permute-start | bytes 44552 | tf_op jit(solution)/shard_map/ppermute | solution.py:402
  114.5 1.1 collective-permute-done.21.refs_3_
  115.7 1.2 collective-permute-done.20.refs_2_
  117.5 1.4 %collective-permute-start.23 = (f32[1,3712]{1,0:T(1,128)S(1)}, f32[1,3712]{1,0:T(1,128)S(1)}, u32[]{:S(2)}, u32[]{:S(2)}) collective-permute-start(f32[1,3712]{1,0:T(1,128)S(1)} %shard_map.135.refs_0_), channel_id=1, source_target_pairs={{0,2},{1,3},{2,0},{3,1},{4,6},{5,7},{6,4},{7,5},{8,10},{9,11},{10,... | collective-permute-start | bytes 44552 | tf_op jit(solution)/shard_map/ppermute | solution.py:402
  118.9 1.5 %collective-permute-start.22 = (f32[1,3712]{1,0:T(1,128)S(1)}, f32[1,3712]{1,0:T(1,128)S(1)}, u32[]{:S(2)}, u32[]{:S(2)}) collective-permute-start(f32[1,3712]{1,0:T(1,128)S(1)} %shard_map.135.refs_0_), channel_id=1, source_target_pairs={{0,1},{1,0},{2,3},{3,2},{4,5},{5,4},{6,7},{7,6},{8,9},{9,8},{10,11... | collective-permute-start | bytes 44552 | tf_op jit(solution)/shard_map/ppermute | solution.py:402
  120.4 1.1 collective-permute-done.24.refs_3_
  121.5 1.1 collective-permute-done.22.refs_1_
  122.7 1.2 collective-permute-done.25.far_ref
  125.2 0.9 shard_map.138
  (71 shorter events, 10.6 us)
Async XLA Ops:
  0.6 23.7 %copy-start.19 = (s32[256,1]{0,1:T(1,128)S(1)}, s32[256,1]{0,1:T(1,128)}, u32[]{:S(2)}) copy-start(s32[256,1]{0,1:T(1,128)} %param.10) | copy-start | bytes 3076
  0.6 25.6 %copy-start.16 = (f32[1024]{0:T(1024)S(1)}, f32[1024]{0:T(1024)}, u32[]{:S(2)}) copy-start(f32[1024]{0:T(1024)} %param.17) | copy-start | bytes 12292
  0.7 29.5 %copy-start.15 = (f32[5000]{0:T(1024)S(1)}, f32[5000]{0:T(1024)}, u32[]{:S(2)}) copy-start(f32[5000]{0:T(1024)} %param.16) | copy-start | bytes 60004
  0.7 23.6 %all-to-all-start = ((bf16[16,16,1024]{2,1,0:T(8,128)(2,1)}), bf16[16,16,1024]{2,1,0:T(8,128)(2,1)S(1)}, u32[]{:S(2)}, u32[]{:S(2)}) async-start(bf16[16,16,1024]{2,1,0:T(8,128)(2,1)} %bitcast.48), calls=%async_computation | async-start | bytes 1048576 | tf_op jit(solution)/shard_map/all_to_all | solution.py:404
  10.5 1.7 %copy-start.2 = (bf16[1,256,5000]{1,2,0:T(8,128)(2,1)S(1)}, bf16[1,256,5000]{1,2,0:T(8,128)(2,1)}, u32[]{:S(2)}) copy-start(bf16[1,256,5000]{1,2,0:T(8,128)(2,1)} %param.9) | copy-start | bytes 7680004
  12.2 0.7 copy-start.17
  17.9 12.2 %collective-permute-start.2 = (bf16[2560,256]{1,0:T(8,128)(2,1)}, bf16[2560,256]{1,0:T(8,128)(2,1)S(1)}, u32[]{:S(2)}, u32[]{:S(2)}) collective-permute-start(bf16[2560,256]{1,0:T(8,128)(2,1)} %get-tuple-element.46), channel_id=1, source_target_pairs={{0,16},{16,0},{1,17},{17,1},{2,18},{18,2},{3,19},{19,3},{4,20},{20... | collective-permute-start | bytes 3932168 | tf_op jit(solution)/shard_map/ppermute | solution.py:393
  24.2 2.0 %collective-permute-start = (bf16[256,1024]{1,0:T(8,128)(2,1)S(1)}, bf16[256,1024]{1,0:T(8,128)(2,1)}, u32[]{:S(2)}, u32[]{:S(2)}) collective-permute-start(bf16[256,1024]{1,0:T(8,128)(2,1)S(1)} %bitcast.41), channel_id=1, source_target_pairs={{0,16},{16,0},{1,17},{17,1},{2,18},{18,2},{3,19},{19,3},{4,20},{20... | collective-permute-start | bytes 1572872 | tf_op jit(solution)/shard_map/ppermute | solution.py:393
  28.6 1.0 copy-start.7
  29.5 13.8 %collective-permute-start.1 = (bf16[512,256]{1,0:T(8,128)(2,1)S(1)}, bf16[512,256]{1,0:T(8,128)(2,1)S(1)}, u32[]{:S(2)}, u32[]{:S(2)}) collective-permute-start(bf16[512,256]{1,0:T(8,128)(2,1)S(1)} %get-tuple-element.43), channel_id=1, source_target_pairs={{0,1},{1,0},{2,3},{3,2},{4,5},{5,4},{6,7},{7,6},{8,9},{9,8},{10,11... | collective-permute-start | bytes 786440 | tf_op jit(solution)/shard_map/ppermute | solution.py:399
  30.1 3.9 %copy-start = (bf16[1024,5000]{0,1:T(8,128)(2,1)S(1)}, bf16[1024,5000]{0,1:T(8,128)(2,1)}, u32[]{:S(2)}) copy-start(bf16[1024,5000]{0,1:T(8,128)(2,1)} %param.15) | copy-start | bytes 30720004
  36.3 1.4 %collective-permute-start.3 = (f32[8,256]{1,0:T(8,128)S(1)}, f32[8,256]{1,0:T(8,128)S(1)}, u32[]{:S(2)}, u32[]{:S(2)}) collective-permute-start(f32[8,256]{1,0:T(8,128)S(1)} %get-tuple-element.48.stats_ref), channel_id=1, source_target_pairs={{0,16},{16,0},{1,17},{17,1},{2,18},{18,2},{3,19},{19,3},{4,20},{20... | collective-permute-start | bytes 24584 | tf_op jit(solution)/shard_map/ppermute | solution.py:393
  36.4 1.3 %collective-permute-start.4 = (f32[1,256]{1,0:T(1,128)S(1)}, f32[1,256]{1,0:T(1,128)S(1)}, u32[]{:S(2)}, u32[]{:S(2)}) collective-permute-start(f32[1,256]{1,0:T(1,128)S(1)} %get-tuple-element.49.mass_ref), channel_id=1, source_target_pairs={{0,16},{16,0},{1,17},{17,1},{2,18},{18,2},{3,19},{19,3},{4,20},{20... | collective-permute-start | bytes 3080 | tf_op jit(solution)/shard_map/ppermute | solution.py:393
  38.3 10.6 %collective-permute-start.11 = (bf16[640,256]{1,0:T(8,128)(2,1)S(1)}, bf16[640,256]{1,0:T(8,128)(2,1)S(1)}, u32[]{:S(2)}, u32[]{:S(2)}) collective-permute-start(bf16[640,256]{1,0:T(8,128)(2,1)S(1)} %get-tuple-element.62.refs_2_.refs_1_), channel_id=1, source_target_pairs={{0,1},{1,0},{2,3},{3,2},{4,5},{5,4},{6,7},{7,6},{8,9},{9,8},{10,11... | collective-permute-start | bytes 983048 | tf_op jit(solution)/shard_map/ppermute | solution.py:399
  39.7 23.2 %collective-permute-start.12 = (bf16[640,256]{1,0:T(8,128)(2,1)S(1)}, bf16[640,256]{1,0:T(8,128)(2,1)S(1)}, u32[]{:S(2)}, u32[]{:S(2)}) collective-permute-start(bf16[640,256]{1,0:T(8,128)(2,1)S(1)} %get-tuple-element.64.refs_2_.refs_3_), channel_id=1, source_target_pairs={{0,2},{1,3},{2,0},{3,1},{4,6},{5,7},{6,4},{7,5},{8,10},{9,11},{10,... | collective-permute-start | bytes 983048 | tf_op jit(solution)/shard_map/ppermute | solution.py:399
  41.7 23.0 %copy-start.3 = (bf16[640,256]{1,0:T(8,128)(2,1)}, bf16[640,256]{1,0:T(8,128)(2,1)S(1)}, u32[]{:S(2)}) copy-start(bf16[640,256]{1,0:T(8,128)(2,1)S(1)} %get-tuple-element.51.refs_2_.refs_0_) | copy-start | bytes 983044
  41.8 25.2 %copy-start.5 = (bf16[640,256]{1,0:T(8,128)(2,1)}, bf16[640,256]{1,0:T(8,128)(2,1)S(1)}, u32[]{:S(2)}) copy-start(bf16[640,256]{1,0:T(8,128)(2,1)S(1)} %get-tuple-element.55.refs_2_) | copy-start | bytes 983044
  41.8 23.0 %collective-permute-start.5 = (bf16[640,256]{1,0:T(8,128)(2,1)S(1)}, bf16[640,256]{1,0:T(8,128)(2,1)S(1)}, u32[]{:S(2)}, u32[]{:S(2)}) collective-permute-start(bf16[640,256]{1,0:T(8,128)(2,1)S(1)} %get-tuple-element.51.refs_2_.refs_0_), channel_id=1, source_target_pairs={{0,1},{1,0},{2,3},{3,2},{4,5},{5,4},{6,7},{7,6},{8,9},{9,8},{10,11... | collective-permute-start | bytes 983048 | tf_op jit(solution)/shard_map/ppermute | solution.py:399
  42.3 24.6 %collective-permute-start.7 = (bf16[640,256]{1,0:T(8,128)(2,1)S(1)}, bf16[640,256]{1,0:T(8,128)(2,1)S(1)}, u32[]{:S(2)}, u32[]{:S(2)}) collective-permute-start(bf16[640,256]{1,0:T(8,128)(2,1)S(1)} %get-tuple-element.55.refs_2_), channel_id=1, source_target_pairs={{0,2},{1,3},{2,0},{3,1},{4,6},{5,7},{6,4},{7,5},{8,10},{9,11},{10,... | collective-permute-start | bytes 983048 | tf_op jit(solution)/shard_map/ppermute | solution.py:399
  43.4 19.6 %collective-permute-start.6 = (bf16[512,256]{1,0:T(8,128)(2,1)S(1)}, bf16[512,256]{1,0:T(8,128)(2,1)S(1)}, u32[]{:S(2)}, u32[]{:S(2)}) collective-permute-start(bf16[512,256]{1,0:T(8,128)(2,1)S(1)} %get-tuple-element.54), channel_id=1, source_target_pairs={{0,2},{1,3},{2,0},{3,1},{4,6},{5,7},{6,4},{7,5},{8,10},{9,11},{10,... | collective-permute-start | bytes 786440 | tf_op jit(solution)/shard_map/ppermute | solution.py:399
  50.1 20.3 %collective-permute-start.13 = (bf16[256,640]{1,0:T(8,128)(2,1)}, bf16[256,640]{1,0:T(8,128)(2,1)S(1)}, u32[]{:S(2)}, u32[]{:S(2)}) collective-permute-start(bf16[256,640]{1,0:T(8,128)(2,1)} %get-tuple-element.66), channel_id=1, source_target_pairs={{0,2},{1,3},{2,0},{3,1},{4,6},{5,7},{6,4},{7,5},{8,10},{9,11},{10,... | collective-permute-start | bytes 983048 | tf_op jit(solution)/shard_map/ppermute | solution.py:402
  64.2 10.9 %collective-permute-start.14 = (bf16[256,640]{1,0:T(8,128)(2,1)}, bf16[256,640]{1,0:T(8,128)(2,1)}, u32[]{:S(2)}, u32[]{:S(2)}) collective-permute-start(bf16[256,640]{1,0:T(8,128)(2,1)} %get-tuple-element.67), channel_id=1, source_target_pairs={{0,1},{1,0},{2,3},{3,2},{4,5},{5,4},{6,7},{7,6},{8,9},{9,8},{10,11... | collective-permute-start | bytes 983048 | tf_op jit(solution)/shard_map/ppermute | solution.py:402
  65.9 13.1 %collective-permute-start.8 = (bf16[256,640]{1,0:T(8,128)(2,1)}, bf16[256,640]{1,0:T(8,128)(2,1)}, u32[]{:S(2)}, u32[]{:S(2)}) collective-permute-start(bf16[256,640]{1,0:T(8,128)(2,1)} %get-tuple-element.57), channel_id=1, source_target_pairs={{0,2},{1,3},{2,0},{3,1},{4,6},{5,7},{6,4},{7,5},{8,10},{9,11},{10,... | collective-permute-start | bytes 983048 | tf_op jit(solution)/shard_map/ppermute | solution.py:402
  68.1 0.8 copy-start.11
  68.9 10.5 %collective-permute-start.9 = (bf16[256,640]{1,0:T(8,128)(2,1)}, bf16[256,640]{1,0:T(8,128)(2,1)}, u32[]{:S(2)}, u32[]{:S(2)}) collective-permute-start(bf16[256,640]{1,0:T(8,128)(2,1)} %get-tuple-element.58), channel_id=1, source_target_pairs={{0,1},{1,0},{2,3},{3,2},{4,5},{5,4},{6,7},{7,6},{8,9},{9,8},{10,11... | collective-permute-start | bytes 983048 | tf_op jit(solution)/shard_map/ppermute | solution.py:402
  76.9 0.9 copy-start.9
  77.7 26.3 %copy-start.4 = (bf16[640,256]{1,0:T(8,128)(2,1)S(1)}, bf16[640,256]{1,0:T(8,128)(2,1)}, u32[]{:S(2)}) copy-start(bf16[640,256]{1,0:T(8,128)(2,1)} %copy-done.3) | copy-start | bytes 983044
  77.7 26.3 %copy-start.6 = (bf16[640,256]{1,0:T(8,128)(2,1)S(1)}, bf16[640,256]{1,0:T(8,128)(2,1)}, u32[]{:S(2)}) copy-start(bf16[640,256]{1,0:T(8,128)(2,1)} %copy-done.5) | copy-start | bytes 983044
  77.7 26.3 %copy-start.8 = (f32[256,1024]{1,0:T(8,128)S(1)}, f32[256,1024]{1,0:T(8,128)}, u32[]{:S(2)}) copy-start(f32[256,1024]{1,0:T(8,128)} %copy-done.7) | copy-start | bytes 3145732
  77.7 8.9 %collective-permute-start.15 = (bf16[128,1280]{1,0:T(8,128)(2,1)}, bf16[128,1280]{1,0:T(8,128)(2,1)}, u32[]{:S(2)}, u32[]{:S(2)}) collective-permute-start(bf16[128,1280]{1,0:T(8,128)(2,1)} %get-tuple-element.69), channel_id=1, source_target_pairs={{0,4},{1,5},{2,6},{3,7},{4,0},{5,1},{6,2},{7,3},{8,12},{9,13},{10,... | collective-permute-start | bytes 983048 | tf_op jit(solution)/shard_map/ppermute | solution.py:402
  79.4 1.1 copy-start.12
  82.4 0.8 copy-start.13
  83.2 11.4 %collective-permute-start.10 = (bf16[128,1280]{1,0:T(8,128)(2,1)}, bf16[128,1280]{1,0:T(8,128)(2,1)S(1)}, u32[]{:S(2)}, u32[]{:S(2)}) collective-permute-start(bf16[128,1280]{1,0:T(8,128)(2,1)} %get-tuple-element.60), channel_id=1, source_target_pairs={{0,4},{1,5},{2,6},{3,7},{4,0},{5,1},{6,2},{7,3},{8,12},{9,13},{10,... | collective-permute-start | bytes 983048 | tf_op jit(solution)/shard_map/ppermute | solution.py:402
  86.6 1.1 copy-start.10
  88.8 10.7 %collective-permute-start.17 = (bf16[64,1280]{1,0:T(8,128)(2,1)S(1)}, bf16[64,1280]{1,0:T(8,128)(2,1)S(1)}, u32[]{:S(2)}, u32[]{:S(2)}) collective-permute-start(bf16[64,1280]{1,0:T(8,128)(2,1)S(1)} %get-tuple-element.72), channel_id=1, source_target_pairs={{0,8},{1,9},{2,10},{3,11},{4,12},{5,13},{6,14},{7,15},{8,0},{9,1},... | collective-permute-start | bytes 491528 | tf_op jit(solution)/shard_map/ppermute | solution.py:402
  94.7 1.1 copy-start.14
  95.8 8.0 %collective-permute-start.16 = (bf16[64,1280]{1,0:T(8,128)(2,1)S(1)}, bf16[64,1280]{1,0:T(8,128)(2,1)S(1)}, u32[]{:S(2)}, u32[]{:S(2)}) collective-permute-start(bf16[64,1280]{1,0:T(8,128)(2,1)S(1)} %get-tuple-element.71), channel_id=1, source_target_pairs={{0,8},{1,9},{2,10},{3,11},{4,12},{5,13},{6,14},{7,15},{8,0},{9,1},... | collective-permute-start | bytes 491528 | tf_op jit(solution)/shard_map/ppermute | solution.py:402
  103.9 20.6 %collective-permute-start.18 = (f32[32,2560]{1,0:T(8,128)S(1)}, f32[32,2560]{1,0:T(8,128)S(1)}, u32[]{:S(2)}, u32[]{:S(2)}) collective-permute-start(f32[32,2560]{1,0:T(8,128)S(1)} %get-tuple-element.74), channel_id=1, source_target_pairs={{0,16},{16,0},{1,17},{17,1},{2,18},{18,2},{3,19},{19,3},{4,20},{20... | collective-permute-start | bytes 983048 | tf_op jit(solution)/shard_map/ppermute | solution.py:393
  104.0 3.9 %copy-start.1 = (bf16[1024,5000]{0,1:T(8,128)(2,1)S(1)}, bf16[1024,5000]{0,1:T(8,128)(2,1)}, u32[]{:S(2)}) copy-start(bf16[1024,5000]{0,1:T(8,128)(2,1)} %param.15) | copy-start | bytes 30720004
  110.1 5.5 %collective-permute-start.21 = (f32[1,3712]{1,0:T(1,128)S(1)}, f32[1,3712]{1,0:T(1,128)S(1)}, u32[]{:S(2)}, u32[]{:S(2)}) collective-permute-start(f32[1,3712]{1,0:T(1,128)S(1)} %shard_map.134.refs_0_), channel_id=1, source_target_pairs={{0,12},{1,13},{2,14},{3,15},{4,8},{5,9},{6,10},{7,11},{8,4},{9,5},... | collective-permute-start | bytes 44552 | tf_op jit(solution)/shard_map/ppermute | solution.py:402
  112.2 4.6 %collective-permute-start.20 = (f32[1,3712]{1,0:T(1,128)S(1)}, f32[1,3712]{1,0:T(1,128)S(1)}, u32[]{:S(2)}, u32[]{:S(2)}) collective-permute-start(f32[1,3712]{1,0:T(1,128)S(1)} %shard_map.134.refs_0_), channel_id=1, source_target_pairs={{0,8},{1,9},{2,10},{3,11},{4,12},{5,13},{6,14},{7,15},{8,0},{9,1},... | collective-permute-start | bytes 44552 | tf_op jit(solution)/shard_map/ppermute | solution.py:402
  112.2 4.6 %collective-permute-start.19 = (f32[1,3712]{1,0:T(1,128)S(1)}, f32[1,3712]{1,0:T(1,128)S(1)}, u32[]{:S(2)}, u32[]{:S(2)}) collective-permute-start(f32[1,3712]{1,0:T(1,128)S(1)} %shard_map.134.refs_0_), channel_id=1, source_target_pairs={{0,4},{1,5},{2,6},{3,7},{4,0},{5,1},{6,2},{7,3},{8,12},{9,13},{10,... | collective-permute-start | bytes 44552 | tf_op jit(solution)/shard_map/ppermute | solution.py:402
  116.9 4.7 %collective-permute-start.24 = (f32[1,3712]{1,0:T(1,128)S(1)}, f32[1,3712]{1,0:T(1,128)S(1)}, u32[]{:S(2)}, u32[]{:S(2)}) collective-permute-start(f32[1,3712]{1,0:T(1,128)S(1)} %shard_map.135.refs_0_), channel_id=1, source_target_pairs={{0,3},{1,2},{2,1},{3,0},{4,7},{5,6},{6,5},{7,4},{8,11},{9,10},{10,... | collective-permute-start | bytes 44552 | tf_op jit(solution)/shard_map/ppermute | solution.py:402
  117.5 4.0 %collective-permute-start.23 = (f32[1,3712]{1,0:T(1,128)S(1)}, f32[1,3712]{1,0:T(1,128)S(1)}, u32[]{:S(2)}, u32[]{:S(2)}) collective-permute-start(f32[1,3712]{1,0:T(1,128)S(1)} %shard_map.135.refs_0_), channel_id=1, source_target_pairs={{0,2},{1,3},{2,0},{3,1},{4,6},{5,7},{6,4},{7,5},{8,10},{9,11},{10,... | collective-permute-start | bytes 44552 | tf_op jit(solution)/shard_map/ppermute | solution.py:402
  118.9 3.7 %collective-permute-start.22 = (f32[1,3712]{1,0:T(1,128)S(1)}, f32[1,3712]{1,0:T(1,128)S(1)}, u32[]{:S(2)}, u32[]{:S(2)}) collective-permute-start(f32[1,3712]{1,0:T(1,128)S(1)} %shard_map.135.refs_0_), channel_id=1, source_target_pairs={{0,1},{1,0},{2,3},{3,2},{4,5},{5,4},{6,7},{7,6},{8,9},{9,8},{10,11... | collective-permute-start | bytes 44552 | tf_op jit(solution)/shard_map/ppermute | solution.py:402
  122.6 1.2 collective-permute-start.25
  124.5 0.7 copy-start.18

commit v4 on v3

--- a/solution.py
+++ b/solution.py
@@ -39,11 +39,13 @@
     return [(index, moved(index)) for index in range(count)]
 
 
-def flips(strides):
-    masks = [0]
-    for stride in strides:
-        masks += [mask | stride for mask in masks]
-    return masks[1:]
+def tile_plan(vocab, cores):
+    groups = -(-vocab // (2 * cores * LANES))
+    sizes = [(groups + turn) // TURNS * LANES for turn in range(TURNS)]
+    starts = [0]
+    for size in sizes * 2:
+        starts.append(starts[-1] + size)
+    return sizes * 2, starts[:-1], starts[-1]
 
 
 def route_slots(dest_device):
@@ -65,18 +67,59 @@
     return jax.ShapeDtypeStruct(dims, dtype)
 
 
-def call(kernel, scalars, arrays, out_shape, grant, scratch=()):
-    in_specs = [pl.BlockSpec(memory_space=pltpu.SMEM)] if scalars is not None else []
-    operands = [scalars] if scalars is not None else []
-    out_specs = jax.tree.map(lambda _: pl.BlockSpec(memory_space=pltpu.VMEM), out_shape)
+class Pulled:
+    def __init__(self, value):
+        self.value = value
+
+
+def call(kernel, scalars, arrays, out_shape, grant, scratch=(), fetched=0):
+    operands, in_specs, pulled = [], [], []
+    if scalars is not None:
+        operands.append(scalars)
+        in_specs.append(pl.BlockSpec(memory_space=pltpu.SMEM))
+    lead = len(operands)
+    for index, array in enumerate(arrays):
+        space = pltpu.VMEM
+        if isinstance(array, Pulled):
+            array, space = array.value, pl.ANY
+            pulled.append(lead + index)
+        elif index < fetched:
+            space = pltpu.HBM
+        operands.append(array)
+        in_specs.append(pl.BlockSpec(memory_space=space))
+    buffers = [pltpu.VMEM(operands[index].shape, operands[index].dtype) for index in pulled]
+    if pulled:
+        buffers.append(pltpu.SemaphoreType.DMA((len(pulled),)))
+
+    def run(*refs):
+        refs = list(refs)
+        if pulled:
+            held, arrived = refs[-len(buffers) : -1], refs[-1]
+            refs = refs[: -len(buffers)]
+            copies = [
+                pltpu.make_async_copy(refs[index], buffer, arrived.at[place])
+                for place, (index, buffer) in enumerate(zip(pulled, held))
+            ]
+            for copy in copies:
+                copy.start()
+            for copy in copies:
+                copy.wait()
+            for index, buffer in zip(pulled, held):
+                refs[index] = buffer
+        kernel(*refs)
+
     return pl.pallas_call(
-        kernel,
-        in_specs=in_specs + [pl.BlockSpec(memory_space=pltpu.VMEM) for _ in arrays],
-        out_specs=out_specs,
+        run,
+        in_specs=in_specs,
+        out_specs=jax.tree.map(lambda _: pl.BlockSpec(memory_space=pltpu.VMEM), out_shape),
         out_shape=out_shape,
-        scratch_shapes=list(scratch),
+        scratch_shapes=list(scratch) + buffers,
         compiler_params=pltpu.CompilerParams(vmem_limit_bytes=grant << 20),
-    )(*operands, *arrays)
+    )(*operands)
+
+
+def in_hbm(value):
+    return pltpu.with_memory_space_constraint(value, pltpu.HBM)
 
 
 def on_core(core, cores, run):
@@ -130,15 +173,39 @@
     on_core(ids_ref[0], cores, run)
 
 
-def select_kernel(
-    cores, chips, plans, ids_ref, place_ref, near_ref, far_ref, gain_ref,
-    normed_ref, scaled_ref, *refs,
+def weight_copies(core, vocab, sizes, starts, half, weight_ref, held_ref, arrived):
+    tiles = []
+    for index, (size, start) in enumerate(zip(sizes, starts)):
+        first = core * half + start
+        count = max(0, min(size, vocab - first))
+        copy = pltpu.make_async_copy(
+            weight_ref.at[pl.ds(first, count), :],
+            held_ref.at[pl.ds(start, count), :],
+            arrived.at[index],
+        )
+        tiles.append((count, copy))
+    return tiles
+
+
+def student_kernel(
+    cores, chips, plans, tiling, ids_ref, weight_ref, place_ref, near_ref, far_ref, gain_ref,
+    bias_ref, mine_ref, other_ref, normed_ref, powers_ref, stats_ref, dots_ref, *refs,
 ):
-    state_refs, turned_ref = refs[:-1], refs[-1]
+    state_refs, (turned_ref, held_ref, arrived) = refs[:-3], refs[-3:]
     rows = place_ref.shape[1]
     count = near_ref.shape[0]
-    width = near_ref.shape[1]
+    vocab, width = weight_ref.shape
     block = width // (cores * chips)
+    sizes, starts, half = tiling
+
+    def copies(core):
+        return weight_copies(core, vocab, sizes, starts, half, weight_ref, held_ref, arrived)
+
+    def fetch(core):
+        for _, copy in copies(core):
+            copy.start()
+
+    on_core(ids_ref[0], cores, fetch)
     ids = lax.broadcasted_iota(jnp.int32, (count, rows), 0)
     place = place_ref[...]
 
@@ -157,15 +224,17 @@
     normed = moved * lax.rsqrt(spread + EPSILON)
     normed_ref[...] = normed
     scaled = normed * gain_ref[...]
-    scaled_ref[...] = scaled.astype(BF16)
     turned_ref[...] = scaled.T
+    scaled = scaled.astype(BF16)
     refs = iter(state_refs)
     for side, ((stride, size), strides) in enumerate(plans):
         for step in range(size):
             to_near = lax.rem(ids_ref[1 + side] + step, size) * stride
             places = [0]
-            for far in strides:
+            for far in strides[1:] if step else strides:
                 places = [at + bit * far for at in places for bit in (0, 1)]
+            if step:
+                to_near = to_near + ids_ref[0] * strides[0]
             groups = []
             for at in places:
                 for core in range(cores):
@@ -173,33 +242,25 @@
                     groups.append(turned_ref[pl.ds(pl.multiple_of(first, block), block), :])
             next(refs)[...] = jnp.concatenate(groups, axis=0).astype(BF16)
 
-
-def forward_kernel(
-    cores, tile, ids_ref, scaled_ref, weight_ref, bias_ref, mine_ref, other_ref,
-    powers_ref, stats_ref, dots_ref,
-):
-    vocab = weight_ref.shape[0]
-    rows = scaled_ref.shape[0]
-
     def run(core):
-        scaled = scaled_ref[...]
         dots = jnp.zeros((1, rows), F32)
-        for index in range(TILES):
-            first = (core * TILES + index) * tile
-            count = max(0, min(tile, vocab - first))
-            at = slice(index * tile, index * tile + count)
+        tiles = copies(core)
+        for _, copy in tiles:
+            copy.wait()
+        for index, (count, _) in enumerate(tiles):
+            first = core * half + starts[index]
+            at = slice(starts[index], starts[index] + count)
             logits = lax.dot_general(
-                weight_ref[first : first + count, :], scaled, CONTRACT_LAST,
-                preferred_element_type=F32,
+                held_ref[at, :], scaled, CONTRACT_LAST, preferred_element_type=F32
             )
             bias = jnp.broadcast_to(bias_ref[:, first : first + count], (LANES, count)).T
             logits = logits + jnp.concatenate([bias] * (rows // LANES), axis=1)
             top = jnp.max(logits, axis=0, keepdims=True)
             powers = jnp.exp(logits - top)
             powers_ref[at, :] = powers
-            if count < tile:
-                powers_ref[index * tile + count : (index + 1) * tile, :] = jnp.zeros(
-                    (tile - count, rows), F32
+            if count < sizes[index]:
+                powers_ref[starts[index] + count : starts[index] + sizes[index], :] = jnp.zeros(
+                    (sizes[index] - count, rows), F32
                 )
             soft = mine_ref[at, :].astype(F32) + other_ref[at, :].astype(F32)
             stats_ref[index : index + 1, :] = top
@@ -213,7 +274,7 @@
 
 
 def grad_kernel(
-    turn, powers_ref, stats_ref, stats_far_ref, mass_ref, mass_far_ref, dots_ref,
+    turn, starts, powers_ref, stats_ref, stats_far_ref, mass_ref, mass_far_ref, dots_ref,
     mine_ref, other_ref, first_ref, second_ref, loss_ref,
 ):
     stats, stats_far = stats_ref[...], stats_far_ref[...]
@@ -226,9 +287,8 @@
     total = jnp.sum(terms, axis=0, keepdims=True)
     mass = mass_ref[...] + mass_far_ref[...]
     scale = shrunk * (mass / total)
-    tile = first_ref.shape[0]
     for index, out_ref in ((turn, first_ref), (turn + TURNS, second_ref)):
-        at = slice(index * tile, (index + 1) * tile)
+        at = slice(starts[index], starts[index] + out_ref.shape[0])
         grad = powers_ref[at, :] * scale[index : index + 1]
         grad = grad - mine_ref[at, :].astype(F32) - other_ref[at, :].astype(F32)
         out_ref[...] = grad.astype(BF16)
@@ -236,23 +296,27 @@
     loss_ref[...] = jnp.broadcast_to(jnp.sum(loss, axis=1, keepdims=True), loss_ref.shape)
 
 
-def back_kernel(cores, tile, ids_ref, weight_ref, normed_ref, loss_ref, live_ref, *refs):
-    grads, out_ref = refs[:TILES], refs[TILES]
+def back_kernel(
+    cores, tiling, ids_ref, weight_ref, normed_ref, loss_ref, live_ref, *refs
+):
+    grads, (out_ref, held_ref, arrived) = refs[:TILES], refs[TILES:]
     vocab, width = weight_ref.shape
     rows = normed_ref.shape[0]
-    half = TILES * tile
+    sizes, starts, half = tiling
     ones = jnp.ones((8, rows), BF16)
 
     def run(core):
+        tiles = weight_copies(core, vocab, sizes, starts, half, weight_ref, held_ref, arrived)
+        for _, copy in tiles:
+            copy.start()
+        for grad_ref, start, size in zip(grads, starts, sizes):
+            sums = lax.dot_general(ones, grad_ref[...], CONTRACT_LAST, preferred_element_type=F32)
+            out_ref[:, start : start + size] = sums[:1]
         total = None
-        for index in range(TILES):
-            first = (core * TILES + index) * tile
-            count = max(0, min(tile, vocab - first))
-            grad = grads[index][...]
-            sums = lax.dot_general(ones, grad, CONTRACT_LAST, preferred_element_type=F32)
-            out_ref[:, index * tile : (index + 1) * tile] = sums[:1]
+        for grad_ref, start, (count, copy) in zip(grads, starts, tiles):
+            copy.wait()
             term = lax.dot_general(
-                grads[index][:count, :], weight_ref[first : first + count, :], CONTRACT_FIRST,
+                grad_ref[:count, :], held_ref[start : start + count, :], CONTRACT_FIRST,
                 preferred_element_type=F32,
             )
             total = term if total is None else total + term
@@ -266,17 +330,21 @@
     )
 
 
-def term_kernel(near, ids_ref, *refs):
-    states, grads, (kept_ref, sent_ref) = refs[:near], refs[near : 2 * near], refs[2 * near :]
+def term_kernel(near, ids_ref, own_ref, *refs):
+    came, grads = refs[: 2 * (near - 1)], refs[2 * (near - 1) : 3 * near - 2]
+    kept_ref, sent_ref, *halves = refs[3 * near - 2 :]
     count = kept_ref.shape[0]
+    for index, half_ref in enumerate(halves):
+        half_ref[ids_ref[1]] = came[2 * index][...]
+        half_ref[1 - ids_ref[1]] = came[2 * index + 1][...]
 
     def product(side):
         rows = pl.ds(pl.multiple_of(side * count, count), count)
         total = None
-        for state, grad in zip(states, grads):
-            term = lax.dot_general(
-                state[rows, :], grad[...], CONTRACT_LAST, preferred_element_type=F32
-            )
+        for state, grad in zip(
+            [own_ref[rows, :]] + [half_ref[side] for half_ref in halves], grads
+        ):
+            term = lax.dot_general(state, grad[...], CONTRACT_LAST, preferred_element_type=F32)
             total = term if total is None else total + term
         return total
 
@@ -285,7 +353,8 @@
 
 
 def halve_kernel(parts, ids_ref, *refs):
-    kept, came, (kept_ref, sent_ref) = refs[:parts], refs[parts : 2 * parts], refs[2 * parts :]
+    came, kept = refs[:parts], refs[parts : 2 * parts]
+    kept_ref, sent_ref = refs[2 * parts :]
     count, width = kept_ref.shape
     width = width // parts
     for index in range(parts):
@@ -302,29 +371,32 @@
 def halve(bit, kept, came):
     count = kept[0].shape[0] // 2
     width = sum(part.shape[1] for part in kept)
-    return call(
+    kept, sent = call(
         functools.partial(halve_kernel, len(kept)),
         bit[None],
-        [*kept, *came],
+        [*map(Pulled, came), *map(Pulled, kept)],
         [shape(count, width), shape(count, width, dtype=BF16)],
-        6,
-    )
-
-
-def split_kernel(tile, ids_ref, *refs):
+        8,
+    )
+    return kept, sent
+
+
+def split_kernel(tiling, ids_ref, *refs):
     kept, came, (mine_ref, sent_ref) = refs[:TURNS], refs[TURNS : 2 * TURNS], refs[2 * TURNS :]
     count = mine_ref.shape[0]
+    sizes, starts, _ = tiling
 
     def total(turn, core):
         rows = pl.ds(pl.multiple_of(core * count, count), count)
         return kept[turn][rows, :] + came[turn][rows, :].astype(F32)
 
     for turn in range(TURNS):
+        size = sizes[turn]
         for out_ref, core in ((mine_ref, ids_ref[0]), (sent_ref, 1 - ids_ref[0])):
             both = total(turn, core)
-            out_ref[:, turn * tile : (turn + 1) * tile] = both[:, :tile]
-            far = (turn + TURNS) * tile
-            out_ref[:, far : far + tile] = both[:, tile:]
+            out_ref[:, starts[turn] : starts[turn] + size] = both[:, :size]
+            far = starts[turn + TURNS]
+            out_ref[:, far : far + size] = both[:, size:]
 
 
 def sum_kernel(*refs):
@@ -334,14 +406,16 @@
     refs[-1][...] = total
 
 
-def small_kernel(cores, half, width, ids_ref, near_ref, far_ref, gain_ref, bias_ref, tail_ref):
+def small_kernel(
+    cores, half, width, ids_ref, near_ref, far_ref, gain_ref, bias_ref, loss_ref, scale_ref
+):
     vocab = bias_ref.shape[1]
     tail, tail_far = near_ref[:, half + width :], far_ref[:, half + width :]
     inverse = 1.0 / tail[:, 1:2]
     near, far = near_ref[:, half : half + width], far_ref[:, half : half + width]
     gain_ref[...] = (near + far) * inverse
-    lane = lax.broadcasted_iota(jnp.int32, tail.shape, 1)
-    tail_ref[...] = jnp.where(lane == 0, (tail + tail_far) * inverse, inverse)
+    loss_ref[...] = (tail + tail_far) * inverse
+    scale_ref[...] = jnp.broadcast_to(inverse, scale_ref.shape)
 
     def run(core):
         low, high = (near_ref, far_ref) if core == 0 else (far_ref, near_ref)
@@ -351,10 +425,10 @@
     on_core(ids_ref[0], cores, run)
 
 
-def finish_kernel(cores, ids_ref, mine_ref, came_ref, tail_ref, out_ref):
+def finish_kernel(cores, ids_ref, mine_ref, came_ref, scale_ref, out_ref):
     half = mine_ref.shape[1]
     vocab = out_ref.shape[1]
-    inverse = tail_ref[:, 1:2]
+    inverse = scale_ref[:, :1]
 
     def run(core):
         low, high = (mine_ref, came_ref) if core == 0 else (came_ref, mine_ref)
@@ -377,8 +451,8 @@
     out_rows = width // devices
     size_a, size_b, size_c = torus_factors(chips)
     bits_a, bits_b, bits_c = bits_of(size_a), bits_of(size_b), bits_of(size_c)
-    tile = -(-vocab // (TILES * cores * LANES)) * LANES
-    half = TILES * tile
+    tiling = tile_plan(vocab, cores)
+    sizes, starts, half = tiling
     core = lax.axis_index("teach").astype(jnp.int32)
     chip = lax.axis_index("dp").astype(jnp.int32)
     ids = core[None]
@@ -431,42 +505,39 @@
     place = (dest_device % chips) * slots + route_slots(dest_device)
     place = jnp.where(dest_device // chips == core, place, place + chips * slots)
     near_ids = [(chip // stride) % size for (stride, size), _ in plans]
-    normed, scaled, *own_states = call(
-        functools.partial(select_kernel, cores, chips, plans),
+    weight = in_hbm(out_weight.T)
+    held = [pltpu.VMEM((half, width), BF16), pltpu.SemaphoreType.DMA((TILES,))]
+    normed, powers, stats, dots, *own_states = call(
+        functools.partial(student_kernel, cores, chips, plans, tiling),
         jnp.stack([core, *near_ids]),
-        [place[None, :], arrived, arrived_far, gain[None, :]],
-        [shape(rows, width), shape(rows, width, dtype=BF16)]
-        + [shape(width // size, rows, dtype=BF16) for (_, size), _ in plans for _ in range(size)],
-        12,
-        [pltpu.VMEM((width, rows), F32)],
-    )
+        [weight, place[None, :], arrived, arrived_far, gain[None, :], out_bias[None, :], mine, other],
+        [shape(rows, width), shape(half, rows), shape(2 * TILES, rows), shape(1, rows)]
+        + [
+            shape(width // size // (2 if step else 1), rows, dtype=BF16)
+            for (_, size), _ in plans
+            for step in range(size)
+        ],
+        24,
+        [pltpu.VMEM((width, rows), F32), *held],
+        fetched=1,
+    )
+    stats_far = swap(stats)
     states = []
     for (stride, size), _ in plans:
-        states.append(
-            [
-                along(piece, stride, size, step) if step else piece
-                for step, piece in enumerate(own_states[:size])
-            ]
-        )
+        group = [own_states[0]]
+        for step in range(1, size):
+            direct = along(own_states[step], stride, size, step)
+            group += [direct, swap(direct)]
+        states.append(group)
         own_states = own_states[size:]
-
-    weight = out_weight.T
-    powers, stats, dots = call(
-        functools.partial(forward_kernel, cores, tile),
-        ids,
-        [scaled, weight, out_bias[None, :], mine, other],
-        [shape(half, rows), shape(2 * TILES, rows), shape(1, rows)],
-        12,
-    )
-    stats_far = swap(stats)
 
     grads = [None] * TILES
     for turn in range(TURNS):
         grads[turn], grads[turn + TURNS], loss = call(
-            functools.partial(grad_kernel, turn),
+            functools.partial(grad_kernel, turn, starts),
             None,
             [powers, stats, stats_far, mass, mass_far, dots, mine, other],
-            [shape(tile, rows, dtype=BF16)] * 2 + [shape(1, LANES)],
+            [shape(sizes[turn], rows, dtype=BF16)] * 2 + [shape(1, LANES)],
             6,
         )
 
@@ -485,15 +556,16 @@
             count = width // size // 2
             part, sent = call(
                 functools.partial(term_kernel, size),
-                bit_of(strides[0])[None],
+                jnp.stack([bit_of(strides[0]), core]),
                 [*states[side], *gathered[turn, side]],
-                [shape(count, tile), shape(count, tile, dtype=BF16)],
-                6,
+                [shape(count, sizes[turn]), shape(count, sizes[turn], dtype=BF16)],
+                8,
+                [pltpu.VMEM((2, count, rows), BF16)] * (size - 1),
             )
             for depth, stride in enumerate(strides[: len(strides) - bits_c]):
                 if depth:
                     part, sent = halve(bit_of(stride), [part], [got])
-                got = flip(sent, stride)
+                got = in_hbm(flip(sent, stride))
             kept.append(part)
             came.append(got)
         for stride in deep:
@@ -502,39 +574,41 @@
         ends += kept + came
 
     small = call(
-        functools.partial(back_kernel, cores, tile),
+        functools.partial(back_kernel, cores, tiling),
         ids,
         [weight, normed, loss, live_rows[None, :], *grads],
         shape(1, half + width + LANES),
-        10,
-    )
-    for strides in (deep, [1 << k for k in range(bits_a + bits_b)]):
-        got = [flip(small, mask) for mask in flips(strides)]
-        small = call(sum_kernel, None, [small, *got], shape(*small.shape), 2)
+        16,
+        held,
+        fetched=1,
+    )
+    for stride in deep + [1 << k for k in range(bits_a + bits_b)]:
+        got = flip(small, stride)
+        small = call(sum_kernel, None, [small, got], shape(*small.shape), 2)
     small_far = swap(small)
-    gain_sum, bias_sum, tail = call(
+    gain_sum, bias_sum, loss_sum, scale = call(
         functools.partial(small_kernel, cores, half, width),
         ids,
         [small, small_far],
-        [shape(1, width), shape(1, vocab), shape(1, LANES)],
+        [shape(1, width), shape(1, vocab), shape(1, LANES), shape(1, LANES)],
         2,
     )
 
     own, sent = call(
-        functools.partial(split_kernel, tile),
+        functools.partial(split_kernel, tiling),
         ids,
-        ends[::2] + ends[1::2],
+        [*map(Pulled, ends[::2]), *map(Pulled, ends[1::2])],
         [shape(out_rows, half)] * 2,
         4,
     )
     weight_grad = call(
         functools.partial(finish_kernel, cores),
         ids,
-        [own, swap(sent), tail],
+        [Pulled(own), Pulled(swap(sent)), scale],
         shape(out_rows, vocab),
         4,
     )
-    return (weight_grad, gain_sum[0], bias_sum[0], tail[0, 0])
+    return (weight_grad, gain_sum[0], bias_sum[0], loss_sum[0, 0])
 
 
 def solution(mesh):

time: 127 us -> 122 us (0.961)
  local copies, waits for them, and re-layouts: 17.7 us -> 8.92 us
  Pallas kernels: 24.7 us -> 32.3 us
  starting transfers between devices: 29.5 us -> 23.8 us
  waiting for transfers between devices: 51.9 us -> 53.7 us
    unnamed x40 -> x36, local copies, waits for them, and re-layouts: 17.7 us -> 8.92 us
    pallas_call x19 -> x20, Pallas kernels: 24.7 us -> 32.3 us  [call(): pl.pallas_call(run, in_specs=in_specs, out_specs=jax.tree.map(lambda _: p...]
    ppermute x14 -> x12, waiting for transfers between devices: 25.3 us -> 32.1 us  [flip(): return lax.ppermute(value, 'dp', [(i, i ^ mask) for i in range(chips)])]
    ppermute x14 -> x12, starting transfers between devices: 14.7 us -> 9.02 us  [flip(): return lax.ppermute(value, 'dp', [(i, i ^ mask) for i in range(chips)])]
    ppermute x6, waiting for transfers between devices: 16.4 us -> 11.1 us  [along(): return lax.ppermute(value, 'dp', rotation(chips, stride, size, step))]
    ppermute x6 -> x8, waiting for transfers between devices: 3.81 us -> 4.15 us  [swap(): return lax.ppermute(value, 'teach', exchange)]
where the time goes in v4:
time: 122 us; the launch traced here: 121 us
  waiting for transfers between devices  53.7 us (44%)
  Pallas kernels  32.3 us (26%)
  starting transfers between devices  23.8 us (20%)
  local copies, waits for them, and re-layouts  8.92 us (7%)
  between operations  1.68 us (1%)
    pallas_call x20, Pallas kernels, call(): pl.pallas_call(run, in_specs=in_specs, out_specs=jax.tree.map(lambda _: p...  32.3 us
    ppermute x12, waiting for transfers between devices, flip(): return lax.ppermute(value, 'dp', [(i, i ^ mask) for i in range(chips)])  32.1 us
    ppermute x6, waiting for transfers between devices, along(): return lax.ppermute(value, 'dp', rotation(chips, stride, size, step))  11.1 us
    ppermute x12, starting transfers between devices, flip(): return lax.ppermute(value, 'dp', [(i, i ^ mask) for i in range(chips)])  9.02 us
    unnamed x36, local copies, waits for them, and re-layouts  8.92 us
    all_to_all x1, starting transfers between devices, body(): lax.all_to_all(student_hidden.reshape(chips, slots, width), 'dp', split_a...  8.48 us
    all_to_all x1, waiting for transfers between devices, body(): lax.all_to_all(student_hidden.reshape(chips, slots, width), 'dp', split_a...  6.3 us
    ppermute x6, starting transfers between devices, along(): return lax.ppermute(value, 'dp', rotation(chips, stride, size, step))  5.67 us
  transfers between devices with their start and end apart: 27, of which 16 were waited for; matrix products, arithmetic and copies ran while one was open for 1% of the time, Pallas kernels for 19%

profile of v4, /device:TPU:0, one launch (start us, length us, event | category | flops | bytes accessed | tf_op | source)
XLA Modules:
  0.0 121.5 jit_solution(7445976776297341426)
XLA Ops:
  0.7 8.5 %all-to-all-start = ((bf16[16,16,1024]{2,1,0:T(8,128)(2,1)}), bf16[16,16,1024]{2,1,0:T(8,128)(2,1)S(1)}, u32[]{:S(2)}, u32[]{:S(2)}) async-start(bf16[16,16,1024]{2,1,0:T(8,128)(2,1)} %bitcast.47), calls=%async_computation | async-start | bytes 1048576 | tf_op jit(solution)/shard_map/all_to_all | solution.py:478
  10.5 1.7 %copy-done = bf16[1,256,5000]{1,2,0:T(8,128)(2,1)S(1)} copy-done((bf16[1,256,5000]{1,2,0:T(8,128)(2,1)S(1)}, bf16[1,256,5000]{1,2,0:T(8,128)(2,1)}, u32[]{:S(2)}) %copy-start) | copy-done | bytes 2560024
  12.9 5.0 %shard_map.120 = (bf16[2560,256]{1,0:T(8,128)(2,1)S(1)}, bf16[2560,256]{1,0:T(8,128)(2,1)}, f32[1,256]{1,0:T(1,128)S(1)}) custom-call(s32[1]{0:T(128)} %bitcast.refs_0_, bf16[5000,256]{1,0:T(8,128)(2,1)S(1)} %bitcast.38, f32[1,256]{1,0:T(1,128)S(1)} %bitcast.43, f32[1,256]{1,0:T(1,128)S(1)} %broadcast_select_fusion.refs_3_, s32[1,256]{1,0:T(1,128)S(1)} %bitcast.44), custom_call_target="tpu_custom_call" | custom-call | tf_op jit(solution)/shard_map/pallas_call | solution.py:111
  17.9 6.3 %all-to-all-done = bf16[16,16,1024]{2,1,0:T(8,128)(2,1)S(1)} async-done(((bf16[16,16,1024]{2,1,0:T(8,128)(2,1)}), bf16[16,16,1024]{2,1,0:T(8,128)(2,1)S(1)}, u32[]{:S(2)}, u32[]{:S(2)}) %all-to-all-start) | async-done | bytes 524320 | tf_op jit(solution)/shard_map/all_to_all | solution.py:478
  24.5 1.8 %collective-permute-done.refs_4_ = bf16[256,1024]{1,0:T(8,128)(2,1)} collective-permute-done((bf16[256,1024]{1,0:T(8,128)(2,1)S(1)}, bf16[256,1024]{1,0:T(8,128)(2,1)}, u32[]{:S(2)}, u32[]{:S(2)}) %collective-permute-start) | collective-permute-done | bytes 524320 | tf_op jit(solution)/shard_map/ppermute | solution.py:467
  26.3 7.0 %shard_map.121 = (f32[256,1024]{1,0:T(8,128)S(1)}, f32[2560,256]{1,0:T(8,128)S(1)}, f32[8,256]{1,0:T(8,128)S(1)}, f32[1,256]{1,0:T(1,128)S(1)}, bf16[512,256]{1,...) custom-call(s32[3]{0:T(128)S(1)} %pad_add_fusion.1.refs_0_, ...), custom_call_target="tpu_custom_call" | custom-call | tf_op jit(solution)/shard_map/pallas_call | solution.py:111
  33.3 1.0 collective-permute-start.8
  34.9 3.8 %collective-permute-done.8.refs_2_ = bf16[256,256]{1,0:T(8,128)(2,1)S(1)} collective-permute-done((bf16[256,256]{1,0:T(8,128)(2,1)S(1)}, bf16[256,256]{1,0:T(8,128)(2,1)S(1)}, u32[]{:S(2)}, u32[]{:S(2)}) %collective-permute-start.8) | collective-permute-done | bytes 131104 | tf_op jit(solution)/shard_map/ppermute | solution.py:473
  39.2 1.2 collective-permute-done.5.refs_4_
  40.9 1.0 collective-permute-start.15
  42.4 1.0 shard_map.122
  43.5 1.0 collective-permute-start.10
  44.5 1.5 %collective-permute-start.6 = (bf16[640,256]{1,0:T(8,128)(2,1)S(1)}, bf16[640,256]{1,0:T(8,128)(2,1)S(1)}, u32[]{:S(2)}, u32[]{:S(2)}) collective-permute-start(bf16[640,256]{1,0:T(8,128)(2,1)S(1)} %get-tuple-element.50.refs_4_.refs_5_), channel_id=1, source_target_pairs={{0,1},{1,0},{2,3},{3,2},{4,5},{5,4},{6,7},{7,6},{8,9},{9,8},{10,11... | collective-permute-start | bytes 983048 | tf_op jit(solution)/shard_map/ppermute | solution.py:473
  46.1 5.3 %collective-permute-done.15.refs_5_ = bf16[640,256]{1,0:T(8,128)(2,1)S(1)} collective-permute-done((bf16[640,256]{1,0:T(8,128)(2,1)S(1)}, bf16[640,256]{1,0:T(8,128)(2,1)S(1)}, u32[]{:S(2)}, u32[]{:S(2)}) %collective-permute-start.15) | collective-permute-done | bytes 327712 | tf_op jit(solution)/shard_map/ppermute | solution.py:473
  51.5 1.7 %shard_map.129 = (f32[256,640]{1,0:T(8,128)S(1)}, bf16[256,640]{1,0:T(8,128)(2,1)}) custom-call(s32[2]{0:T(128)S(1)} %pad_add_fusion.2.refs_0_, bf16[512,256]{1,0:T(8,128)(2,1)S(1)} %get-tuple-element.52.refs_1_, bf16[256,256]{1,0:T(8,128)(2,1)S(1)} %collective-permute-done.8.refs_2_, bf16[256,256]{1,0:T(8,128)(2,1)S(1)} %collective-permute-done.9.refs_3_, ...), custom_call_target="tpu_custom_call" | custom-call | tf_op jit(solution)/shard_map/pallas_call | solution.py:111
  53.8 1.7 %shard_map.128 = (f32[256,640]{1,0:T(8,128)S(1)}, bf16[256,640]{1,0:T(8,128)(2,1)}) custom-call(s32[2]{0:T(128)S(1)} %pad_add_fusion.refs_0_, bf16[512,256]{1,0:T(8,128)(2,1)S(1)} %get-tuple-element.44.refs_1_, bf16[256,256]{1,0:T(8,128)(2,1)S(1)} %collective-permute-done.2.refs_2_, bf16[256,256]{1,0:T(8,128)(2,1)S(1)} %collective-permute-done.3.refs_3_, ...), custom_call_target="tpu_custom_call" | custom-call | tf_op jit(solution)/shard_map/pallas_call | solution.py:111
  55.5 1.0 collective-permute-start.14
  56.5 2.0 %collective-permute-done.10.refs_5_ = bf16[640,256]{1,0:T(8,128)(2,1)S(1)} collective-permute-done((bf16[640,256]{1,0:T(8,128)(2,1)S(1)}, bf16[640,256]{1,0:T(8,128)(2,1)S(1)}, u32[]{:S(2)}, u32[]{:S(2)}) %collective-permute-start.10) | collective-permute-done | bytes 327712 | tf_op jit(solution)/shard_map/ppermute | solution.py:473
  58.5 1.7 %shard_map.124 = (f32[256,640]{1,0:T(8,128)S(1)}, bf16[256,640]{1,0:T(8,128)(2,1)}) custom-call(s32[2]{0:T(128)S(1)} %pad_add_fusion.2.refs_0_, bf16[512,256]{1,0:T(8,128)(2,1)S(1)} %get-tuple-element.52.refs_1_, bf16[256,256]{1,0:T(8,128)(2,1)S(1)} %collective-permute-done.8.refs_2_, bf16[256,256]{1,0:T(8,128)(2,1)S(1)} %collective-permute-done.9.refs_3_, ...), custom_call_target="tpu_custom_call" | custom-call | tf_op jit(solution)/shard_map/pallas_call | solution.py:111
  60.2 1.7 %shard_map.123 = (f32[256,640]{1,0:T(8,128)S(1)}, bf16[256,640]{1,0:T(8,128)(2,1)}) custom-call(s32[2]{0:T(128)S(1)} %pad_add_fusion.refs_0_, bf16[512,256]{1,0:T(8,128)(2,1)S(1)} %get-tuple-element.44.refs_1_, bf16[256,256]{1,0:T(8,128)(2,1)S(1)} %collective-permute-done.2.refs_2_, bf16[256,256]{1,0:T(8,128)(2,1)S(1)} %collective-permute-done.3.refs_3_, ...), custom_call_target="tpu_custom_call" | custom-call | tf_op jit(solution)/shard_map/pallas_call | solution.py:111
  62.0 0.8 copy-done.9
  62.8 1.0 collective-permute-start.7
  63.8 2.7 %collective-permute-done.16.refs_2_ = bf16[256,640]{1,0:T(8,128)(2,1)S(1)} collective-permute-done((bf16[256,640]{1,0:T(8,128)(2,1)}, bf16[256,640]{1,0:T(8,128)(2,1)S(1)}, u32[]{:S(2)}, u32[]{:S(2)}) %collective-permute-start.16) | collective-permute-done | bytes 327712 | tf_op jit(solution)/shard_map/ppermute | solution.py:476
  66.5 0.7 copy-done.16
  67.2 1.9 %shard_map.130 = (f32[128,1280]{1,0:T(8,128)S(1)}, bf16[128,1280]{1,0:T(8,128)(2,1)}) custom-call(s32[1]{0:T(128)} %bitcast.2.refs_0_, bf16[256,640]{1,0:T(8,128)(2,1)} %collective-permute-done.14.refs_1_, bf16[256,640]{1,0:T(8,128)(2,1)} %copy-done.16, f32[256,640]{1,0:T(8,128)S(1)} %get-tuple-element.65.refs_3_, f32[256,640]{1,0:T(8,128)S(1)} %get-tuple-element.66.refs_4_), custom_call_target="tpu_custom_call" | custom-call | tf_op jit(solution)/shard_map/pallas_call | solution.py:111
  69.2 0.8 copy-done.7
  70.0 1.3 %collective-permute-start.17 = (bf16[128,1280]{1,0:T(8,128)(2,1)}, bf16[128,1280]{1,0:T(8,128)(2,1)}, u32[]{:S(2)}, u32[]{:S(2)}) collective-permute-start(bf16[128,1280]{1,0:T(8,128)(2,1)} %get-tuple-element.67), channel_id=1, source_target_pairs={{0,4},{1,5},{2,6},{3,7},{4,0},{5,1},{6,2},{7,3},{8,12},{9,13},{10,... | collective-permute-start | bytes 983048 | tf_op jit(solution)/shard_map/ppermute | solution.py:476
  71.3 1.3 %collective-permute-done.11.refs_2_ = bf16[256,640]{1,0:T(8,128)(2,1)} collective-permute-done((bf16[256,640]{1,0:T(8,128)(2,1)}, bf16[256,640]{1,0:T(8,128)(2,1)}, u32[]{:S(2)}, u32[]{:S(2)}) %collective-permute-start.11) | collective-permute-done | bytes 327712 | tf_op jit(solution)/shard_map/ppermute | solution.py:476
  72.5 1.1 copy-done.10
  73.6 1.9 %shard_map.125 = (f32[128,1280]{1,0:T(8,128)S(1)}, bf16[128,1280]{1,0:T(8,128)(2,1)}) custom-call(s32[1]{0:T(128)} %bitcast.2.refs_0_, bf16[256,640]{1,0:T(8,128)(2,1)} %collective-permute-done.7.refs_1_, bf16[256,640]{1,0:T(8,128)(2,1)} %collective-permute-done.11.refs_2_, f32[256,640]{1,0:T(8,128)S(1)} %copy-done.10, f32[256,640]{1,0:T(8,128)S(1)} %get-tuple-element.57.refs_4_), custom_call_target="tpu_custom_call" | custom-call | tf_op jit(solution)/shard_map/pallas_call | solution.py:111
  75.6 0.8 copy-done.11
  76.4 1.3 %collective-permute-start.12 = (bf16[128,1280]{1,0:T(8,128)(2,1)}, bf16[128,1280]{1,0:T(8,128)(2,1)S(1)}, u32[]{:S(2)}, u32[]{:S(2)}) collective-permute-start(bf16[128,1280]{1,0:T(8,128)(2,1)} %get-tuple-element.58), channel_id=1, source_target_pairs={{0,4},{1,5},{2,6},{3,7},{4,0},{5,1},{6,2},{7,3},{8,12},{9,13},{10,... | collective-permute-start | bytes 983048 | tf_op jit(solution)/shard_map/ppermute | solution.py:476
  78.0 1.1 copy-done.8
  79.1 1.0 shard_map.131
  80.1 1.2 collective-permute-start.19
  81.3 7.1 %collective-permute-done.12.refs_1_ = bf16[128,1280]{1,0:T(8,128)(2,1)S(1)} collective-permute-done((bf16[128,1280]{1,0:T(8,128)(2,1)}, bf16[128,1280]{1,0:T(8,128)(2,1)S(1)}, u32[]{:S(2)}, u32[]{:S(2)}) %collective-permute-start.12) | collective-permute-done | bytes 327712 | tf_op jit(solution)/shard_map/ppermute | solution.py:476
  88.5 1.1 copy-done.12
  89.9 0.7 collective-permute-start.18
  90.7 6.9 %collective-permute-done.18.refs_3_ = bf16[64,1280]{1,0:T(8,128)(2,1)S(1)} collective-permute-done((bf16[64,1280]{1,0:T(8,128)(2,1)S(1)}, bf16[64,1280]{1,0:T(8,128)(2,1)S(1)}, u32[]{:S(2)}, u32[]{:S(2)}) %collective-permute-start.18) | collective-permute-done | bytes 163872 | tf_op jit(solution)/shard_map/ppermute | solution.py:476
  97.5 0.7 shard_map.132
  98.4 4.0 %shard_map.133.refs_0_ = f32[1,3712]{1,0:T(1,128)S(1)} custom-call(s32[1]{0:T(128)} %bitcast.refs_0_, bf16[5000,1024]{1,0:T(8,128)(2,1)} %bitcast.46, f32[256,1024]{1,0:T(8,128)S(1)} %copy-done.6, f32[1,128]{1,0:T(1,128)S(1)} %get-tuple-element.75.refs_3_, f32[1,256]{1,0:T(1,128)S(1)} %fusion.4.refs_4_, bf16[640,256]{1,0:T(8,128)(2,1)S(1)} %copy-done.2, ...), custom_call_target="tpu_custom_call" | custom-call | tf_op jit(solution)/shard_map/pallas_call | solution.py:111
  102.5 3.7 %collective-permute-done.21.refs_1_ = f32[1,3712]{1,0:T(1,128)S(1)} collective-permute-done((f32[1,3712]{1,0:T(1,128)S(1)}, f32[1,3712]{1,0:T(1,128)S(1)}, u32[]{:S(2)}, u32[]{:S(2)}) %collective-permute-start.21) | collective-permute-done | bytes 14880 | tf_op jit(solution)/shard_map/ppermute | solution.py:476
  106.7 4.1 %collective-permute-done.22.refs_1_ = f32[1,3712]{1,0:T(1,128)S(1)} collective-permute-done((f32[1,3712]{1,0:T(1,128)S(1)}, f32[1,3712]{1,0:T(1,128)S(1)}, u32[]{:S(2)}, u32[]{:S(2)}) %collective-permute-start.22) | collective-permute-done | bytes 14880 | tf_op jit(solution)/shard_map/ppermute | solution.py:476
  111.4 3.2 %collective-permute-done.23.refs_1_ = f32[1,3712]{1,0:T(1,128)S(1)} collective-permute-done((f32[1,3712]{1,0:T(1,128)S(1)}, f32[1,3712]{1,0:T(1,128)S(1)}, u32[]{:S(2)}, u32[]{:S(2)}) %collective-permute-start.23) | collective-permute-done | bytes 14880 | tf_op jit(solution)/shard_map/ppermute | solution.py:476
  114.5 0.8 collective-permute-start.24
  115.3 2.9 %collective-permute-done.24.refs_1_ = f32[1,3712]{1,0:T(1,128)S(1)} collective-permute-done((f32[1,3712]{1,0:T(1,128)S(1)}, f32[1,3712]{1,0:T(1,128)S(1)}, u32[]{:S(2)}, u32[]{:S(2)}) %collective-permute-start.24) | collective-permute-done | bytes 14880 | tf_op jit(solution)/shard_map/ppermute | solution.py:476
  118.3 1.2 collective-permute-done.25.refs_2_
  120.1 1.2 shard_map.139
  (70 shorter events, 7.3 us)
Async XLA Ops:
  0.6 23.7 %copy-start.17 = (s32[256,1]{0,1:T(1,128)S(1)}, s32[256,1]{0,1:T(1,128)}, u32[]{:S(2)}) copy-start(s32[256,1]{0,1:T(1,128)} %param.10) | copy-start | bytes 3076
  0.6 25.6 %copy-start.14 = (f32[1024]{0:T(1024)S(1)}, f32[1024]{0:T(1024)}, u32[]{:S(2)}) copy-start(f32[1024]{0:T(1024)} %param.17) | copy-start | bytes 12292
  0.7 25.6 %copy-start.13 = (f32[5000]{0:T(1024)S(1)}, f32[5000]{0:T(1024)}, u32[]{:S(2)}) copy-start(f32[5000]{0:T(1024)} %param.16) | copy-start | bytes 60004
  0.7 23.6 %all-to-all-start = ((bf16[16,16,1024]{2,1,0:T(8,128)(2,1)}), bf16[16,16,1024]{2,1,0:T(8,128)(2,1)S(1)}, u32[]{:S(2)}, u32[]{:S(2)}) async-start(bf16[16,16,1024]{2,1,0:T(8,128)(2,1)} %bitcast.47), calls=%async_computation | async-start | bytes 1048576 | tf_op jit(solution)/shard_map/all_to_all | solution.py:478
  10.5 1.7 %copy-start = (bf16[1,256,5000]{1,2,0:T(8,128)(2,1)S(1)}, bf16[1,256,5000]{1,2,0:T(8,128)(2,1)}, u32[]{:S(2)}) copy-start(bf16[1,256,5000]{1,2,0:T(8,128)(2,1)} %param.9) | copy-start | bytes 7680004
  12.2 0.7 copy-start.15
  17.9 6.5 %collective-permute-start.1 = (bf16[2560,256]{1,0:T(8,128)(2,1)}, bf16[2560,256]{1,0:T(8,128)(2,1)S(1)}, u32[]{:S(2)}, u32[]{:S(2)}) collective-permute-start(bf16[2560,256]{1,0:T(8,128)(2,1)} %get-tuple-element.43), channel_id=1, source_target_pairs={{0,16},{16,0},{1,17},{17,1},{2,18},{18,2},{3,19},{19,3},{4,20},{20... | collective-permute-start | bytes 3932168 | tf_op jit(solution)/shard_map/ppermute | solution.py:467
  24.2 2.0 %collective-permute-start = (bf16[256,1024]{1,0:T(8,128)(2,1)S(1)}, bf16[256,1024]{1,0:T(8,128)(2,1)}, u32[]{:S(2)}, u32[]{:S(2)}) collective-permute-start(bf16[256,1024]{1,0:T(8,128)(2,1)S(1)} %bitcast.39), channel_id=1, source_target_pairs={{0,16},{16,0},{1,17},{17,1},{2,18},{18,2},{3,19},{19,3},{4,20},{20... | collective-permute-start | bytes 1572872 | tf_op jit(solution)/shard_map/ppermute | solution.py:467
  33.2 7.6 %copy-start.5 = (f32[256,1024]{1,0:T(8,128)}, f32[256,1024]{1,0:T(8,128)S(1)}, u32[]{:S(2)}) copy-start(f32[256,1024]{1,0:T(8,128)S(1)} %get-tuple-element.74.refs_2_) | copy-start | bytes 3145732
  33.3 5.4 %collective-permute-start.8 = (bf16[256,256]{1,0:T(8,128)(2,1)S(1)}, bf16[256,256]{1,0:T(8,128)(2,1)S(1)}, u32[]{:S(2)}, u32[]{:S(2)}) collective-permute-start(bf16[256,256]{1,0:T(8,128)(2,1)S(1)} %get-tuple-element.53), channel_id=1, source_target_pairs={{0,2},{1,3},{2,0},{3,1},{4,6},{5,7},{6,4},{7,5},{8,10},{9,11},{10,... | collective-permute-start | bytes 393224 | tf_op jit(solution)/shard_map/ppermute | solution.py:473
  34.3 10.2 %collective-permute-start.2 = (bf16[256,256]{1,0:T(8,128)(2,1)S(1)}, bf16[256,256]{1,0:T(8,128)(2,1)S(1)}, u32[]{:S(2)}, u32[]{:S(2)}) collective-permute-start(bf16[256,256]{1,0:T(8,128)(2,1)S(1)} %get-tuple-element.45), channel_id=1, source_target_pairs={{0,1},{1,0},{2,3},{3,2},{4,5},{5,4},{6,7},{7,6},{8,9},{9,8},{10,11... | collective-permute-start | bytes 393224 | tf_op jit(solution)/shard_map/ppermute | solution.py:473
  38.7 7.3 %collective-permute-start.9 = (bf16[256,256]{1,0:T(8,128)(2,1)S(1)}, bf16[256,256]{1,0:T(8,128)(2,1)S(1)}, u32[]{:S(2)}, u32[]{:S(2)}) collective-permute-start(bf16[256,256]{1,0:T(8,128)(2,1)S(1)} %collective-permute-done.8.refs_2_), channel_id=1, source_target_pairs={{0,16},{16,0},{1,17},{17,1},{2,18},{18,2},{3,19},{19,3},{4,20},{20... | collective-permute-start | bytes 393224 | tf_op jit(solution)/shard_map/ppermute | solution.py:467
  38.7 1.7 %collective-permute-start.4 = (f32[8,256]{1,0:T(8,128)S(1)}, f32[8,256]{1,0:T(8,128)S(1)}, u32[]{:S(2)}, u32[]{:S(2)}) collective-permute-start(f32[8,256]{1,0:T(8,128)S(1)} %get-tuple-element.47.refs_1_), channel_id=1, source_target_pairs={{0,16},{16,0},{1,17},{17,1},{2,18},{18,2},{3,19},{19,3},{4,20},{20... | collective-permute-start | bytes 24584 | tf_op jit(solution)/shard_map/ppermute | solution.py:467
  39.2 1.2 collective-permute-start.5
  40.9 10.6 %collective-permute-start.15 = (bf16[640,256]{1,0:T(8,128)(2,1)S(1)}, bf16[640,256]{1,0:T(8,128)(2,1)S(1)}, u32[]{:S(2)}, u32[]{:S(2)}) collective-permute-start(bf16[640,256]{1,0:T(8,128)(2,1)S(1)} %get-tuple-element.63.refs_4_.refs_8_), channel_id=1, source_target_pairs={{0,2},{1,3},{2,0},{3,1},{4,6},{5,7},{6,4},{7,5},{8,10},{9,11},{10,... | collective-permute-start | bytes 983048 | tf_op jit(solution)/shard_map/ppermute | solution.py:473
  41.9 11.9 %collective-permute-start.13 = (bf16[640,256]{1,0:T(8,128)(2,1)S(1)}, bf16[640,256]{1,0:T(8,128)(2,1)S(1)}, u32[]{:S(2)}, u32[]{:S(2)}) collective-permute-start(bf16[640,256]{1,0:T(8,128)(2,1)S(1)} %get-tuple-element.61.refs_4_.refs_6_), channel_id=1, source_target_pairs={{0,1},{1,0},{2,3},{3,2},{4,5},{5,4},{6,7},{7,6},{8,9},{9,8},{10,11... | collective-permute-start | bytes 983048 | tf_op jit(solution)/shard_map/ppermute | solution.py:473
  43.5 16.8 %copy-start.1 = (bf16[640,256]{1,0:T(8,128)(2,1)}, bf16[640,256]{1,0:T(8,128)(2,1)S(1)}, u32[]{:S(2)}) copy-start(bf16[640,256]{1,0:T(8,128)(2,1)S(1)} %get-tuple-element.50.refs_4_.refs_5_) | copy-start | bytes 983044
  43.5 18.5 %copy-start.3 = (bf16[640,256]{1,0:T(8,128)(2,1)}, bf16[640,256]{1,0:T(8,128)(2,1)S(1)}, u32[]{:S(2)}) copy-start(bf16[640,256]{1,0:T(8,128)(2,1)S(1)} %get-tuple-element.54.refs_4_.refs_7_) | copy-start | bytes 983044
  43.5 15.0 %collective-permute-start.10 = (bf16[640,256]{1,0:T(8,128)(2,1)S(1)}, bf16[640,256]{1,0:T(8,128)(2,1)S(1)}, u32[]{:S(2)}, u32[]{:S(2)}) collective-permute-start(bf16[640,256]{1,0:T(8,128)(2,1)S(1)} %get-tuple-element.54.refs_4_.refs_7_), channel_id=1, source_target_pairs={{0,2},{1,3},{2,0},{3,1},{4,6},{5,7},{6,4},{7,5},{8,10},{9,11},{10,... | collective-permute-start | bytes 983048 | tf_op jit(solution)/shard_map/ppermute | solution.py:473
  44.5 15.7 %collective-permute-start.6 = (bf16[640,256]{1,0:T(8,128)(2,1)S(1)}, bf16[640,256]{1,0:T(8,128)(2,1)S(1)}, u32[]{:S(2)}, u32[]{:S(2)}) collective-permute-start(bf16[640,256]{1,0:T(8,128)(2,1)S(1)} %get-tuple-element.50.refs_4_.refs_5_), channel_id=1, source_target_pairs={{0,1},{1,0},{2,3},{3,2},{4,5},{5,4},{6,7},{7,6},{8,9},{9,8},{10,11... | collective-permute-start | bytes 983048 | tf_op jit(solution)/shard_map/ppermute | solution.py:473
  46.0 7.8 %collective-permute-start.3 = (bf16[256,256]{1,0:T(8,128)(2,1)S(1)}, bf16[256,256]{1,0:T(8,128)(2,1)S(1)}, u32[]{:S(2)}, u32[]{:S(2)}) collective-permute-start(bf16[256,256]{1,0:T(8,128)(2,1)S(1)} %collective-permute-done.2.refs_2_), channel_id=1, source_target_pairs={{0,16},{16,0},{1,17},{17,1},{2,18},{18,2},{3,19},{19,3},{4,20},{20... | collective-permute-start | bytes 393224 | tf_op jit(solution)/shard_map/ppermute | solution.py:467
  53.2 13.3 %collective-permute-start.16 = (bf16[256,640]{1,0:T(8,128)(2,1)}, bf16[256,640]{1,0:T(8,128)(2,1)S(1)}, u32[]{:S(2)}, u32[]{:S(2)}) collective-permute-start(bf16[256,640]{1,0:T(8,128)(2,1)} %get-tuple-element.64), channel_id=1, source_target_pairs={{0,1},{1,0},{2,3},{3,2},{4,5},{5,4},{6,7},{7,6},{8,9},{9,8},{10,11... | collective-permute-start | bytes 983048 | tf_op jit(solution)/shard_map/ppermute | solution.py:476
  55.5 11.0 %collective-permute-start.14 = (bf16[256,640]{1,0:T(8,128)(2,1)}, bf16[256,640]{1,0:T(8,128)(2,1)}, u32[]{:S(2)}, u32[]{:S(2)}) collective-permute-start(bf16[256,640]{1,0:T(8,128)(2,1)} %get-tuple-element.62), channel_id=1, source_target_pairs={{0,2},{1,3},{2,0},{3,1},{4,6},{5,7},{6,4},{7,5},{8,10},{9,11},{10,... | collective-permute-start | bytes 983048 | tf_op jit(solution)/shard_map/ppermute | solution.py:476
  60.2 12.3 %collective-permute-start.11 = (bf16[256,640]{1,0:T(8,128)(2,1)}, bf16[256,640]{1,0:T(8,128)(2,1)}, u32[]{:S(2)}, u32[]{:S(2)}) collective-permute-start(bf16[256,640]{1,0:T(8,128)(2,1)} %get-tuple-element.55), channel_id=1, source_target_pairs={{0,1},{1,0},{2,3},{3,2},{4,5},{5,4},{6,7},{7,6},{8,9},{9,8},{10,11... | collective-permute-start | bytes 983048 | tf_op jit(solution)/shard_map/ppermute | solution.py:476
  62.0 0.8 copy-start.9
  62.8 9.7 %collective-permute-start.7 = (bf16[256,640]{1,0:T(8,128)(2,1)}, bf16[256,640]{1,0:T(8,128)(2,1)}, u32[]{:S(2)}, u32[]{:S(2)}) collective-permute-start(bf16[256,640]{1,0:T(8,128)(2,1)} %get-tuple-element.51), channel_id=1, source_target_pairs={{0,2},{1,3},{2,0},{3,1},{4,6},{5,7},{6,4},{7,5},{8,10},{9,11},{10,... | collective-permute-start | bytes 983048 | tf_op jit(solution)/shard_map/ppermute | solution.py:476
  66.5 0.7 copy-start.16
  69.2 0.8 copy-start.7
  70.0 28.4 %copy-start.2 = (bf16[640,256]{1,0:T(8,128)(2,1)S(1)}, bf16[640,256]{1,0:T(8,128)(2,1)}, u32[]{:S(2)}) copy-start(bf16[640,256]{1,0:T(8,128)(2,1)} %copy-done.1) | copy-start | bytes 983044
  70.0 28.4 %copy-start.4 = (bf16[640,256]{1,0:T(8,128)(2,1)S(1)}, bf16[640,256]{1,0:T(8,128)(2,1)}, u32[]{:S(2)}) copy-start(bf16[640,256]{1,0:T(8,128)(2,1)} %copy-done.3) | copy-start | bytes 983044
  70.0 28.4 %copy-start.6 = (f32[256,1024]{1,0:T(8,128)S(1)}, f32[256,1024]{1,0:T(8,128)}, u32[]{:S(2)}) copy-start(f32[256,1024]{1,0:T(8,128)} %copy-done.5) | copy-start | bytes 3145732
  70.0 8.0 %collective-permute-start.17 = (bf16[128,1280]{1,0:T(8,128)(2,1)}, bf16[128,1280]{1,0:T(8,128)(2,1)}, u32[]{:S(2)}, u32[]{:S(2)}) collective-permute-start(bf16[128,1280]{1,0:T(8,128)(2,1)} %get-tuple-element.67), channel_id=1, source_target_pairs={{0,4},{1,5},{2,6},{3,7},{4,0},{5,1},{6,2},{7,3},{8,12},{9,13},{10,... | collective-permute-start | bytes 983048 | tf_op jit(solution)/shard_map/ppermute | solution.py:476
  72.5 1.1 copy-start.10
  75.6 0.8 copy-start.11
  76.4 12.1 %collective-permute-start.12 = (bf16[128,1280]{1,0:T(8,128)(2,1)}, bf16[128,1280]{1,0:T(8,128)(2,1)S(1)}, u32[]{:S(2)}, u32[]{:S(2)}) collective-permute-start(bf16[128,1280]{1,0:T(8,128)(2,1)} %get-tuple-element.58), channel_id=1, source_target_pairs={{0,4},{1,5},{2,6},{3,7},{4,0},{5,1},{6,2},{7,3},{8,12},{9,13},{10,... | collective-permute-start | bytes 983048 | tf_op jit(solution)/shard_map/ppermute | solution.py:476
  78.0 1.1 copy-start.8
  80.1 10.5 %collective-permute-start.19 = (bf16[64,1280]{1,0:T(8,128)(2,1)S(1)}, bf16[64,1280]{1,0:T(8,128)(2,1)S(1)}, u32[]{:S(2)}, u32[]{:S(2)}) collective-permute-start(bf16[64,1280]{1,0:T(8,128)(2,1)S(1)} %get-tuple-element.71), channel_id=1, source_target_pairs={{0,8},{1,9},{2,10},{3,11},{4,12},{5,13},{6,14},{7,15},{8,0},{9,1},... | collective-permute-start | bytes 491528 | tf_op jit(solution)/shard_map/ppermute | solution.py:476
  88.5 1.1 copy-start.12
  89.9 7.6 %collective-permute-start.18 = (bf16[64,1280]{1,0:T(8,128)(2,1)S(1)}, bf16[64,1280]{1,0:T(8,128)(2,1)S(1)}, u32[]{:S(2)}, u32[]{:S(2)}) collective-permute-start(bf16[64,1280]{1,0:T(8,128)(2,1)S(1)} %get-tuple-element.70), channel_id=1, source_target_pairs={{0,8},{1,9},{2,10},{3,11},{4,12},{5,13},{6,14},{7,15},{8,0},{9,1},... | collective-permute-start | bytes 491528 | tf_op jit(solution)/shard_map/ppermute | solution.py:476
  98.3 21.9 %collective-permute-start.20 = (f32[32,2560]{1,0:T(8,128)S(1)}, f32[32,2560]{1,0:T(8,128)S(1)}, u32[]{:S(2)}, u32[]{:S(2)}) collective-permute-start(f32[32,2560]{1,0:T(8,128)S(1)} %get-tuple-element.73), channel_id=1, source_target_pairs={{0,16},{16,0},{1,17},{17,1},{2,18},{18,2},{3,19},{19,3},{4,20},{20... | collective-permute-start | bytes 983048 | tf_op jit(solution)/shard_map/ppermute | solution.py:467
  102.4 3.8 %collective-permute-start.21 = (f32[1,3712]{1,0:T(1,128)S(1)}, f32[1,3712]{1,0:T(1,128)S(1)}, u32[]{:S(2)}, u32[]{:S(2)}) collective-permute-start(f32[1,3712]{1,0:T(1,128)S(1)} %shard_map.133.refs_0_), channel_id=1, source_target_pairs={{0,4},{1,5},{2,6},{3,7},{4,0},{5,1},{6,2},{7,3},{8,12},{9,13},{10,... | collective-permute-start | bytes 44552 | tf_op jit(solution)/shard_map/ppermute | solution.py:476
  106.2 4.6 %collective-permute-start.22 = (f32[1,3712]{1,0:T(1,128)S(1)}, f32[1,3712]{1,0:T(1,128)S(1)}, u32[]{:S(2)}, u32[]{:S(2)}) collective-permute-start(f32[1,3712]{1,0:T(1,128)S(1)} %shard_map.134.refs_0_), channel_id=1, source_target_pairs={{0,8},{1,9},{2,10},{3,11},{4,12},{5,13},{6,14},{7,15},{8,0},{9,1},... | collective-permute-start | bytes 44552 | tf_op jit(solution)/shard_map/ppermute | solution.py:476
  110.8 3.7 %collective-permute-start.23 = (f32[1,3712]{1,0:T(1,128)S(1)}, f32[1,3712]{1,0:T(1,128)S(1)}, u32[]{:S(2)}, u32[]{:S(2)}) collective-permute-start(f32[1,3712]{1,0:T(1,128)S(1)} %shard_map.135.refs_0_), channel_id=1, source_target_pairs={{0,1},{1,0},{2,3},{3,2},{4,5},{5,4},{6,7},{7,6},{8,9},{9,8},{10,11... | collective-permute-start | bytes 44552 | tf_op jit(solution)/shard_map/ppermute | solution.py:476
  114.5 3.7 %collective-permute-start.24 = (f32[1,3712]{1,0:T(1,128)S(1)}, f32[1,3712]{1,0:T(1,128)S(1)}, u32[]{:S(2)}, u32[]{:S(2)}) collective-permute-start(f32[1,3712]{1,0:T(1,128)S(1)} %shard_map.136.refs_0_), channel_id=1, source_target_pairs={{0,2},{1,3},{2,0},{3,1},{4,6},{5,7},{6,4},{7,5},{8,10},{9,11},{10,... | collective-permute-start | bytes 44552 | tf_op jit(solution)/shard_map/ppermute | solution.py:476
  118.3 1.2 collective-permute-start.25

commit v5 on v4

--- a/solution.py
+++ b/solution.py
@@ -201,11 +201,11 @@
     def copies(core):
         return weight_copies(core, vocab, sizes, starts, half, weight_ref, held_ref, arrived)
 
-    def fetch(core):
-        for _, copy in copies(core):
+    def fetch(tiles, core):
+        for _, copy in copies(core)[tiles]:
             copy.start()
 
-    on_core(ids_ref[0], cores, fetch)
+    on_core(ids_ref[0], cores, functools.partial(fetch, slice(0, 2)))
     ids = lax.broadcasted_iota(jnp.int32, (count, rows), 0)
     place = place_ref[...]
 
@@ -218,6 +218,7 @@
         )
 
     hidden = taken(place == ids, near_ref) + taken(place - count == ids, far_ref)
+    on_core(ids_ref[0], cores, functools.partial(fetch, slice(2, None)))
     centre = jnp.mean(hidden, axis=1, keepdims=True)
     moved = hidden - centre
     spread = jnp.mean(moved * moved, axis=1, keepdims=True)
@@ -245,9 +246,10 @@
     def run(core):
         dots = jnp.zeros((1, rows), F32)
         tiles = copies(core)
-        for _, copy in tiles:
-            copy.wait()
         for index, (count, _) in enumerate(tiles):
+            if index % 2 == 0:
+                for _, copy in tiles[index : index + 2]:
+                    copy.wait()
             first = core * half + starts[index]
             at = slice(starts[index], starts[index] + count)
             logits = lax.dot_general(
@@ -381,22 +383,19 @@
     return kept, sent
 
 
-def split_kernel(tiling, ids_ref, *refs):
-    kept, came, (mine_ref, sent_ref) = refs[:TURNS], refs[TURNS : 2 * TURNS], refs[2 * TURNS :]
-    count = mine_ref.shape[0]
-    sizes, starts, _ = tiling
-
-    def total(turn, core):
-        rows = pl.ds(pl.multiple_of(core * count, count), count)
-        return kept[turn][rows, :] + came[turn][rows, :].astype(F32)
-
-    for turn in range(TURNS):
-        size = sizes[turn]
-        for out_ref, core in ((mine_ref, ids_ref[0]), (sent_ref, 1 - ids_ref[0])):
-            both = total(turn, core)
-            out_ref[:, starts[turn] : starts[turn] + size] = both[:, :size]
-            far = starts[turn + TURNS]
-            out_ref[:, far : far + size] = both[:, size:]
+def quarter_kernel(parts, ids_ref, *refs):
+    came, kept, outs = refs[:parts], refs[parts : 2 * parts], refs[2 * parts :]
+    count, width = outs[0].shape
+    width = width // parts
+    bit, core = ids_ref[0], ids_ref[1]
+    for index in range(parts):
+        at = slice(index * width, (index + 1) * width)
+        for out_ref, chip_side, core_side in zip(
+            outs, (bit, 1 - bit, bit, 1 - bit), (core, core, 1 - core, 1 - core)
+        ):
+            rows = pl.ds(pl.multiple_of((chip_side * 2 + core_side) * count, count), count)
+            total = kept[index][rows, :] + came[index][rows, :].astype(F32)
+            out_ref[:, at] = total.astype(out_ref.dtype)
 
 
 def sum_kernel(*refs):
@@ -425,15 +424,23 @@
     on_core(ids_ref[0], cores, run)
 
 
-def finish_kernel(cores, ids_ref, mine_ref, came_ref, scale_ref, out_ref):
-    half = mine_ref.shape[1]
+def finish_kernel(cores, tiling, ids_ref, scale_ref, *refs):
+    parts, out_ref = refs[:-1], refs[-1]
+    sizes, starts, half = tiling
     vocab = out_ref.shape[1]
     inverse = scale_ref[:, :1]
 
     def run(core):
-        low, high = (mine_ref, came_ref) if core == 0 else (came_ref, mine_ref)
-        out_ref[:, :half] = low[...] * inverse
-        out_ref[:, half:] = high[:, : vocab - half] * inverse
+        for turn in range(TURNS):
+            kept, away, cross, far = parts[4 * turn : 4 * turn + 4]
+            for owner, near_ref, came_ref in ((core, kept, away), (1 - core, cross, far)):
+                total = (near_ref[...] + came_ref[...].astype(F32)) * inverse
+                first = 0
+                for index in (turn, turn + TURNS):
+                    start = owner * half + starts[index]
+                    count = max(0, min(sizes[index], vocab - start))
+                    out_ref[:, start : start + count] = total[:, first : first + count]
+                    first += sizes[index]
 
     on_core(ids_ref[0], cores, run)
 
@@ -568,10 +575,31 @@
                 got = in_hbm(flip(sent, stride))
             kept.append(part)
             came.append(got)
-        for stride in deep:
+        for stride in deep[:-1]:
             part, sent = halve(bit_of(stride), kept, came)
             kept, came = [part], [flip(sent, stride)]
-        ends += kept + came
+        width_here = sum(part.shape[1] for part in kept)
+        part, away, cross, far = call(
+            functools.partial(quarter_kernel, len(kept)),
+            jnp.stack([bit_of(deep[-1]), core]),
+            [*map(Pulled, came), *map(Pulled, kept)],
+            [
+                shape(out_rows, width_here),
+                shape(out_rows, width_here, dtype=BF16),
+                shape(out_rows, width_here),
+                shape(out_rows, width_here, dtype=BF16),
+            ],
+            8,
+        )
+        away = flip(away, deep[-1])
+        pairs = [
+            (c * chips + i, (1 - c) * chips + (i ^ deep[-1]))
+            for c in range(cores)
+            for i in range(chips)
+        ]
+        far = lax.ppermute(far, ("teach", "dp"), pairs)
+        cross = swap(cross)
+        ends += [part, away, cross, far]
 
     small = call(
         functools.partial(back_kernel, cores, tiling),
@@ -594,19 +622,12 @@
         2,
     )
 
-    own, sent = call(
-        functools.partial(split_kernel, tiling),
+    weight_grad = call(
+        functools.partial(finish_kernel, cores, tiling),
         ids,
-        [*map(Pulled, ends[::2]), *map(Pulled, ends[1::2])],
-        [shape(out_rows, half)] * 2,
-        4,
-    )
-    weight_grad = call(
-        functools.partial(finish_kernel, cores),
-        ids,
-        [Pulled(own), Pulled(swap(sent)), scale],
+        [scale, *map(Pulled, ends)],
         shape(out_rows, vocab),
-        4,
+        8,
     )
     return (weight_grad, gain_sum[0], bias_sum[0], loss_sum[0, 0])
 

time: 122 us -> 126 us (1.033)
  starting transfers between devices: 23.8 us -> 31.8 us
  waiting for transfers between devices: 53.7 us -> 46.7 us
  local copies, waits for them, and re-layouts: 8.92 us -> 10.9 us
    ppermute x12, waiting for transfers between devices: 32.1 us -> 18.8 us  [flip(): return lax.ppermute(value, 'dp', [(i, i ^ mask) for i in range(chips)])]
    ppermute x0 -> x2, waiting for transfers between devices: none -> 6.51 us  [body(): far = lax.ppermute(far, ('teach', 'dp'), pairs)]
    ppermute x12, starting transfers between devices: 9.02 us -> 14.9 us  [flip(): return lax.ppermute(value, 'dp', [(i, i ^ mask) for i in range(chips)])]
    ppermute x0 -> x2, starting transfers between devices: none -> 2.11 us  [body(): far = lax.ppermute(far, ('teach', 'dp'), pairs)]
    unnamed x36 -> x40, local copies, waits for them, and re-layouts: 8.92 us -> 10.9 us
    ppermute x8 -> x9, waiting for transfers between devices: 4.15 us -> 2.98 us  [swap(): return lax.ppermute(value, 'teach', exchange)]
    pallas_call x20 -> x19, Pallas kernels: 32.3 us -> 32.9 us  [call(): pl.pallas_call(run, in_specs=in_specs, out_specs=jax.tree.map(lambda _: p...]
  transfers between devices with their start and end apart: 27 -> 30, of which waited for: 16 -> 17; matrix products, arithmetic and copies ran while one was open for 1% -> 1% of each run, Pallas kernels for 19% -> 19%
where the time goes in v5:
time: 126 us; the launch traced here: 125 us
  waiting for transfers between devices  46.7 us (37%)
  Pallas kernels  32.9 us (26%)
  starting transfers between devices  31.8 us (25%)
  local copies, waits for them, and re-layouts  10.9 us (9%)
  between operations  1.68 us (1%)
    pallas_call x19, Pallas kernels, call(): pl.pallas_call(run, in_specs=in_specs, out_specs=jax.tree.map(lambda _: p...  32.9 us
    ppermute x12, waiting for transfers between devices, flip(): return lax.ppermute(value, 'dp', [(i, i ^ mask) for i in range(chips)])  18.8 us
    ppermute x12, starting transfers between devices, flip(): return lax.ppermute(value, 'dp', [(i, i ^ mask) for i in range(chips)])  14.9 us
    ppermute x6, waiting for transfers between devices, along(): return lax.ppermute(value, 'dp', rotation(chips, stride, size, step))  12.1 us
    unnamed x40, local copies, waits for them, and re-layouts  10.9 us
    all_to_all x1, starting transfers between devices, body(): lax.all_to_all(student_hidden.reshape(chips, slots, width), 'dp', split_a...  8.48 us
    ppermute x2, waiting for transfers between devices, body(): far = lax.ppermute(far, ('teach', 'dp'), pairs)  6.51 us
    all_to_all x1, waiting for transfers between devices, body(): lax.all_to_all(student_hidden.reshape(chips, slots, width), 'dp', split_a...  6.32 us
  transfers between devices with their start and end apart: 30, of which 17 were waited for; matrix products, arithmetic and copies ran while one was open for 1% of the time, Pallas kernels for 19%

profile of v5, /device:TPU:0, one launch (start us, length us, event | category | flops | bytes accessed | tf_op | source)
XLA Modules:
  0.0 125.1 jit_solution(5164351641350013858)
XLA Ops:
  0.7 8.5 %all-to-all-start = ((bf16[16,16,1024]{2,1,0:T(8,128)(2,1)}), bf16[16,16,1024]{2,1,0:T(8,128)(2,1)S(1)}, u32[]{:S(2)}, u32[]{:S(2)}) async-start(bf16[16,16,1024]{2,1,0:T(8,128)(2,1)} %bitcast.47), calls=%async_computation | async-start | bytes 1048576 | tf_op jit(solution)/shard_map/all_to_all | solution.py:485
  10.5 1.7 %copy-done = bf16[1,256,5000]{1,2,0:T(8,128)(2,1)S(1)} copy-done((bf16[1,256,5000]{1,2,0:T(8,128)(2,1)S(1)}, bf16[1,256,5000]{1,2,0:T(8,128)(2,1)}, u32[]{:S(2)}) %copy-start) | copy-done | bytes 2560024
  12.9 5.0 %shard_map.120 = (bf16[2560,256]{1,0:T(8,128)(2,1)S(1)}, bf16[2560,256]{1,0:T(8,128)(2,1)}, f32[1,256]{1,0:T(1,128)S(1)}) custom-call(s32[1]{0:T(128)} %bitcast.refs_0_, bf16[5000,256]{1,0:T(8,128)(2,1)S(1)} %bitcast.38, f32[1,256]{1,0:T(1,128)S(1)} %bitcast.43, f32[1,256]{1,0:T(1,128)S(1)} %broadcast_select_fusion.refs_3_, s32[1,256]{1,0:T(1,128)S(1)} %bitcast.44), custom_call_target="tpu_custom_call" | custom-call | tf_op jit(solution)/shard_map/pallas_call | solution.py:111
  17.9 6.3 %all-to-all-done = bf16[16,16,1024]{2,1,0:T(8,128)(2,1)S(1)} async-done(((bf16[16,16,1024]{2,1,0:T(8,128)(2,1)}), bf16[16,16,1024]{2,1,0:T(8,128)(2,1)S(1)}, u32[]{:S(2)}, u32[]{:S(2)}) %all-to-all-start) | async-done | bytes 524320 | tf_op jit(solution)/shard_map/all_to_all | solution.py:485
  24.5 1.8 %collective-permute-done.refs_4_ = bf16[256,1024]{1,0:T(8,128)(2,1)} collective-permute-done((bf16[256,1024]{1,0:T(8,128)(2,1)S(1)}, bf16[256,1024]{1,0:T(8,128)(2,1)}, u32[]{:S(2)}, u32[]{:S(2)}) %collective-permute-start) | collective-permute-done | bytes 524320 | tf_op jit(solution)/shard_map/ppermute | solution.py:474
  26.3 6.4 %shard_map.121 = (f32[256,1024]{1,0:T(8,128)S(1)}, f32[2560,256]{1,0:T(8,128)S(1)}, f32[8,256]{1,0:T(8,128)S(1)}, f32[1,256]{1,0:T(1,128)S(1)}, bf16[512,256]{1,...) custom-call(s32[3]{0:T(128)S(1)} %pad_add_fusion.refs_0_, ...), custom_call_target="tpu_custom_call" | custom-call | tf_op jit(solution)/shard_map/pallas_call | solution.py:111
  33.3 1.0 collective-permute-start.13
  34.3 4.0 %collective-permute-done.9.refs_2_ = bf16[256,256]{1,0:T(8,128)(2,1)S(1)} collective-permute-done((bf16[256,256]{1,0:T(8,128)(2,1)S(1)}, bf16[256,256]{1,0:T(8,128)(2,1)S(1)}, u32[]{:S(2)}, u32[]{:S(2)}) %collective-permute-start.9) | collective-permute-done | bytes 131104 | tf_op jit(solution)/shard_map/ppermute | solution.py:480
  38.8 1.2 collective-permute-done.3.refs_4_
  40.0 1.0 shard_map.123
  41.6 1.0 collective-permute-start.15
  43.1 1.5 %collective-permute-start.21 = (bf16[640,256]{1,0:T(8,128)(2,1)S(1)}, bf16[640,256]{1,0:T(8,128)(2,1)S(1)}, u32[]{:S(2)}, u32[]{:S(2)}) collective-permute-start(bf16[640,256]{1,0:T(8,128)(2,1)S(1)} %get-tuple-element.53.refs_6_.refs_4_), channel_id=1, source_target_pairs={{0,1},{1,0},{2,3},{3,2},{4,5},{5,4},{6,7},{7,6},{8,9},{9,8},{10,11... | collective-permute-start | bytes 983048 | tf_op jit(solution)/shard_map/ppermute | solution.py:480
  44.6 1.1 collective-permute-start.23
  45.8 5.8 %collective-permute-done.11.refs_5_ = bf16[640,256]{1,0:T(8,128)(2,1)S(1)} collective-permute-done((bf16[640,256]{1,0:T(8,128)(2,1)S(1)}, bf16[640,256]{1,0:T(8,128)(2,1)S(1)}, u32[]{:S(2)}, u32[]{:S(2)}) %collective-permute-start.11) | collective-permute-done | bytes 327712 | tf_op jit(solution)/shard_map/ppermute | solution.py:480
  51.6 1.1 shard_map.130
  52.8 1.0 collective-permute-start.12
  53.8 1.1 shard_map.131
  56.4 2.3 %collective-permute-done.21.refs_5_ = bf16[640,256]{1,0:T(8,128)(2,1)S(1)} collective-permute-done((bf16[640,256]{1,0:T(8,128)(2,1)S(1)}, bf16[640,256]{1,0:T(8,128)(2,1)S(1)}, u32[]{:S(2)}, u32[]{:S(2)}) %collective-permute-start.21) | collective-permute-done | bytes 327712 | tf_op jit(solution)/shard_map/ppermute | solution.py:480
  58.6 1.8 %shard_map.134 = (f32[256,640]{1,0:T(8,128)S(1)}, bf16[256,640]{1,0:T(8,128)(2,1)}) custom-call(s32[2]{0:T(128)S(1)} %pad_add_fusion.2.refs_0_, bf16[512,256]{1,0:T(8,128)(2,1)S(1)} %get-tuple-element.57.refs_1_, bf16[256,256]{1,0:T(8,128)(2,1)S(1)} %collective-permute-done.9.refs_2_, bf16[256,256]{1,0:T(8,128)(2,1)S(1)} %collective-permute-done.10.refs_3_, ...), custom_call_target="tpu_custom_call" | custom-call | tf_op jit(solution)/shard_map/pallas_call | solution.py:111
  61.2 1.0 collective-permute-start.22
  62.2 1.8 %shard_map.135 = (f32[256,640]{1,0:T(8,128)S(1)}, bf16[256,640]{1,0:T(8,128)(2,1)}) custom-call(s32[2]{0:T(128)S(1)} %pad_add_fusion.3.refs_0_, bf16[512,256]{1,0:T(8,128)(2,1)S(1)} %get-tuple-element.60.refs_1_, bf16[256,256]{1,0:T(8,128)(2,1)S(1)} %collective-permute-done.13.refs_2_, bf16[256,256]{1,0:T(8,128)(2,1)S(1)} %collective-permute-done.14.refs_3_, ...), custom_call_target="tpu_custom_call" | custom-call | tf_op jit(solution)/shard_map/pallas_call | solution.py:111
  67.0 1.1 copy-done.12
  68.1 2.0 %shard_map.132 = (f32[128,1280]{1,0:T(8,128)S(1)}, bf16[128,1280]{1,0:T(8,128)(2,1)}) custom-call(s32[1]{0:T(128)} %bitcast.17.refs_0_, bf16[256,640]{1,0:T(8,128)(2,1)} %copy-done.18, bf16[256,640]{1,0:T(8,128)(2,1)} %collective-permute-done.16.refs_2_, f32[256,640]{1,0:T(8,128)S(1)} %get-tuple-element.63.refs_3_, f32[256,640]{1,0:T(8,128)S(1)} %copy-done.12), custom_call_target="tpu_custom_call" | custom-call | tf_op jit(solution)/shard_map/pallas_call | solution.py:111
  70.9 1.3 %collective-permute-start.17 = (bf16[128,1280]{1,0:T(8,128)(2,1)}, bf16[128,1280]{1,0:T(8,128)(2,1)}, u32[]{:S(2)}, u32[]{:S(2)}) collective-permute-start(bf16[128,1280]{1,0:T(8,128)(2,1)} %get-tuple-element.65), channel_id=1, source_target_pairs={{0,4},{1,5},{2,6},{3,7},{4,0},{5,1},{6,2},{7,3},{8,12},{9,13},{10,... | collective-permute-start | bytes 983048 | tf_op jit(solution)/shard_map/ppermute | solution.py:483
  73.0 1.1 copy-done.8
  74.0 1.1 copy-done.14
  75.1 1.9 %shard_map.136 = (f32[128,1280]{1,0:T(8,128)S(1)}, bf16[128,1280]{1,0:T(8,128)(2,1)}) custom-call(s32[1]{0:T(128)} %bitcast.17.refs_0_, bf16[256,640]{1,0:T(8,128)(2,1)} %collective-permute-done.22.refs_1_, bf16[256,640]{1,0:T(8,128)(2,1)} %collective-permute-done.24.refs_2_, f32[256,640]{1,0:T(8,128)S(1)} %copy-done.8, f32[256,640]{1,0:T(8,128)S(1)} %copy-done.14), custom_call_target="tpu_custom_call" | custom-call | tf_op jit(solution)/shard_map/pallas_call | solution.py:111
  77.1 1.3 %collective-permute-start.25 = (bf16[128,1280]{1,0:T(8,128)(2,1)}, bf16[128,1280]{1,0:T(8,128)(2,1)}, u32[]{:S(2)}, u32[]{:S(2)}) collective-permute-start(bf16[128,1280]{1,0:T(8,128)(2,1)} %get-tuple-element.75), channel_id=1, source_target_pairs={{0,4},{1,5},{2,6},{3,7},{4,0},{5,1},{6,2},{7,3},{8,12},{9,13},{10,... | collective-permute-start | bytes 983048 | tf_op jit(solution)/shard_map/ppermute | solution.py:483
  78.5 1.0 collective-permute-done.17.refs_1_
  79.5 1.1 copy-done.10
  80.5 1.6 %shard_map.133 = (f32[32,1280]{1,0:T(8,128)S(1)}, bf16[32,1280]{1,0:T(8,128)(2,1)S(1)}, f32[32,1280]{1,0:T(8,128)S(1)}, bf16[32,1280]{1,0:T(8,128)(2,1)S(1)}) custom-call(s32[2]{0:T(128)S(1)} %pad_add_fusion.1.refs_0_, bf16[128,1280]{1,0:T(8,128)(2,1)} %collective-permute-done.17.refs_1_, f32[128,1280]{1,0:T(8,128)S(1)} %copy-done.10), custom_call_target="tpu_custom_call" | custom-call | tf_op jit(solution)/shard_map/pallas_call | solution.py:111
  82.1 1.5 %collective-permute-start.18 = (bf16[32,1280]{1,0:T(8,128)(2,1)S(1)}, bf16[32,1280]{1,0:T(8,128)(2,1)S(1)}, u32[]{:S(2)}, u32[]{:S(2)}) collective-permute-start(bf16[32,1280]{1,0:T(8,128)(2,1)S(1)} %get-tuple-element.68), channel_id=1, source_target_pairs={{0,8},{1,9},{2,10},{3,11},{4,12},{5,13},{6,14},{7,15},{8,0},{9,1},... | collective-permute-start | bytes 245768 | tf_op jit(solution)/shard_map/ppermute | solution.py:483
  83.7 3.2 %collective-permute-done.25.refs_1_ = bf16[128,1280]{1,0:T(8,128)(2,1)} collective-permute-done((bf16[128,1280]{1,0:T(8,128)(2,1)}, bf16[128,1280]{1,0:T(8,128)(2,1)}, u32[]{:S(2)}, u32[]{:S(2)}) %collective-permute-start.25) | collective-permute-done | bytes 327712 | tf_op jit(solution)/shard_map/ppermute | solution.py:483
  86.9 1.6 %shard_map.137 = (f32[32,1280]{1,0:T(8,128)S(1)}, bf16[32,1280]{1,0:T(8,128)(2,1)S(1)}, f32[32,1280]{1,0:T(8,128)S(1)}, bf16[32,1280]{1,0:T(8,128)(2,1)S(1)}) custom-call(s32[2]{0:T(128)S(1)} %pad_add_fusion.1.refs_0_, bf16[128,1280]{1,0:T(8,128)(2,1)} %collective-permute-done.25.refs_1_, f32[128,1280]{1,0:T(8,128)S(1)} %get-tuple-element.76.refs_2_), custom_call_target="tpu_custom_call" | custom-call | tf_op jit(solution)/shard_map/pallas_call | solution.py:111
  88.6 4.0 %shard_map.124.refs_0_ = f32[1,3712]{1,0:T(1,128)S(1)} custom-call(s32[1]{0:T(128)} %bitcast.refs_0_, bf16[5000,1024]{1,0:T(8,128)(2,1)} %bitcast.46, f32[256,1024]{1,0:T(8,128)S(1)} %copy-done.6, f32[1,128]{1,0:T(1,128)S(1)} %get-tuple-element.51.refs_3_, f32[1,256]{1,0:T(1,128)S(1)} %fusion.4.refs_4_, ...), custom_call_target="tpu_custom_call" | custom-call | tf_op jit(solution)/shard_map/pallas_call | solution.py:111
  92.6 1.3 %collective-permute-start.4 = (f32[1,3712]{1,0:T(1,128)S(1)}, f32[1,3712]{1,0:T(1,128)S(1)}, u32[]{:S(2)}, u32[]{:S(2)}) collective-permute-start(f32[1,3712]{1,0:T(1,128)S(1)} %shard_map.124.refs_0_), channel_id=1, source_target_pairs={{0,4},{1,5},{2,6},{3,7},{4,0},{5,1},{6,2},{7,3},{8,12},{9,13},{10,... | collective-permute-start | bytes 44552 | tf_op jit(solution)/shard_map/ppermute | solution.py:483
  94.0 2.5 %collective-permute-done.4.refs_1_ = f32[1,3712]{1,0:T(1,128)S(1)} collective-permute-done((f32[1,3712]{1,0:T(1,128)S(1)}, f32[1,3712]{1,0:T(1,128)S(1)}, u32[]{:S(2)}, u32[]{:S(2)}) %collective-permute-start.4) | collective-permute-done | bytes 14880 | tf_op jit(solution)/shard_map/ppermute | solution.py:483
  96.4 1.5 %collective-permute-start.5 = (f32[1,3712]{1,0:T(1,128)S(1)}, f32[1,3712]{1,0:T(1,128)S(1)}, u32[]{:S(2)}, u32[]{:S(2)}) collective-permute-start(f32[1,3712]{1,0:T(1,128)S(1)} %shard_map.125.refs_0_), channel_id=1, source_target_pairs={{0,8},{1,9},{2,10},{3,11},{4,12},{5,13},{6,14},{7,15},{8,0},{9,1},... | collective-permute-start | bytes 44552 | tf_op jit(solution)/shard_map/ppermute | solution.py:483
  97.9 3.1 %collective-permute-done.5.refs_1_ = f32[1,3712]{1,0:T(1,128)S(1)} collective-permute-done((f32[1,3712]{1,0:T(1,128)S(1)}, f32[1,3712]{1,0:T(1,128)S(1)}, u32[]{:S(2)}, u32[]{:S(2)}) %collective-permute-start.5) | collective-permute-done | bytes 14880 | tf_op jit(solution)/shard_map/ppermute | solution.py:483
  101.0 2.2 %collective-permute-start.6 = (f32[1,3712]{1,0:T(1,128)S(1)}, f32[1,3712]{1,0:T(1,128)S(1)}, u32[]{:S(2)}, u32[]{:S(2)}) collective-permute-start(f32[1,3712]{1,0:T(1,128)S(1)} %shard_map.126.refs_0_), channel_id=1, source_target_pairs={{0,1},{1,0},{2,3},{3,2},{4,5},{5,4},{6,7},{7,6},{8,9},{9,8},{10,11... | collective-permute-start | bytes 44552 | tf_op jit(solution)/shard_map/ppermute | solution.py:483
  103.3 1.7 %collective-permute-done.6.refs_1_ = f32[1,3712]{1,0:T(1,128)S(1)} collective-permute-done((f32[1,3712]{1,0:T(1,128)S(1)}, f32[1,3712]{1,0:T(1,128)S(1)}, u32[]{:S(2)}, u32[]{:S(2)}) %collective-permute-start.6) | collective-permute-done | bytes 14880 | tf_op jit(solution)/shard_map/ppermute | solution.py:483
  105.0 0.9 collective-permute-start.7
  105.9 2.8 %collective-permute-done.7.refs_1_ = f32[1,3712]{1,0:T(1,128)S(1)} collective-permute-done((f32[1,3712]{1,0:T(1,128)S(1)}, f32[1,3712]{1,0:T(1,128)S(1)}, u32[]{:S(2)}, u32[]{:S(2)}) %collective-permute-start.7) | collective-permute-done | bytes 14880 | tf_op jit(solution)/shard_map/ppermute | solution.py:483
  108.7 1.4 %collective-permute-start.20 = (bf16[32,1280]{1,0:T(8,128)(2,1)S(1)}, bf16[32,1280]{1,0:T(8,128)(2,1)S(1)}, u32[]{:S(2)}, u32[]{:S(2)}) collective-permute-start(bf16[32,1280]{1,0:T(8,128)(2,1)S(1)} %get-tuple-element.70), channel_id=1, source_target_pairs={{0,24},{1,25},{2,26},{3,27},{4,28},{5,29},{6,30},{7,31},{8,16},{9,... | collective-permute-start | bytes 245768 | tf_op jit(solution)/shard_map/ppermute | solution.py:600
  110.1 1.6 %collective-permute-start.26 = (bf16[32,1280]{1,0:T(8,128)(2,1)S(1)}, bf16[32,1280]{1,0:T(8,128)(2,1)S(1)}, u32[]{:S(2)}, u32[]{:S(2)}) collective-permute-start(bf16[32,1280]{1,0:T(8,128)(2,1)S(1)} %get-tuple-element.78), channel_id=1, source_target_pairs={{0,8},{1,9},{2,10},{3,11},{4,12},{5,13},{6,14},{7,15},{8,0},{9,1},... | collective-permute-start | bytes 245768 | tf_op jit(solution)/shard_map/ppermute | solution.py:483
  113.1 5.9 %collective-permute-done.20.refs_5_ = bf16[32,1280]{1,0:T(8,128)(2,1)S(1)} collective-permute-done((bf16[32,1280]{1,0:T(8,128)(2,1)S(1)}, bf16[32,1280]{1,0:T(8,128)(2,1)S(1)}, u32[]{:S(2)}, u32[]{:S(2)}) %collective-permute-start.20) | collective-permute-done | bytes 81952 | tf_op jit(solution)/shard_map/ppermute | solution.py:600
  119.1 2.9 %collective-permute-done.26.refs_7_ = bf16[32,1280]{1,0:T(8,128)(2,1)S(1)} collective-permute-done((bf16[32,1280]{1,0:T(8,128)(2,1)S(1)}, bf16[32,1280]{1,0:T(8,128)(2,1)S(1)}, u32[]{:S(2)}, u32[]{:S(2)}) %collective-permute-start.26) | collective-permute-done | bytes 81952 | tf_op jit(solution)/shard_map/ppermute | solution.py:483
  122.6 2.3 %shard_map.138 = f32[32,5000]{1,0:T(8,128)} custom-call(s32[1]{0:T(128)} %bitcast.refs_0_, f32[1,128]{1,0:T(1,128)S(1)} %get-tuple-element.56.refs_1_, f32[32,1280]{1,0:T(8,128)S(1)} %get-tuple-element.67.refs_2_, bf16[32,1280]{1,0:T(8,128)(2,1)S(1)} %collective-permute-done.18.refs_3_, f32[32,1280]{1,0:T(8,128)S(1)} %collective-permute-done.19.refs_4_, ...), custom_call_target="tpu_custom_call" | custom-call | tf_op jit(solution)/shard_map/pallas_call | solution.py:111
  (80 shorter events, 13.0 us)
Async XLA Ops:
  0.6 23.7 %copy-start.19 = (s32[256,1]{0,1:T(1,128)S(1)}, s32[256,1]{0,1:T(1,128)}, u32[]{:S(2)}) copy-start(s32[256,1]{0,1:T(1,128)} %param.10) | copy-start | bytes 3076
  0.6 25.6 %copy-start.16 = (f32[1024]{0:T(1024)S(1)}, f32[1024]{0:T(1024)}, u32[]{:S(2)}) copy-start(f32[1024]{0:T(1024)} %param.17) | copy-start | bytes 12292
  0.7 25.6 %copy-start.15 = (f32[5000]{0:T(1024)S(1)}, f32[5000]{0:T(1024)}, u32[]{:S(2)}) copy-start(f32[5000]{0:T(1024)} %param.16) | copy-start | bytes 60004
  0.7 23.6 %all-to-all-start = ((bf16[16,16,1024]{2,1,0:T(8,128)(2,1)}), bf16[16,16,1024]{2,1,0:T(8,128)(2,1)S(1)}, u32[]{:S(2)}, u32[]{:S(2)}) async-start(bf16[16,16,1024]{2,1,0:T(8,128)(2,1)} %bitcast.47), calls=%async_computation | async-start | bytes 1048576 | tf_op jit(solution)/shard_map/all_to_all | solution.py:485
  10.5 1.7 %copy-start = (bf16[1,256,5000]{1,2,0:T(8,128)(2,1)S(1)}, bf16[1,256,5000]{1,2,0:T(8,128)(2,1)}, u32[]{:S(2)}) copy-start(bf16[1,256,5000]{1,2,0:T(8,128)(2,1)} %param.9) | copy-start | bytes 7680004
  17.9 6.6 %collective-permute-start.1 = (bf16[2560,256]{1,0:T(8,128)(2,1)}, bf16[2560,256]{1,0:T(8,128)(2,1)S(1)}, u32[]{:S(2)}, u32[]{:S(2)}) collective-permute-start(bf16[2560,256]{1,0:T(8,128)(2,1)} %get-tuple-element.45), channel_id=1, source_target_pairs={{0,16},{16,0},{1,17},{17,1},{2,18},{18,2},{3,19},{19,3},{4,20},{20... | collective-permute-start | bytes 3932168 | tf_op jit(solution)/shard_map/ppermute | solution.py:474
  24.2 2.0 %collective-permute-start = (bf16[256,1024]{1,0:T(8,128)(2,1)S(1)}, bf16[256,1024]{1,0:T(8,128)(2,1)}, u32[]{:S(2)}, u32[]{:S(2)}) collective-permute-start(bf16[256,1024]{1,0:T(8,128)(2,1)S(1)} %bitcast.39), channel_id=1, source_target_pairs={{0,16},{16,0},{1,17},{17,1},{2,18},{18,2},{3,19},{19,3},{4,20},{20... | collective-permute-start | bytes 1572872 | tf_op jit(solution)/shard_map/ppermute | solution.py:474
  32.7 8.4 %copy-start.5 = (f32[256,1024]{1,0:T(8,128)}, f32[256,1024]{1,0:T(8,128)S(1)}, u32[]{:S(2)}) copy-start(f32[256,1024]{1,0:T(8,128)S(1)} %get-tuple-element.46.refs_2_) | copy-start | bytes 3145732
  32.7 5.6 %collective-permute-start.9 = (bf16[256,256]{1,0:T(8,128)(2,1)S(1)}, bf16[256,256]{1,0:T(8,128)(2,1)S(1)}, u32[]{:S(2)}, u32[]{:S(2)}) collective-permute-start(bf16[256,256]{1,0:T(8,128)(2,1)S(1)} %get-tuple-element.58), channel_id=1, source_target_pairs={{0,1},{1,0},{2,3},{3,2},{4,5},{5,4},{6,7},{7,6},{8,9},{9,8},{10,11... | collective-permute-start | bytes 393224 | tf_op jit(solution)/shard_map/ppermute | solution.py:480
  33.3 11.3 %collective-permute-start.13 = (bf16[256,256]{1,0:T(8,128)(2,1)S(1)}, bf16[256,256]{1,0:T(8,128)(2,1)S(1)}, u32[]{:S(2)}, u32[]{:S(2)}) collective-permute-start(bf16[256,256]{1,0:T(8,128)(2,1)S(1)} %get-tuple-element.61), channel_id=1, source_target_pairs={{0,2},{1,3},{2,0},{3,1},{4,6},{5,7},{6,4},{7,5},{8,10},{9,11},{10,... | collective-permute-start | bytes 393224 | tf_op jit(solution)/shard_map/ppermute | solution.py:480
  38.3 7.3 %collective-permute-start.10 = (bf16[256,256]{1,0:T(8,128)(2,1)S(1)}, bf16[256,256]{1,0:T(8,128)(2,1)S(1)}, u32[]{:S(2)}, u32[]{:S(2)}) collective-permute-start(bf16[256,256]{1,0:T(8,128)(2,1)S(1)} %collective-permute-done.9.refs_2_), channel_id=1, source_target_pairs={{0,16},{16,0},{1,17},{17,1},{2,18},{18,2},{3,19},{19,3},{4,20},{20... | collective-permute-start | bytes 393224 | tf_op jit(solution)/shard_map/ppermute | solution.py:474
  38.3 1.7 %collective-permute-start.2 = (f32[8,256]{1,0:T(8,128)S(1)}, f32[8,256]{1,0:T(8,128)S(1)}, u32[]{:S(2)}, u32[]{:S(2)}) collective-permute-start(f32[8,256]{1,0:T(8,128)S(1)} %get-tuple-element.48.refs_1_), channel_id=1, source_target_pairs={{0,16},{16,0},{1,17},{17,1},{2,18},{18,2},{3,19},{19,3},{4,20},{20... | collective-permute-start | bytes 24584 | tf_op jit(solution)/shard_map/ppermute | solution.py:474
  38.8 1.2 collective-permute-start.3
  41.0 10.6 %collective-permute-start.11 = (bf16[640,256]{1,0:T(8,128)(2,1)S(1)}, bf16[640,256]{1,0:T(8,128)(2,1)S(1)}, u32[]{:S(2)}, u32[]{:S(2)}) collective-permute-start(bf16[640,256]{1,0:T(8,128)(2,1)S(1)} %get-tuple-element.52.refs_5_.refs_4_), channel_id=1, source_target_pairs={{0,1},{1,0},{2,3},{3,2},{4,5},{5,4},{6,7},{7,6},{8,9},{9,8},{10,11... | collective-permute-start | bytes 983048 | tf_op jit(solution)/shard_map/ppermute | solution.py:480
  41.6 12.2 %collective-permute-start.15 = (bf16[640,256]{1,0:T(8,128)(2,1)S(1)}, bf16[640,256]{1,0:T(8,128)(2,1)S(1)}, u32[]{:S(2)}, u32[]{:S(2)}) collective-permute-start(bf16[640,256]{1,0:T(8,128)(2,1)S(1)} %get-tuple-element.54.refs_7_.refs_4_), channel_id=1, source_target_pairs={{0,2},{1,3},{2,0},{3,1},{4,6},{5,7},{6,4},{7,5},{8,10},{9,11},{10,... | collective-permute-start | bytes 983048 | tf_op jit(solution)/shard_map/ppermute | solution.py:480
  43.1 15.5 %copy-start.1 = (bf16[640,256]{1,0:T(8,128)(2,1)}, bf16[640,256]{1,0:T(8,128)(2,1)S(1)}, u32[]{:S(2)}) copy-start(bf16[640,256]{1,0:T(8,128)(2,1)S(1)} %get-tuple-element.53.refs_6_.refs_4_) | copy-start | bytes 983044
  43.1 19.1 %copy-start.3 = (bf16[640,256]{1,0:T(8,128)(2,1)}, bf16[640,256]{1,0:T(8,128)(2,1)S(1)}, u32[]{:S(2)}) copy-start(bf16[640,256]{1,0:T(8,128)(2,1)S(1)} %get-tuple-element.55.refs_8_.refs_4_) | copy-start | bytes 983044
  43.1 15.5 %collective-permute-start.21 = (bf16[640,256]{1,0:T(8,128)(2,1)S(1)}, bf16[640,256]{1,0:T(8,128)(2,1)S(1)}, u32[]{:S(2)}, u32[]{:S(2)}) collective-permute-start(bf16[640,256]{1,0:T(8,128)(2,1)S(1)} %get-tuple-element.53.refs_6_.refs_4_), channel_id=1, source_target_pairs={{0,1},{1,0},{2,3},{3,2},{4,5},{5,4},{6,7},{7,6},{8,9},{9,8},{10,11... | collective-permute-start | bytes 983048 | tf_op jit(solution)/shard_map/ppermute | solution.py:480
  44.6 17.6 %collective-permute-start.23 = (bf16[640,256]{1,0:T(8,128)(2,1)S(1)}, bf16[640,256]{1,0:T(8,128)(2,1)S(1)}, u32[]{:S(2)}, u32[]{:S(2)}) collective-permute-start(bf16[640,256]{1,0:T(8,128)(2,1)S(1)} %get-tuple-element.55.refs_8_.refs_4_), channel_id=1, source_target_pairs={{0,2},{1,3},{2,0},{3,1},{4,6},{5,7},{6,4},{7,5},{8,10},{9,11},{10,... | collective-permute-start | bytes 983048 | tf_op jit(solution)/shard_map/ppermute | solution.py:480
  45.6 8.2 %collective-permute-start.14 = (bf16[256,256]{1,0:T(8,128)(2,1)S(1)}, bf16[256,256]{1,0:T(8,128)(2,1)S(1)}, u32[]{:S(2)}, u32[]{:S(2)}) collective-permute-start(bf16[256,256]{1,0:T(8,128)(2,1)S(1)} %collective-permute-done.13.refs_2_), channel_id=1, source_target_pairs={{0,16},{16,0},{1,17},{17,1},{2,18},{18,2},{3,19},{19,3},{4,20},{20... | collective-permute-start | bytes 393224 | tf_op jit(solution)/shard_map/ppermute | solution.py:474
  52.8 13.5 %collective-permute-start.12 = (bf16[256,640]{1,0:T(8,128)(2,1)S(1)}, bf16[256,640]{1,0:T(8,128)(2,1)S(1)}, u32[]{:S(2)}, u32[]{:S(2)}) collective-permute-start(bf16[256,640]{1,0:T(8,128)(2,1)S(1)} %get-tuple-element.59), channel_id=1, source_target_pairs={{0,2},{1,3},{2,0},{3,1},{4,6},{5,7},{6,4},{7,5},{8,10},{9,11},{10,... | collective-permute-start | bytes 983048 | tf_op jit(solution)/shard_map/ppermute | solution.py:483
  55.0 0.8 copy-start.11
  55.8 10.4 %collective-permute-start.16 = (bf16[256,640]{1,0:T(8,128)(2,1)S(1)}, bf16[256,640]{1,0:T(8,128)(2,1)}, u32[]{:S(2)}, u32[]{:S(2)}) collective-permute-start(bf16[256,640]{1,0:T(8,128)(2,1)S(1)} %get-tuple-element.62), channel_id=1, source_target_pairs={{0,1},{1,0},{2,3},{3,2},{4,5},{5,4},{6,7},{7,6},{8,9},{9,8},{10,11... | collective-permute-start | bytes 983048 | tf_op jit(solution)/shard_map/ppermute | solution.py:483
  60.4 0.8 copy-start.7
  61.2 11.1 %collective-permute-start.22 = (bf16[256,640]{1,0:T(8,128)(2,1)}, bf16[256,640]{1,0:T(8,128)(2,1)}, u32[]{:S(2)}, u32[]{:S(2)}) collective-permute-start(bf16[256,640]{1,0:T(8,128)(2,1)} %get-tuple-element.71), channel_id=1, source_target_pairs={{0,2},{1,3},{2,0},{3,1},{4,6},{5,7},{6,4},{7,5},{8,10},{9,11},{10,... | collective-permute-start | bytes 983048 | tf_op jit(solution)/shard_map/ppermute | solution.py:483
  63.9 0.8 copy-start.13
  64.8 8.2 %collective-permute-start.24 = (bf16[256,640]{1,0:T(8,128)(2,1)}, bf16[256,640]{1,0:T(8,128)(2,1)}, u32[]{:S(2)}, u32[]{:S(2)}) collective-permute-start(bf16[256,640]{1,0:T(8,128)(2,1)} %get-tuple-element.72), channel_id=1, source_target_pairs={{0,1},{1,0},{2,3},{3,2},{4,5},{5,4},{6,7},{7,6},{8,9},{9,8},{10,11... | collective-permute-start | bytes 983048 | tf_op jit(solution)/shard_map/ppermute | solution.py:483
  67.0 1.1 copy-start.12
  68.0 20.5 %copy-start.2 = (bf16[640,256]{1,0:T(8,128)(2,1)S(1)}, bf16[640,256]{1,0:T(8,128)(2,1)}, u32[]{:S(2)}) copy-start(bf16[640,256]{1,0:T(8,128)(2,1)} %copy-done.1) | copy-start | bytes 983044
  68.0 20.5 %copy-start.4 = (bf16[640,256]{1,0:T(8,128)(2,1)S(1)}, bf16[640,256]{1,0:T(8,128)(2,1)}, u32[]{:S(2)}) copy-start(bf16[640,256]{1,0:T(8,128)(2,1)} %copy-done.3) | copy-start | bytes 983044
  68.1 20.5 %copy-start.6 = (f32[256,1024]{1,0:T(8,128)S(1)}, f32[256,1024]{1,0:T(8,128)}, u32[]{:S(2)}) copy-start(f32[256,1024]{1,0:T(8,128)} %copy-done.5) | copy-start | bytes 3145732
  70.1 0.8 copy-start.9
  70.9 8.5 %collective-permute-start.17 = (bf16[128,1280]{1,0:T(8,128)(2,1)}, bf16[128,1280]{1,0:T(8,128)(2,1)}, u32[]{:S(2)}, u32[]{:S(2)}) collective-permute-start(bf16[128,1280]{1,0:T(8,128)(2,1)} %get-tuple-element.65), channel_id=1, source_target_pairs={{0,4},{1,5},{2,6},{3,7},{4,0},{5,1},{6,2},{7,3},{8,12},{9,13},{10,... | collective-permute-start | bytes 983048 | tf_op jit(solution)/shard_map/ppermute | solution.py:483
  73.0 1.1 copy-start.8
  74.0 1.1 copy-start.14
  77.1 9.8 %collective-permute-start.25 = (bf16[128,1280]{1,0:T(8,128)(2,1)}, bf16[128,1280]{1,0:T(8,128)(2,1)}, u32[]{:S(2)}, u32[]{:S(2)}) collective-permute-start(bf16[128,1280]{1,0:T(8,128)(2,1)} %get-tuple-element.75), channel_id=1, source_target_pairs={{0,4},{1,5},{2,6},{3,7},{4,0},{5,1},{6,2},{7,3},{8,12},{9,13},{10,... | collective-permute-start | bytes 983048 | tf_op jit(solution)/shard_map/ppermute | solution.py:483
  79.5 1.1 copy-start.10
  82.1 29.6 %collective-permute-start.18 = (bf16[32,1280]{1,0:T(8,128)(2,1)S(1)}, bf16[32,1280]{1,0:T(8,128)(2,1)S(1)}, u32[]{:S(2)}, u32[]{:S(2)}) collective-permute-start(bf16[32,1280]{1,0:T(8,128)(2,1)S(1)} %get-tuple-element.68), channel_id=1, source_target_pairs={{0,8},{1,9},{2,10},{3,11},{4,12},{5,13},{6,14},{7,15},{8,0},{9,1},... | collective-permute-start | bytes 245768 | tf_op jit(solution)/shard_map/ppermute | solution.py:483
  83.7 38.9 %collective-permute-start.19 = (f32[32,1280]{1,0:T(8,128)S(1)}, f32[32,1280]{1,0:T(8,128)S(1)}, u32[]{:S(2)}, u32[]{:S(2)}) collective-permute-start(f32[32,1280]{1,0:T(8,128)S(1)} %get-tuple-element.69), channel_id=1, source_target_pairs={{0,16},{16,0},{1,17},{17,1},{2,18},{18,2},{3,19},{19,3},{4,20},{20... | collective-permute-start | bytes 491528 | tf_op jit(solution)/shard_map/ppermute | solution.py:474
  88.5 34.1 %collective-permute-start.27 = (f32[32,1280]{1,0:T(8,128)S(1)}, f32[32,1280]{1,0:T(8,128)S(1)}, u32[]{:S(2)}, u32[]{:S(2)}) collective-permute-start(f32[32,1280]{1,0:T(8,128)S(1)} %get-tuple-element.79), channel_id=1, source_target_pairs={{0,16},{16,0},{1,17},{17,1},{2,18},{18,2},{3,19},{19,3},{4,20},{20... | collective-permute-start | bytes 491528 | tf_op jit(solution)/shard_map/ppermute | solution.py:474
  92.6 3.8 %collective-permute-start.4 = (f32[1,3712]{1,0:T(1,128)S(1)}, f32[1,3712]{1,0:T(1,128)S(1)}, u32[]{:S(2)}, u32[]{:S(2)}) collective-permute-start(f32[1,3712]{1,0:T(1,128)S(1)} %shard_map.124.refs_0_), channel_id=1, source_target_pairs={{0,4},{1,5},{2,6},{3,7},{4,0},{5,1},{6,2},{7,3},{8,12},{9,13},{10,... | collective-permute-start | bytes 44552 | tf_op jit(solution)/shard_map/ppermute | solution.py:483
  96.4 4.6 %collective-permute-start.5 = (f32[1,3712]{1,0:T(1,128)S(1)}, f32[1,3712]{1,0:T(1,128)S(1)}, u32[]{:S(2)}, u32[]{:S(2)}) collective-permute-start(f32[1,3712]{1,0:T(1,128)S(1)} %shard_map.125.refs_0_), channel_id=1, source_target_pairs={{0,8},{1,9},{2,10},{3,11},{4,12},{5,13},{6,14},{7,15},{8,0},{9,1},... | collective-permute-start | bytes 44552 | tf_op jit(solution)/shard_map/ppermute | solution.py:483
  101.0 3.9 %collective-permute-start.6 = (f32[1,3712]{1,0:T(1,128)S(1)}, f32[1,3712]{1,0:T(1,128)S(1)}, u32[]{:S(2)}, u32[]{:S(2)}) collective-permute-start(f32[1,3712]{1,0:T(1,128)S(1)} %shard_map.126.refs_0_), channel_id=1, source_target_pairs={{0,1},{1,0},{2,3},{3,2},{4,5},{5,4},{6,7},{7,6},{8,9},{9,8},{10,11... | collective-permute-start | bytes 44552 | tf_op jit(solution)/shard_map/ppermute | solution.py:483
  105.0 3.7 %collective-permute-start.7 = (f32[1,3712]{1,0:T(1,128)S(1)}, f32[1,3712]{1,0:T(1,128)S(1)}, u32[]{:S(2)}, u32[]{:S(2)}) collective-permute-start(f32[1,3712]{1,0:T(1,128)S(1)} %shard_map.127.refs_0_), channel_id=1, source_target_pairs={{0,2},{1,3},{2,0},{3,1},{4,6},{5,7},{6,4},{7,5},{8,10},{9,11},{10,... | collective-permute-start | bytes 44552 | tf_op jit(solution)/shard_map/ppermute | solution.py:483
  108.7 1.4 %collective-permute-start.8 = (f32[1,3712]{1,0:T(1,128)S(1)}, f32[1,3712]{1,0:T(1,128)S(1)}, u32[]{:S(2)}, u32[]{:S(2)}) collective-permute-start(f32[1,3712]{1,0:T(1,128)S(1)} %shard_map.128.refs_1_), channel_id=1, source_target_pairs={{0,16},{16,0},{1,17},{17,1},{2,18},{18,2},{3,19},{19,3},{4,20},{20... | collective-permute-start | bytes 44552 | tf_op jit(solution)/shard_map/ppermute | solution.py:474
  108.7 10.4 %collective-permute-start.20 = (bf16[32,1280]{1,0:T(8,128)(2,1)S(1)}, bf16[32,1280]{1,0:T(8,128)(2,1)S(1)}, u32[]{:S(2)}, u32[]{:S(2)}) collective-permute-start(bf16[32,1280]{1,0:T(8,128)(2,1)S(1)} %get-tuple-element.70), channel_id=1, source_target_pairs={{0,24},{1,25},{2,26},{3,27},{4,28},{5,29},{6,30},{7,31},{8,16},{9,... | collective-permute-start | bytes 245768 | tf_op jit(solution)/shard_map/ppermute | solution.py:600
  110.1 11.9 %collective-permute-start.26 = (bf16[32,1280]{1,0:T(8,128)(2,1)S(1)}, bf16[32,1280]{1,0:T(8,128)(2,1)S(1)}, u32[]{:S(2)}, u32[]{:S(2)}) collective-permute-start(bf16[32,1280]{1,0:T(8,128)(2,1)S(1)} %get-tuple-element.78), channel_id=1, source_target_pairs={{0,8},{1,9},{2,10},{3,11},{4,12},{5,13},{6,14},{7,15},{8,0},{9,1},... | collective-permute-start | bytes 245768 | tf_op jit(solution)/shard_map/ppermute | solution.py:483
  111.8 10.8 %collective-permute-start.28 = (bf16[32,1280]{1,0:T(8,128)(2,1)S(1)}, bf16[32,1280]{1,0:T(8,128)(2,1)S(1)}, u32[]{:S(2)}, u32[]{:S(2)}) collective-permute-start(bf16[32,1280]{1,0:T(8,128)(2,1)S(1)} %get-tuple-element.80), channel_id=1, source_target_pairs={{0,24},{1,25},{2,26},{3,27},{4,28},{5,29},{6,30},{7,31},{8,16},{9,... | collective-permute-start | bytes 245768 | tf_op jit(solution)/shard_map/ppermute | solution.py:600
  (2 other events, 1.4 us)

commit v6 on v5

--- a/solution.py
+++ b/solution.py
@@ -424,6 +424,11 @@
     on_core(ids_ref[0], cores, run)
 
 
+def join_kernel(kept_ref, away_ref, cross_ref, far_ref, own_ref, other_ref):
+    own_ref[...] = kept_ref[...] + away_ref[...].astype(F32)
+    other_ref[...] = cross_ref[...] + far_ref[...].astype(F32)
+
+
 def finish_kernel(cores, tiling, ids_ref, scale_ref, *refs):
     parts, out_ref = refs[:-1], refs[-1]
     sizes, starts, half = tiling
@@ -432,9 +437,16 @@
 
     def run(core):
         for turn in range(TURNS):
-            kept, away, cross, far = parts[4 * turn : 4 * turn + 4]
-            for owner, near_ref, came_ref in ((core, kept, away), (1 - core, cross, far)):
-                total = (near_ref[...] + came_ref[...].astype(F32)) * inverse
+            if turn < TURNS - 1:
+                sums = [ref[...] for ref in parts[2 * turn : 2 * turn + 2]]
+            else:
+                kept, away, cross, far = parts[2 * turn :]
+                sums = [
+                    kept[...] + away[...].astype(F32),
+                    cross[...] + far[...].astype(F32),
+                ]
+            for owner, total in zip((core, 1 - core), sums):
+                total = total * inverse
                 first = 0
                 for index in (turn, turn + TURNS):
                     start = owner * half + starts[index]
@@ -599,7 +611,16 @@
         ]
         far = lax.ppermute(far, ("teach", "dp"), pairs)
         cross = swap(cross)
-        ends += [part, away, cross, far]
+        if turn < TURNS - 1:
+            ends += call(
+                join_kernel,
+                None,
+                [*map(Pulled, (part, away, cross, far))],
+                [shape(out_rows, width_here)] * 2,
+                4,
+            )
+        else:
+            ends += [part, away, cross, far]
 
     small = call(
         functools.partial(back_kernel, cores, tiling),

time: 126 us -> 126 us (level)
    pallas_call x19 -> x20, Pallas kernels: 32.9 us -> 33.3 us  [call(): pl.pallas_call(run, in_specs=in_specs, out_specs=jax.tree.map(lambda _: p...]
  transfers between devices with their start and end apart: 30 -> 30, of which waited for: 17 -> 17; matrix products, arithmetic and copies ran while one was open for 1% -> 1% of each run, Pallas kernels for 19% -> 20%
where the time goes in v6:
time: 126 us; the launch traced here: 125 us
  waiting for transfers between devices  46 us (37%)
  Pallas kernels  33.3 us (26%)
  starting transfers between devices  31.8 us (25%)
  local copies, waits for them, and re-layouts  10.9 us (9%)
  between operations  1.68 us (1%)
    pallas_call x20, Pallas kernels, call(): pl.pallas_call(run, in_specs=in_specs, out_specs=jax.tree.map(lambda _: p...  33.3 us
    ppermute x12, waiting for transfers between devices, flip(): return lax.ppermute(value, 'dp', [(i, i ^ mask) for i in range(chips)])  18.1 us
    ppermute x12, starting transfers between devices, flip(): return lax.ppermute(value, 'dp', [(i, i ^ mask) for i in range(chips)])  15 us
    ppermute x6, waiting for transfers between devices, along(): return lax.ppermute(value, 'dp', rotation(chips, stride, size, step))  12.1 us
    unnamed x40, local copies, waits for them, and re-layouts  10.9 us
    all_to_all x1, starting transfers between devices, body(): lax.all_to_all(student_hidden.reshape(chips, slots, width), 'dp', split_a...  8.48 us
    ppermute x2, waiting for transfers between devices, body(): far = lax.ppermute(far, ('teach', 'dp'), pairs)  6.48 us
    all_to_all x1, waiting for transfers between devices, body(): lax.all_to_all(student_hidden.reshape(chips, slots, width), 'dp', split_a...  6.32 us
  transfers between devices with their start and end apart: 30, of which 17 were waited for; matrix products, arithmetic and copies ran while one was open for 1% of the time, Pallas kernels for 20%

profile of v6, /device:TPU:0, one launch (start us, length us, event | category | flops | bytes accessed | tf_op | source)
XLA Modules:
  0.0 124.8 jit_solution(14321500094549534750)
XLA Ops:
  0.7 8.5 %all-to-all-start = ((bf16[16,16,1024]{2,1,0:T(8,128)(2,1)}), bf16[16,16,1024]{2,1,0:T(8,128)(2,1)S(1)}, u32[]{:S(2)}, u32[]{:S(2)}) async-start(bf16[16,16,1024]{2,1,0:T(8,128)(2,1)} %bitcast.47), calls=%async_computation | async-start | bytes 1048576 | tf_op jit(solution)/shard_map/all_to_all | solution.py:497
  10.5 1.7 %copy-done = bf16[1,256,5000]{1,2,0:T(8,128)(2,1)S(1)} copy-done((bf16[1,256,5000]{1,2,0:T(8,128)(2,1)S(1)}, bf16[1,256,5000]{1,2,0:T(8,128)(2,1)}, u32[]{:S(2)}) %copy-start) | copy-done | bytes 2560024
  12.9 5.0 %shard_map.120 = (bf16[2560,256]{1,0:T(8,128)(2,1)S(1)}, bf16[2560,256]{1,0:T(8,128)(2,1)}, f32[1,256]{1,0:T(1,128)S(1)}) custom-call(s32[1]{0:T(128)} %bitcast.refs_0_, bf16[5000,256]{1,0:T(8,128)(2,1)S(1)} %bitcast.38, f32[1,256]{1,0:T(1,128)S(1)} %bitcast.43, f32[1,256]{1,0:T(1,128)S(1)} %broadcast_select_fusion.refs_3_, s32[1,256]{1,0:T(1,128)S(1)} %bitcast.44), custom_call_target="tpu_custom_call" | custom-call | tf_op jit(solution)/shard_map/pallas_call | solution.py:111
  17.9 6.3 %all-to-all-done = bf16[16,16,1024]{2,1,0:T(8,128)(2,1)S(1)} async-done(((bf16[16,16,1024]{2,1,0:T(8,128)(2,1)}), bf16[16,16,1024]{2,1,0:T(8,128)(2,1)S(1)}, u32[]{:S(2)}, u32[]{:S(2)}) %all-to-all-start) | async-done | bytes 524320 | tf_op jit(solution)/shard_map/all_to_all | solution.py:497
  24.5 1.8 %collective-permute-done.refs_4_ = bf16[256,1024]{1,0:T(8,128)(2,1)} collective-permute-done((bf16[256,1024]{1,0:T(8,128)(2,1)S(1)}, bf16[256,1024]{1,0:T(8,128)(2,1)}, u32[]{:S(2)}, u32[]{:S(2)}) %collective-permute-start) | collective-permute-done | bytes 524320 | tf_op jit(solution)/shard_map/ppermute | solution.py:486
  26.3 6.4 %shard_map.121 = (f32[256,1024]{1,0:T(8,128)S(1)}, f32[2560,256]{1,0:T(8,128)S(1)}, f32[8,256]{1,0:T(8,128)S(1)}, f32[1,256]{1,0:T(1,128)S(1)}, bf16[512,256]{1,...) custom-call(s32[3]{0:T(128)S(1)} %pad_add_fusion.refs_0_, ...), custom_call_target="tpu_custom_call" | custom-call | tf_op jit(solution)/shard_map/pallas_call | solution.py:111
  33.3 1.0 collective-permute-start.13
  34.3 4.0 %collective-permute-done.9.refs_2_ = bf16[256,256]{1,0:T(8,128)(2,1)S(1)} collective-permute-done((bf16[256,256]{1,0:T(8,128)(2,1)S(1)}, bf16[256,256]{1,0:T(8,128)(2,1)S(1)}, u32[]{:S(2)}, u32[]{:S(2)}) %collective-permute-start.9) | collective-permute-done | bytes 131104 | tf_op jit(solution)/shard_map/ppermute | solution.py:492
  38.8 1.2 collective-permute-done.3.refs_4_
  40.0 1.0 shard_map.123
  41.6 1.0 collective-permute-start.15
  43.1 1.5 %collective-permute-start.21 = (bf16[640,256]{1,0:T(8,128)(2,1)S(1)}, bf16[640,256]{1,0:T(8,128)(2,1)S(1)}, u32[]{:S(2)}, u32[]{:S(2)}) collective-permute-start(bf16[640,256]{1,0:T(8,128)(2,1)S(1)} %get-tuple-element.55.refs_6_.refs_4_), channel_id=1, source_target_pairs={{0,1},{1,0},{2,3},{3,2},{4,5},{5,4},{6,7},{7,6},{8,9},{9,8},{10,11... | collective-permute-start | bytes 983048 | tf_op jit(solution)/shard_map/ppermute | solution.py:492
  44.6 1.1 collective-permute-start.23
  45.8 5.8 %collective-permute-done.11.refs_5_ = bf16[640,256]{1,0:T(8,128)(2,1)S(1)} collective-permute-done((bf16[640,256]{1,0:T(8,128)(2,1)S(1)}, bf16[640,256]{1,0:T(8,128)(2,1)S(1)}, u32[]{:S(2)}, u32[]{:S(2)}) %collective-permute-start.11) | collective-permute-done | bytes 327712 | tf_op jit(solution)/shard_map/ppermute | solution.py:492
  51.6 1.1 shard_map.130
  52.8 1.0 collective-permute-start.12
  53.8 1.1 shard_map.131
  56.4 2.3 %collective-permute-done.21.refs_5_ = bf16[640,256]{1,0:T(8,128)(2,1)S(1)} collective-permute-done((bf16[640,256]{1,0:T(8,128)(2,1)S(1)}, bf16[640,256]{1,0:T(8,128)(2,1)S(1)}, u32[]{:S(2)}, u32[]{:S(2)}) %collective-permute-start.21) | collective-permute-done | bytes 327712 | tf_op jit(solution)/shard_map/ppermute | solution.py:492
  58.6 1.7 %shard_map.135 = (f32[256,640]{1,0:T(8,128)S(1)}, bf16[256,640]{1,0:T(8,128)(2,1)}) custom-call(s32[2]{0:T(128)S(1)} %pad_add_fusion.2.refs_0_, bf16[512,256]{1,0:T(8,128)(2,1)S(1)} %get-tuple-element.59.refs_1_, bf16[256,256]{1,0:T(8,128)(2,1)S(1)} %collective-permute-done.9.refs_2_, bf16[256,256]{1,0:T(8,128)(2,1)S(1)} %collective-permute-done.10.refs_3_, ...), custom_call_target="tpu_custom_call" | custom-call | tf_op jit(solution)/shard_map/pallas_call | solution.py:111
  61.2 1.0 collective-permute-start.22
  62.2 1.8 %shard_map.136 = (f32[256,640]{1,0:T(8,128)S(1)}, bf16[256,640]{1,0:T(8,128)(2,1)}) custom-call(s32[2]{0:T(128)S(1)} %pad_add_fusion.3.refs_0_, bf16[512,256]{1,0:T(8,128)(2,1)S(1)} %get-tuple-element.62.refs_1_, bf16[256,256]{1,0:T(8,128)(2,1)S(1)} %collective-permute-done.13.refs_2_, bf16[256,256]{1,0:T(8,128)(2,1)S(1)} %collective-permute-done.14.refs_3_, ...), custom_call_target="tpu_custom_call" | custom-call | tf_op jit(solution)/shard_map/pallas_call | solution.py:111
  67.0 1.1 copy-done.12
  68.0 2.1 %shard_map.132 = (f32[128,1280]{1,0:T(8,128)S(1)}, bf16[128,1280]{1,0:T(8,128)(2,1)}) custom-call(s32[1]{0:T(128)} %bitcast.17.refs_0_, bf16[256,640]{1,0:T(8,128)(2,1)} %copy-done.18, bf16[256,640]{1,0:T(8,128)(2,1)} %collective-permute-done.16.refs_2_, f32[256,640]{1,0:T(8,128)S(1)} %get-tuple-element.65.refs_3_, f32[256,640]{1,0:T(8,128)S(1)} %copy-done.12), custom_call_target="tpu_custom_call" | custom-call | tf_op jit(solution)/shard_map/pallas_call | solution.py:111
  70.9 1.3 %collective-permute-start.17 = (bf16[128,1280]{1,0:T(8,128)(2,1)}, bf16[128,1280]{1,0:T(8,128)(2,1)}, u32[]{:S(2)}, u32[]{:S(2)}) collective-permute-start(bf16[128,1280]{1,0:T(8,128)(2,1)} %get-tuple-element.67), channel_id=1, source_target_pairs={{0,4},{1,5},{2,6},{3,7},{4,0},{5,1},{6,2},{7,3},{8,12},{9,13},{10,... | collective-permute-start | bytes 983048 | tf_op jit(solution)/shard_map/ppermute | solution.py:495
  73.0 1.1 copy-done.8
  74.0 1.1 copy-done.14
  75.1 1.9 %shard_map.137 = (f32[128,1280]{1,0:T(8,128)S(1)}, bf16[128,1280]{1,0:T(8,128)(2,1)}) custom-call(s32[1]{0:T(128)} %bitcast.17.refs_0_, bf16[256,640]{1,0:T(8,128)(2,1)} %collective-permute-done.22.refs_1_, bf16[256,640]{1,0:T(8,128)(2,1)} %collective-permute-done.24.refs_2_, f32[256,640]{1,0:T(8,128)S(1)} %copy-done.8, f32[256,640]{1,0:T(8,128)S(1)} %copy-done.14), custom_call_target="tpu_custom_call" | custom-call | tf_op jit(solution)/shard_map/pallas_call | solution.py:111
  77.1 1.3 %collective-permute-start.25 = (bf16[128,1280]{1,0:T(8,128)(2,1)}, bf16[128,1280]{1,0:T(8,128)(2,1)}, u32[]{:S(2)}, u32[]{:S(2)}) collective-permute-start(bf16[128,1280]{1,0:T(8,128)(2,1)} %get-tuple-element.79), channel_id=1, source_target_pairs={{0,4},{1,5},{2,6},{3,7},{4,0},{5,1},{6,2},{7,3},{8,12},{9,13},{10,... | collective-permute-start | bytes 983048 | tf_op jit(solution)/shard_map/ppermute | solution.py:495
  78.5 1.0 collective-permute-done.17.refs_1_
  79.5 1.1 copy-done.10
  80.6 1.6 %shard_map.133 = (f32[32,1280]{1,0:T(8,128)S(1)}, bf16[32,1280]{1,0:T(8,128)(2,1)S(1)}, f32[32,1280]{1,0:T(8,128)S(1)}, bf16[32,1280]{1,0:T(8,128)(2,1)S(1)}) custom-call(s32[2]{0:T(128)S(1)} %pad_add_fusion.1.refs_0_, bf16[128,1280]{1,0:T(8,128)(2,1)} %collective-permute-done.17.refs_1_, f32[128,1280]{1,0:T(8,128)S(1)} %copy-done.10), custom_call_target="tpu_custom_call" | custom-call | tf_op jit(solution)/shard_map/pallas_call | solution.py:111
  82.2 1.5 %collective-permute-start.18 = (bf16[32,1280]{1,0:T(8,128)(2,1)S(1)}, bf16[32,1280]{1,0:T(8,128)(2,1)S(1)}, u32[]{:S(2)}, u32[]{:S(2)}) collective-permute-start(bf16[32,1280]{1,0:T(8,128)(2,1)S(1)} %get-tuple-element.70), channel_id=1, source_target_pairs={{0,8},{1,9},{2,10},{3,11},{4,12},{5,13},{6,14},{7,15},{8,0},{9,1},... | collective-permute-start | bytes 245768 | tf_op jit(solution)/shard_map/ppermute | solution.py:495
  83.7 3.2 %collective-permute-done.25.refs_1_ = bf16[128,1280]{1,0:T(8,128)(2,1)} collective-permute-done((bf16[128,1280]{1,0:T(8,128)(2,1)}, bf16[128,1280]{1,0:T(8,128)(2,1)}, u32[]{:S(2)}, u32[]{:S(2)}) %collective-permute-start.25) | collective-permute-done | bytes 327712 | tf_op jit(solution)/shard_map/ppermute | solution.py:495
  86.9 1.6 %shard_map.138 = (f32[32,1280]{1,0:T(8,128)S(1)}, bf16[32,1280]{1,0:T(8,128)(2,1)S(1)}, f32[32,1280]{1,0:T(8,128)S(1)}, bf16[32,1280]{1,0:T(8,128)(2,1)S(1)}) custom-call(s32[2]{0:T(128)S(1)} %pad_add_fusion.1.refs_0_, bf16[128,1280]{1,0:T(8,128)(2,1)} %collective-permute-done.25.refs_1_, f32[128,1280]{1,0:T(8,128)S(1)} %get-tuple-element.80.refs_2_), custom_call_target="tpu_custom_call" | custom-call | tf_op jit(solution)/shard_map/pallas_call | solution.py:111
  88.6 4.0 %shard_map.124.refs_0_ = f32[1,3712]{1,0:T(1,128)S(1)} custom-call(s32[1]{0:T(128)} %bitcast.refs_0_, bf16[5000,1024]{1,0:T(8,128)(2,1)} %bitcast.46, f32[256,1024]{1,0:T(8,128)S(1)} %copy-done.6, f32[1,128]{1,0:T(1,128)S(1)} %get-tuple-element.53.refs_3_, f32[1,256]{1,0:T(1,128)S(1)} %fusion.4.refs_4_, ...), custom_call_target="tpu_custom_call" | custom-call | tf_op jit(solution)/shard_map/pallas_call | solution.py:111
  92.6 1.4 %collective-permute-start.4 = (f32[1,3712]{1,0:T(1,128)S(1)}, f32[1,3712]{1,0:T(1,128)S(1)}, u32[]{:S(2)}, u32[]{:S(2)}) collective-permute-start(f32[1,3712]{1,0:T(1,128)S(1)} %shard_map.124.refs_0_), channel_id=1, source_target_pairs={{0,4},{1,5},{2,6},{3,7},{4,0},{5,1},{6,2},{7,3},{8,12},{9,13},{10,... | collective-permute-start | bytes 44552 | tf_op jit(solution)/shard_map/ppermute | solution.py:495
  94.0 2.4 %collective-permute-done.4.refs_1_ = f32[1,3712]{1,0:T(1,128)S(1)} collective-permute-done((f32[1,3712]{1,0:T(1,128)S(1)}, f32[1,3712]{1,0:T(1,128)S(1)}, u32[]{:S(2)}, u32[]{:S(2)}) %collective-permute-start.4) | collective-permute-done | bytes 14880 | tf_op jit(solution)/shard_map/ppermute | solution.py:495
  96.4 1.5 %collective-permute-start.5 = (f32[1,3712]{1,0:T(1,128)S(1)}, f32[1,3712]{1,0:T(1,128)S(1)}, u32[]{:S(2)}, u32[]{:S(2)}) collective-permute-start(f32[1,3712]{1,0:T(1,128)S(1)} %shard_map.125.refs_0_), channel_id=1, source_target_pairs={{0,8},{1,9},{2,10},{3,11},{4,12},{5,13},{6,14},{7,15},{8,0},{9,1},... | collective-permute-start | bytes 44552 | tf_op jit(solution)/shard_map/ppermute | solution.py:495
  97.9 3.1 %collective-permute-done.5.refs_1_ = f32[1,3712]{1,0:T(1,128)S(1)} collective-permute-done((f32[1,3712]{1,0:T(1,128)S(1)}, f32[1,3712]{1,0:T(1,128)S(1)}, u32[]{:S(2)}, u32[]{:S(2)}) %collective-permute-start.5) | collective-permute-done | bytes 14880 | tf_op jit(solution)/shard_map/ppermute | solution.py:495
  101.0 2.2 %collective-permute-start.6 = (f32[1,3712]{1,0:T(1,128)S(1)}, f32[1,3712]{1,0:T(1,128)S(1)}, u32[]{:S(2)}, u32[]{:S(2)}) collective-permute-start(f32[1,3712]{1,0:T(1,128)S(1)} %shard_map.126.refs_0_), channel_id=1, source_target_pairs={{0,1},{1,0},{2,3},{3,2},{4,5},{5,4},{6,7},{7,6},{8,9},{9,8},{10,11... | collective-permute-start | bytes 44552 | tf_op jit(solution)/shard_map/ppermute | solution.py:495
  103.3 1.7 %collective-permute-done.6.refs_1_ = f32[1,3712]{1,0:T(1,128)S(1)} collective-permute-done((f32[1,3712]{1,0:T(1,128)S(1)}, f32[1,3712]{1,0:T(1,128)S(1)}, u32[]{:S(2)}, u32[]{:S(2)}) %collective-permute-start.6) | collective-permute-done | bytes 14880 | tf_op jit(solution)/shard_map/ppermute | solution.py:495
  105.0 0.9 collective-permute-start.7
  105.9 2.8 %collective-permute-done.7.refs_1_ = f32[1,3712]{1,0:T(1,128)S(1)} collective-permute-done((f32[1,3712]{1,0:T(1,128)S(1)}, f32[1,3712]{1,0:T(1,128)S(1)}, u32[]{:S(2)}, u32[]{:S(2)}) %collective-permute-start.7) | collective-permute-done | bytes 14880 | tf_op jit(solution)/shard_map/ppermute | solution.py:495
  108.7 1.4 %collective-permute-start.20 = (bf16[32,1280]{1,0:T(8,128)(2,1)S(1)}, bf16[32,1280]{1,0:T(8,128)(2,1)S(1)}, u32[]{:S(2)}, u32[]{:S(2)}) collective-permute-start(bf16[32,1280]{1,0:T(8,128)(2,1)S(1)} %get-tuple-element.72), channel_id=1, source_target_pairs={{0,24},{1,25},{2,26},{3,27},{4,28},{5,29},{6,30},{7,31},{8,16},{9,... | collective-permute-start | bytes 245768 | tf_op jit(solution)/shard_map/ppermute | solution.py:612
  110.1 1.6 %collective-permute-start.26 = (bf16[32,1280]{1,0:T(8,128)(2,1)S(1)}, bf16[32,1280]{1,0:T(8,128)(2,1)S(1)}, u32[]{:S(2)}, u32[]{:S(2)}) collective-permute-start(bf16[32,1280]{1,0:T(8,128)(2,1)S(1)} %get-tuple-element.82), channel_id=1, source_target_pairs={{0,8},{1,9},{2,10},{3,11},{4,12},{5,13},{6,14},{7,15},{8,0},{9,1},... | collective-permute-start | bytes 245768 | tf_op jit(solution)/shard_map/ppermute | solution.py:495
  113.1 5.9 %collective-permute-done.20.refs_3_ = bf16[32,1280]{1,0:T(8,128)(2,1)S(1)} collective-permute-done((bf16[32,1280]{1,0:T(8,128)(2,1)S(1)}, bf16[32,1280]{1,0:T(8,128)(2,1)S(1)}, u32[]{:S(2)}, u32[]{:S(2)}) %collective-permute-start.20) | collective-permute-done | bytes 81952 | tf_op jit(solution)/shard_map/ppermute | solution.py:612
  119.8 2.3 %collective-permute-done.26.refs_5_ = bf16[32,1280]{1,0:T(8,128)(2,1)S(1)} collective-permute-done((bf16[32,1280]{1,0:T(8,128)(2,1)S(1)}, bf16[32,1280]{1,0:T(8,128)(2,1)S(1)}, u32[]{:S(2)}, u32[]{:S(2)}) %collective-permute-start.26) | collective-permute-done | bytes 81952 | tf_op jit(solution)/shard_map/ppermute | solution.py:495
  122.6 2.0 %shard_map.139 = f32[32,5000]{1,0:T(8,128)} custom-call(s32[1]{0:T(128)} %bitcast.refs_0_, f32[1,128]{1,0:T(1,128)S(1)} %get-tuple-element.58.refs_1_, f32[32,1280]{1,0:T(8,128)S(1)} %get-tuple-element.73.refs_2_, f32[32,1280]{1,0:T(8,128)S(1)} %get-tuple-element.74.refs_3_, f32[32,1280]{1,0:T(8,128)S(1)} %get-tuple-element.81.refs_4_, ...), custom_call_target="tpu_custom_call" | custom-call | tf_op jit(solution)/shard_map/pallas_call | solution.py:111
  (81 shorter events, 13.6 us)
Async XLA Ops:
  0.6 23.7 %copy-start.19 = (s32[256,1]{0,1:T(1,128)S(1)}, s32[256,1]{0,1:T(1,128)}, u32[]{:S(2)}) copy-start(s32[256,1]{0,1:T(1,128)} %param.10) | copy-start | bytes 3076
  0.6 25.6 %copy-start.16 = (f32[1024]{0:T(1024)S(1)}, f32[1024]{0:T(1024)}, u32[]{:S(2)}) copy-start(f32[1024]{0:T(1024)} %param.17) | copy-start | bytes 12292
  0.7 25.6 %copy-start.15 = (f32[5000]{0:T(1024)S(1)}, f32[5000]{0:T(1024)}, u32[]{:S(2)}) copy-start(f32[5000]{0:T(1024)} %param.16) | copy-start | bytes 60004
  0.7 23.6 %all-to-all-start = ((bf16[16,16,1024]{2,1,0:T(8,128)(2,1)}), bf16[16,16,1024]{2,1,0:T(8,128)(2,1)S(1)}, u32[]{:S(2)}, u32[]{:S(2)}) async-start(bf16[16,16,1024]{2,1,0:T(8,128)(2,1)} %bitcast.47), calls=%async_computation | async-start | bytes 1048576 | tf_op jit(solution)/shard_map/all_to_all | solution.py:497
  10.5 1.7 %copy-start = (bf16[1,256,5000]{1,2,0:T(8,128)(2,1)S(1)}, bf16[1,256,5000]{1,2,0:T(8,128)(2,1)}, u32[]{:S(2)}) copy-start(bf16[1,256,5000]{1,2,0:T(8,128)(2,1)} %param.9) | copy-start | bytes 7680004
  17.9 6.5 %collective-permute-start.1 = (bf16[2560,256]{1,0:T(8,128)(2,1)}, bf16[2560,256]{1,0:T(8,128)(2,1)S(1)}, u32[]{:S(2)}, u32[]{:S(2)}) collective-permute-start(bf16[2560,256]{1,0:T(8,128)(2,1)} %get-tuple-element.47), channel_id=1, source_target_pairs={{0,16},{16,0},{1,17},{17,1},{2,18},{18,2},{3,19},{19,3},{4,20},{20... | collective-permute-start | bytes 3932168 | tf_op jit(solution)/shard_map/ppermute | solution.py:486
  24.2 2.0 %collective-permute-start = (bf16[256,1024]{1,0:T(8,128)(2,1)S(1)}, bf16[256,1024]{1,0:T(8,128)(2,1)}, u32[]{:S(2)}, u32[]{:S(2)}) collective-permute-start(bf16[256,1024]{1,0:T(8,128)(2,1)S(1)} %bitcast.39), channel_id=1, source_target_pairs={{0,16},{16,0},{1,17},{17,1},{2,18},{18,2},{3,19},{19,3},{4,20},{20... | collective-permute-start | bytes 1572872 | tf_op jit(solution)/shard_map/ppermute | solution.py:486
  32.7 8.4 %copy-start.5 = (f32[256,1024]{1,0:T(8,128)}, f32[256,1024]{1,0:T(8,128)S(1)}, u32[]{:S(2)}) copy-start(f32[256,1024]{1,0:T(8,128)S(1)} %get-tuple-element.48.refs_2_) | copy-start | bytes 3145732
  32.7 5.6 %collective-permute-start.9 = (bf16[256,256]{1,0:T(8,128)(2,1)S(1)}, bf16[256,256]{1,0:T(8,128)(2,1)S(1)}, u32[]{:S(2)}, u32[]{:S(2)}) collective-permute-start(bf16[256,256]{1,0:T(8,128)(2,1)S(1)} %get-tuple-element.60), channel_id=1, source_target_pairs={{0,1},{1,0},{2,3},{3,2},{4,5},{5,4},{6,7},{7,6},{8,9},{9,8},{10,11... | collective-permute-start | bytes 393224 | tf_op jit(solution)/shard_map/ppermute | solution.py:492
  33.3 11.3 %collective-permute-start.13 = (bf16[256,256]{1,0:T(8,128)(2,1)S(1)}, bf16[256,256]{1,0:T(8,128)(2,1)S(1)}, u32[]{:S(2)}, u32[]{:S(2)}) collective-permute-start(bf16[256,256]{1,0:T(8,128)(2,1)S(1)} %get-tuple-element.63), channel_id=1, source_target_pairs={{0,2},{1,3},{2,0},{3,1},{4,6},{5,7},{6,4},{7,5},{8,10},{9,11},{10,... | collective-permute-start | bytes 393224 | tf_op jit(solution)/shard_map/ppermute | solution.py:492
  38.3 7.3 %collective-permute-start.10 = (bf16[256,256]{1,0:T(8,128)(2,1)S(1)}, bf16[256,256]{1,0:T(8,128)(2,1)S(1)}, u32[]{:S(2)}, u32[]{:S(2)}) collective-permute-start(bf16[256,256]{1,0:T(8,128)(2,1)S(1)} %collective-permute-done.9.refs_2_), channel_id=1, source_target_pairs={{0,16},{16,0},{1,17},{17,1},{2,18},{18,2},{3,19},{19,3},{4,20},{20... | collective-permute-start | bytes 393224 | tf_op jit(solution)/shard_map/ppermute | solution.py:486
  38.3 1.7 %collective-permute-start.2 = (f32[8,256]{1,0:T(8,128)S(1)}, f32[8,256]{1,0:T(8,128)S(1)}, u32[]{:S(2)}, u32[]{:S(2)}) collective-permute-start(f32[8,256]{1,0:T(8,128)S(1)} %get-tuple-element.50.refs_1_), channel_id=1, source_target_pairs={{0,16},{16,0},{1,17},{17,1},{2,18},{18,2},{3,19},{19,3},{4,20},{20... | collective-permute-start | bytes 24584 | tf_op jit(solution)/shard_map/ppermute | solution.py:486
  38.8 1.2 collective-permute-start.3
  41.0 10.6 %collective-permute-start.11 = (bf16[640,256]{1,0:T(8,128)(2,1)S(1)}, bf16[640,256]{1,0:T(8,128)(2,1)S(1)}, u32[]{:S(2)}, u32[]{:S(2)}) collective-permute-start(bf16[640,256]{1,0:T(8,128)(2,1)S(1)} %get-tuple-element.54.refs_5_.refs_4_), channel_id=1, source_target_pairs={{0,1},{1,0},{2,3},{3,2},{4,5},{5,4},{6,7},{7,6},{8,9},{9,8},{10,11... | collective-permute-start | bytes 983048 | tf_op jit(solution)/shard_map/ppermute | solution.py:492
  41.6 12.2 %collective-permute-start.15 = (bf16[640,256]{1,0:T(8,128)(2,1)S(1)}, bf16[640,256]{1,0:T(8,128)(2,1)S(1)}, u32[]{:S(2)}, u32[]{:S(2)}) collective-permute-start(bf16[640,256]{1,0:T(8,128)(2,1)S(1)} %get-tuple-element.56.refs_7_.refs_4_), channel_id=1, source_target_pairs={{0,2},{1,3},{2,0},{3,1},{4,6},{5,7},{6,4},{7,5},{8,10},{9,11},{10,... | collective-permute-start | bytes 983048 | tf_op jit(solution)/shard_map/ppermute | solution.py:492
  43.1 15.5 %copy-start.1 = (bf16[640,256]{1,0:T(8,128)(2,1)}, bf16[640,256]{1,0:T(8,128)(2,1)S(1)}, u32[]{:S(2)}) copy-start(bf16[640,256]{1,0:T(8,128)(2,1)S(1)} %get-tuple-element.55.refs_6_.refs_4_) | copy-start | bytes 983044
  43.1 19.1 %copy-start.3 = (bf16[640,256]{1,0:T(8,128)(2,1)}, bf16[640,256]{1,0:T(8,128)(2,1)S(1)}, u32[]{:S(2)}) copy-start(bf16[640,256]{1,0:T(8,128)(2,1)S(1)} %get-tuple-element.57.refs_8_.refs_4_) | copy-start | bytes 983044
  43.1 15.5 %collective-permute-start.21 = (bf16[640,256]{1,0:T(8,128)(2,1)S(1)}, bf16[640,256]{1,0:T(8,128)(2,1)S(1)}, u32[]{:S(2)}, u32[]{:S(2)}) collective-permute-start(bf16[640,256]{1,0:T(8,128)(2,1)S(1)} %get-tuple-element.55.refs_6_.refs_4_), channel_id=1, source_target_pairs={{0,1},{1,0},{2,3},{3,2},{4,5},{5,4},{6,7},{7,6},{8,9},{9,8},{10,11... | collective-permute-start | bytes 983048 | tf_op jit(solution)/shard_map/ppermute | solution.py:492
  44.6 17.6 %collective-permute-start.23 = (bf16[640,256]{1,0:T(8,128)(2,1)S(1)}, bf16[640,256]{1,0:T(8,128)(2,1)S(1)}, u32[]{:S(2)}, u32[]{:S(2)}) collective-permute-start(bf16[640,256]{1,0:T(8,128)(2,1)S(1)} %get-tuple-element.57.refs_8_.refs_4_), channel_id=1, source_target_pairs={{0,2},{1,3},{2,0},{3,1},{4,6},{5,7},{6,4},{7,5},{8,10},{9,11},{10,... | collective-permute-start | bytes 983048 | tf_op jit(solution)/shard_map/ppermute | solution.py:492
  45.6 8.2 %collective-permute-start.14 = (bf16[256,256]{1,0:T(8,128)(2,1)S(1)}, bf16[256,256]{1,0:T(8,128)(2,1)S(1)}, u32[]{:S(2)}, u32[]{:S(2)}) collective-permute-start(bf16[256,256]{1,0:T(8,128)(2,1)S(1)} %collective-permute-done.13.refs_2_), channel_id=1, source_target_pairs={{0,16},{16,0},{1,17},{17,1},{2,18},{18,2},{3,19},{19,3},{4,20},{20... | collective-permute-start | bytes 393224 | tf_op jit(solution)/shard_map/ppermute | solution.py:486
  52.8 13.5 %collective-permute-start.12 = (bf16[256,640]{1,0:T(8,128)(2,1)S(1)}, bf16[256,640]{1,0:T(8,128)(2,1)S(1)}, u32[]{:S(2)}, u32[]{:S(2)}) collective-permute-start(bf16[256,640]{1,0:T(8,128)(2,1)S(1)} %get-tuple-element.61), channel_id=1, source_target_pairs={{0,2},{1,3},{2,0},{3,1},{4,6},{5,7},{6,4},{7,5},{8,10},{9,11},{10,... | collective-permute-start | bytes 983048 | tf_op jit(solution)/shard_map/ppermute | solution.py:495
  55.0 0.8 copy-start.11
  55.8 10.4 %collective-permute-start.16 = (bf16[256,640]{1,0:T(8,128)(2,1)S(1)}, bf16[256,640]{1,0:T(8,128)(2,1)}, u32[]{:S(2)}, u32[]{:S(2)}) collective-permute-start(bf16[256,640]{1,0:T(8,128)(2,1)S(1)} %get-tuple-element.64), channel_id=1, source_target_pairs={{0,1},{1,0},{2,3},{3,2},{4,5},{5,4},{6,7},{7,6},{8,9},{9,8},{10,11... | collective-permute-start | bytes 983048 | tf_op jit(solution)/shard_map/ppermute | solution.py:495
  60.4 0.8 copy-start.7
  61.2 11.1 %collective-permute-start.22 = (bf16[256,640]{1,0:T(8,128)(2,1)}, bf16[256,640]{1,0:T(8,128)(2,1)}, u32[]{:S(2)}, u32[]{:S(2)}) collective-permute-start(bf16[256,640]{1,0:T(8,128)(2,1)} %get-tuple-element.75), channel_id=1, source_target_pairs={{0,2},{1,3},{2,0},{3,1},{4,6},{5,7},{6,4},{7,5},{8,10},{9,11},{10,... | collective-permute-start | bytes 983048 | tf_op jit(solution)/shard_map/ppermute | solution.py:495
  64.0 0.8 copy-start.13
  64.8 8.2 %collective-permute-start.24 = (bf16[256,640]{1,0:T(8,128)(2,1)}, bf16[256,640]{1,0:T(8,128)(2,1)}, u32[]{:S(2)}, u32[]{:S(2)}) collective-permute-start(bf16[256,640]{1,0:T(8,128)(2,1)} %get-tuple-element.76), channel_id=1, source_target_pairs={{0,1},{1,0},{2,3},{3,2},{4,5},{5,4},{6,7},{7,6},{8,9},{9,8},{10,11... | collective-permute-start | bytes 983048 | tf_op jit(solution)/shard_map/ppermute | solution.py:495
  67.0 1.1 copy-start.12
  68.0 20.5 %copy-start.2 = (bf16[640,256]{1,0:T(8,128)(2,1)S(1)}, bf16[640,256]{1,0:T(8,128)(2,1)}, u32[]{:S(2)}) copy-start(bf16[640,256]{1,0:T(8,128)(2,1)} %copy-done.1) | copy-start | bytes 983044
  68.0 20.5 %copy-start.4 = (bf16[640,256]{1,0:T(8,128)(2,1)S(1)}, bf16[640,256]{1,0:T(8,128)(2,1)}, u32[]{:S(2)}) copy-start(bf16[640,256]{1,0:T(8,128)(2,1)} %copy-done.3) | copy-start | bytes 983044
  68.0 20.5 %copy-start.6 = (f32[256,1024]{1,0:T(8,128)S(1)}, f32[256,1024]{1,0:T(8,128)}, u32[]{:S(2)}) copy-start(f32[256,1024]{1,0:T(8,128)} %copy-done.5) | copy-start | bytes 3145732
  70.1 0.8 copy-start.9
  70.9 8.5 %collective-permute-start.17 = (bf16[128,1280]{1,0:T(8,128)(2,1)}, bf16[128,1280]{1,0:T(8,128)(2,1)}, u32[]{:S(2)}, u32[]{:S(2)}) collective-permute-start(bf16[128,1280]{1,0:T(8,128)(2,1)} %get-tuple-element.67), channel_id=1, source_target_pairs={{0,4},{1,5},{2,6},{3,7},{4,0},{5,1},{6,2},{7,3},{8,12},{9,13},{10,... | collective-permute-start | bytes 983048 | tf_op jit(solution)/shard_map/ppermute | solution.py:495
  73.0 1.1 copy-start.8
  74.0 1.1 copy-start.14
  77.1 9.8 %collective-permute-start.25 = (bf16[128,1280]{1,0:T(8,128)(2,1)}, bf16[128,1280]{1,0:T(8,128)(2,1)}, u32[]{:S(2)}, u32[]{:S(2)}) collective-permute-start(bf16[128,1280]{1,0:T(8,128)(2,1)} %get-tuple-element.79), channel_id=1, source_target_pairs={{0,4},{1,5},{2,6},{3,7},{4,0},{5,1},{6,2},{7,3},{8,12},{9,13},{10,... | collective-permute-start | bytes 983048 | tf_op jit(solution)/shard_map/ppermute | solution.py:495
  79.5 1.1 copy-start.10
  82.2 29.6 %collective-permute-start.18 = (bf16[32,1280]{1,0:T(8,128)(2,1)S(1)}, bf16[32,1280]{1,0:T(8,128)(2,1)S(1)}, u32[]{:S(2)}, u32[]{:S(2)}) collective-permute-start(bf16[32,1280]{1,0:T(8,128)(2,1)S(1)} %get-tuple-element.70), channel_id=1, source_target_pairs={{0,8},{1,9},{2,10},{3,11},{4,12},{5,13},{6,14},{7,15},{8,0},{9,1},... | collective-permute-start | bytes 245768 | tf_op jit(solution)/shard_map/ppermute | solution.py:495
  83.7 35.4 %collective-permute-start.19 = (f32[32,1280]{1,0:T(8,128)S(1)}, f32[32,1280]{1,0:T(8,128)S(1)}, u32[]{:S(2)}, u32[]{:S(2)}) collective-permute-start(f32[32,1280]{1,0:T(8,128)S(1)} %get-tuple-element.71), channel_id=1, source_target_pairs={{0,16},{16,0},{1,17},{17,1},{2,18},{18,2},{3,19},{19,3},{4,20},{20... | collective-permute-start | bytes 491528 | tf_op jit(solution)/shard_map/ppermute | solution.py:486
  88.5 34.1 %collective-permute-start.27 = (f32[32,1280]{1,0:T(8,128)S(1)}, f32[32,1280]{1,0:T(8,128)S(1)}, u32[]{:S(2)}, u32[]{:S(2)}) collective-permute-start(f32[32,1280]{1,0:T(8,128)S(1)} %get-tuple-element.83), channel_id=1, source_target_pairs={{0,16},{16,0},{1,17},{17,1},{2,18},{18,2},{3,19},{19,3},{4,20},{20... | collective-permute-start | bytes 491528 | tf_op jit(solution)/shard_map/ppermute | solution.py:486
  92.6 3.8 %collective-permute-start.4 = (f32[1,3712]{1,0:T(1,128)S(1)}, f32[1,3712]{1,0:T(1,128)S(1)}, u32[]{:S(2)}, u32[]{:S(2)}) collective-permute-start(f32[1,3712]{1,0:T(1,128)S(1)} %shard_map.124.refs_0_), channel_id=1, source_target_pairs={{0,4},{1,5},{2,6},{3,7},{4,0},{5,1},{6,2},{7,3},{8,12},{9,13},{10,... | collective-permute-start | bytes 44552 | tf_op jit(solution)/shard_map/ppermute | solution.py:495
  96.4 4.6 %collective-permute-start.5 = (f32[1,3712]{1,0:T(1,128)S(1)}, f32[1,3712]{1,0:T(1,128)S(1)}, u32[]{:S(2)}, u32[]{:S(2)}) collective-permute-start(f32[1,3712]{1,0:T(1,128)S(1)} %shard_map.125.refs_0_), channel_id=1, source_target_pairs={{0,8},{1,9},{2,10},{3,11},{4,12},{5,13},{6,14},{7,15},{8,0},{9,1},... | collective-permute-start | bytes 44552 | tf_op jit(solution)/shard_map/ppermute | solution.py:495
  101.0 3.9 %collective-permute-start.6 = (f32[1,3712]{1,0:T(1,128)S(1)}, f32[1,3712]{1,0:T(1,128)S(1)}, u32[]{:S(2)}, u32[]{:S(2)}) collective-permute-start(f32[1,3712]{1,0:T(1,128)S(1)} %shard_map.126.refs_0_), channel_id=1, source_target_pairs={{0,1},{1,0},{2,3},{3,2},{4,5},{5,4},{6,7},{7,6},{8,9},{9,8},{10,11... | collective-permute-start | bytes 44552 | tf_op jit(solution)/shard_map/ppermute | solution.py:495
  105.0 3.7 %collective-permute-start.7 = (f32[1,3712]{1,0:T(1,128)S(1)}, f32[1,3712]{1,0:T(1,128)S(1)}, u32[]{:S(2)}, u32[]{:S(2)}) collective-permute-start(f32[1,3712]{1,0:T(1,128)S(1)} %shard_map.127.refs_0_), channel_id=1, source_target_pairs={{0,2},{1,3},{2,0},{3,1},{4,6},{5,7},{6,4},{7,5},{8,10},{9,11},{10,... | collective-permute-start | bytes 44552 | tf_op jit(solution)/shard_map/ppermute | solution.py:495
  108.7 1.4 %collective-permute-start.8 = (f32[1,3712]{1,0:T(1,128)S(1)}, f32[1,3712]{1,0:T(1,128)S(1)}, u32[]{:S(2)}, u32[]{:S(2)}) collective-permute-start(f32[1,3712]{1,0:T(1,128)S(1)} %shard_map.128.refs_1_), channel_id=1, source_target_pairs={{0,16},{16,0},{1,17},{17,1},{2,18},{18,2},{3,19},{19,3},{4,20},{20... | collective-permute-start | bytes 44552 | tf_op jit(solution)/shard_map/ppermute | solution.py:486
  108.7 10.4 %collective-permute-start.20 = (bf16[32,1280]{1,0:T(8,128)(2,1)S(1)}, bf16[32,1280]{1,0:T(8,128)(2,1)S(1)}, u32[]{:S(2)}, u32[]{:S(2)}) collective-permute-start(bf16[32,1280]{1,0:T(8,128)(2,1)S(1)} %get-tuple-element.72), channel_id=1, source_target_pairs={{0,24},{1,25},{2,26},{3,27},{4,28},{5,29},{6,30},{7,31},{8,16},{9,... | collective-permute-start | bytes 245768 | tf_op jit(solution)/shard_map/ppermute | solution.py:612
  110.1 11.9 %collective-permute-start.26 = (bf16[32,1280]{1,0:T(8,128)(2,1)S(1)}, bf16[32,1280]{1,0:T(8,128)(2,1)S(1)}, u32[]{:S(2)}, u32[]{:S(2)}) collective-permute-start(bf16[32,1280]{1,0:T(8,128)(2,1)S(1)} %get-tuple-element.82), channel_id=1, source_target_pairs={{0,8},{1,9},{2,10},{3,11},{4,12},{5,13},{6,14},{7,15},{8,0},{9,1},... | collective-permute-start | bytes 245768 | tf_op jit(solution)/shard_map/ppermute | solution.py:495
  111.8 10.8 %collective-permute-start.28 = (bf16[32,1280]{1,0:T(8,128)(2,1)S(1)}, bf16[32,1280]{1,0:T(8,128)(2,1)S(1)}, u32[]{:S(2)}, u32[]{:S(2)}) collective-permute-start(bf16[32,1280]{1,0:T(8,128)(2,1)S(1)} %get-tuple-element.84), channel_id=1, source_target_pairs={{0,24},{1,25},{2,26},{3,27},{4,28},{5,29},{6,30},{7,31},{8,16},{9,... | collective-permute-start | bytes 245768 | tf_op jit(solution)/shard_map/ppermute | solution.py:612
  (2 other events, 1.4 us)
